TPU v7x, 32 devices: a whole 2x2x4 slice. The times are simulated.
32 devices in a mesh: depth: 8 (over y, x, core), dp: 4 (over z).
Axes of the slice: x: 2, y: 2, z: 4, core: 2. Of those that a mesh axis runs over, the one named last changes fastest.
Arguments:
- token_ids: int32 [512], P('dp'), may hold values from 0 to 10239
- embedding: bfloat16 [10240, 512], P('depth'), may hold values from -6 to 6
- w_up: bfloat16 [16, 512, 2048], P('depth'), may hold values from -0.25 to 0.25
- w_down: bfloat16 [16, 2048, 512], P('depth'), may hold values from -0.125 to 0.125
- cotangent: bfloat16 [512, 512], P('dp'), may hold values from -0.119628906 to 0.119628906
Outputs:
- grad_up: float32 [16, 512, 2048], P('depth', 'dp')
- grad_down: float32 [16, 2048, 512], P('depth', 'dp')
All inputs are finite; a program needn't handle non-finite values.
Results may differ from a plain program's by a relative error of at most 0.03.
Values may be sent and summed in bfloat16 or wider, within the bound.
No kernel may reach another device: no remote copies, remote signals or barrier semaphores. Data moves between devices by JAX's collectives and lax.ppermute only.
A program may use at most 64 MiB of HBM per device.

v0:
```python
import jax
import jax.numpy as jnp
from jax import lax
from jax.sharding import PartitionSpec as P

RELAX = 3


EPSILON = 1e-06
GAMMA = 0.05


def shifted(block, axis, distance):
    devices = range(lax.axis_size(axis))
    route = [(i - distance, i) for i in devices if i - distance in devices]
    return lax.ppermute(block, axis, route)


def layer_forward(state, weight_up, weight_down):
    scale = lax.rsqrt(jnp.mean(state * state, axis=-1, keepdims=True) + EPSILON)
    normed = (state * scale).astype(jnp.bfloat16)
    before = jnp.dot(normed, weight_up, preferred_element_type=jnp.float32)
    hidden = jax.nn.silu(before).astype(jnp.bfloat16)
    output = state + jnp.dot(hidden, weight_down, preferred_element_type=jnp.float32)
    return (output, (scale, normed, before, hidden))


def layer_adjoint(state, saved, adjoint, weight_up, weight_down):
    scale, normed, before, hidden = saved
    adjoint_low = adjoint.astype(jnp.bfloat16)
    toward_hidden = lax.dot_general(
        adjoint_low, weight_down, (((1,), (1,)), ((), ())), preferred_element_type=jnp.float32
    )
    sigma = jax.nn.sigmoid(before)
    delta = (toward_hidden * sigma * (1.0 + before * (1.0 - sigma))).astype(jnp.bfloat16)
    toward_normed = lax.dot_general(
        delta, weight_up, (((1,), (1,)), ((), ())), preferred_element_type=jnp.float32
    )
    unit = state * scale
    inner = jnp.mean(toward_normed * unit, axis=-1, keepdims=True)
    return (adjoint + scale * (toward_normed - unit * inner), adjoint_low, delta)


def coarse_matrix(weight_up, weight_down):
    total = jnp.dot(weight_up[0], weight_down[0], preferred_element_type=jnp.float32)
    total = total + jnp.dot(weight_up[1], weight_down[1], preferred_element_type=jnp.float32)
    return jnp.eye(weight_up.shape[1], dtype=jnp.float32) + GAMMA * total


def shards(token_ids, embedding, w_up, w_down, cotangent):
    depth = lax.axis_size("depth")
    position = lax.axis_index("depth")
    first = position == 0
    final_block = position == depth - 1
    layers = w_up.shape[0]
    vocab_rows = embedding.shape[0]
    local_ids = token_ids - position * vocab_rows
    inside = (local_ids >= 0) & (local_ids < vocab_rows)
    picked = jnp.take(embedding, jnp.clip(local_ids, 0, vocab_rows - 1), axis=0)
    picked = jnp.where(inside[:, None], picked, jnp.zeros_like(picked)).astype(jnp.float32)
    start = lax.psum(picked.astype(jnp.bfloat16), "depth").astype(jnp.float32)
    matrix = coarse_matrix(w_up, w_down)
    transposed = matrix.T
    zeros = jnp.zeros_like(start)
    coarse = start
    arrived_projection = zeros
    for sweep in range(RELAX):
        run_state = coarse
        for run_layer in range(layers):
            run_state, unused = layer_forward(run_state, w_up[run_layer], w_down[run_layer])
        projection = jnp.dot(coarse, matrix, precision=lax.Precision.HIGHEST)
        arrived, arrived_projection = shifted((run_state, projection), "depth", 1)
        coarse = jnp.where(first, start, arrived)
    tau = coarse - arrived_projection

    def forward_turn(turn, incoming):
        carried = jnp.dot(incoming + tau, matrix, precision=lax.Precision.HIGHEST)
        return shifted(carried.astype(jnp.bfloat16), "depth", 1).astype(carried.dtype)

    incoming = lax.fori_loop(0, depth - 1, forward_turn, zeros)
    corrected = incoming + tau
    states = []
    saves = []
    state = corrected
    for layer in range(layers):
        states.append(state)
        state, saved = layer_forward(state, w_up[layer], w_down[layer])
        saves.append(saved)

    def run_adjoint(adjoint):
        for layer in reversed(range(layers)):
            adjoint, low, delta = layer_adjoint(
                states[layer], saves[layer], adjoint, w_up[layer], w_down[layer]
            )
        return adjoint

    final = cotangent.astype(jnp.float32)
    adjoint_state = final
    back_projection = zeros
    for sweep in range(RELAX):
        begun = run_adjoint(adjoint_state)
        projection = jnp.dot(adjoint_state, transposed, precision=lax.Precision.HIGHEST)
        arrived, back_projection = (
            shifted(begun.astype(jnp.bfloat16), "depth", -1).astype(begun.dtype),
            shifted(projection.astype(jnp.bfloat16), "depth", -1).astype(projection.dtype),
        )
        adjoint_state = jnp.where(final_block, final, arrived)
    back_tau = adjoint_state - back_projection

    def backward_turn(turn, incoming):
        carried = jnp.dot(incoming + back_tau, transposed, precision=lax.Precision.HIGHEST)
        return shifted(carried.astype(jnp.bfloat16), "depth", -1).astype(carried.dtype)

    back_incoming = lax.fori_loop(0, depth - 1, backward_turn, zeros)
    adjoint = back_incoming + back_tau
    lows = [None] * layers
    deltas = [None] * layers
    for layer in reversed(range(layers)):
        adjoint, low, delta = layer_adjoint(
            states[layer], saves[layer], adjoint, w_up[layer], w_down[layer]
        )
        lows[layer] = low
        deltas[layer] = delta
    normed_all = jnp.stack([saves[layer][1] for layer in range(layers)], 0)
    hidden_all = jnp.stack([saves[layer][3] for layer in range(layers)], 0)
    delta_all = jnp.stack(deltas, 0)
    low_all = jnp.stack(lows, 0)
    normed_part, hidden_part = (
        lax.all_to_all(normed_all, "dp", split_axis=2, concat_axis=1, tiled=True),
        lax.all_to_all(hidden_all, "dp", split_axis=2, concat_axis=1, tiled=True),
    )
    delta_whole, low_whole = (
        lax.all_gather(delta_all, "dp", axis=1, tiled=True),
        lax.all_gather(low_all, "dp", axis=1, tiled=True),
    )
    grad_up = jnp.einsum(
        "ltd,ltf->ldf", normed_part, delta_whole, preferred_element_type=jnp.float32
    )
    grad_down = jnp.einsum(
        "ltf,ltd->lfd", hidden_part, low_whole, preferred_element_type=jnp.float32
    )
    return (grad_up, grad_down)


def solution(mesh):
    in_specs = (
        P("dp"),
        P("depth", None),
        P("depth", None, None),
        P("depth", None, None),
        P("dp", None),
    )
    out_specs = (P("depth", "dp", None), P("depth", "dp", None))
    return jax.shard_map(shards, mesh=mesh, in_specs=in_specs, out_specs=out_specs, check_vma=False)
```

profile of v0, /device:TPU:0, one launch (start us, length us, event | category | flops | bytes accessed | tf_op | source)
XLA Modules:
  0.0 437.5 jit_solution(14068713169038172877)
XLA Ops:
  10.2 57.6 %all-reduce.2.cloned.1.call-done = bf16[128,512]{1,0:T(8,128)(2,1)} async-done(((bf16[128,512]{1,0:T(8,128)(2,1)}), bf16[128,512]{1,0:T(8,128)(2,1)}) %all-reduce.2.cloned.1.call-update) | async-done | bytes 131088 | tf_op jit(solution)/shard_map/psum | solution.py:61
  76.4 4.4 %fusion.27 = f32[512,512]{1,0:T(8,128)} fusion(bf16[2,2048,512]{2,1,0:T(8,128)(2,1)} %param.12, bf16[2,512,2048]{2,1,0:T(8,128)(2,1)} %param.11), kind=kOutput, calls=%fused_computation.40 | convolution fusion | flops 1073741824 | bytes 5242880 | tf_op jit(solution)/shard_map/dot_general | solution.py:46
  103.6 4.0 collective-permute-start.4
  109.1 4.5 %collective-permute-start.5 = (f32[128,512]{1,0:T(8,128)}, f32[128,512]{1,0:T(8,128)S(1)}, u32[]{:S(2)}, u32[]{:S(2)}) collective-permute-start(f32[128,512]{1,0:T(8,128)} %fusion.244), channel_id=1, source_target_pairs={{0,4},{4,8},{8,12},{12,16},{16,20},{20,24},{24,28},{1,5},{5,9},{9,... | collective-permute-start | bytes 786440 | tf_op jit(solution)/shard_map/ppermute | solution.py:16
  114.8 50.3 %while.22 = (s32[]{:T(128)}, f32[128,512]{1,0:T(8,128)S(1)}, f32[128,512]{1,0:T(8,128)S(1)}, f32[512,512]{1,0:T(8,128)S(1)}, s32[]{:T(128)}, /*index=5*/s32[]{:T(128)}) while((s32[]{:T(128)}, f32[128,512]{1,0:T(8,128)S(1)}, f32[128,512]{1,0:T(8,128)S(1)}, f32[512,512]{1,0:T(8,128)S(1)}, s32[]{:T(128)}, /*index=5*/s32[]{:T(128)}) %tuple.64), condition=%wide.region_8.9_spmd.clone, body=%wide.region_7.8_spmd.clone.sunk | while | flops 402915328 | bytes 2621559 | solution.py:80
  115.6 5.4 %collective-permute-start = (bf16[128,512]{1,0:T(8,128)(2,1)S(1)}, bf16[128,512]{1,0:T(8,128)(2,1)S(1)}, u32[]{:S(2)}, u32[]{:S(2)}) collective-permute-start(bf16[128,512]{1,0:T(8,128)(2,1)S(1)} %convolution_convert_fusion.5), channel_id=1, source_target_pairs={{0,4},{4,8},{8,12},{12,16},{16,20},{20,24},{24,28},{1,5},{5,9},{9,... | collective-permute-start | bytes 393224 | tf_op jit(solution)/shard_map/while/body/eval_jaxpr/ppermute | solution.py:16
  122.8 5.2 %collective-permute-start = (bf16[128,512]{1,0:T(8,128)(2,1)S(1)}, bf16[128,512]{1,0:T(8,128)(2,1)S(1)}, u32[]{:S(2)}, u32[]{:S(2)}) collective-permute-start(bf16[128,512]{1,0:T(8,128)(2,1)S(1)} %convolution_convert_fusion.5), channel_id=1, source_target_pairs={{0,4},{4,8},{8,12},{12,16},{16,20},{20,24},{24,28},{1,5},{5,9},{9,... | collective-permute-start | bytes 393224 | tf_op jit(solution)/shard_map/while/body/eval_jaxpr/ppermute | solution.py:16
  129.8 5.3 %collective-permute-start = (bf16[128,512]{1,0:T(8,128)(2,1)S(1)}, bf16[128,512]{1,0:T(8,128)(2,1)S(1)}, u32[]{:S(2)}, u32[]{:S(2)}) collective-permute-start(bf16[128,512]{1,0:T(8,128)(2,1)S(1)} %convolution_convert_fusion.5), channel_id=1, source_target_pairs={{0,4},{4,8},{8,12},{12,16},{16,20},{20,24},{24,28},{1,5},{5,9},{9,... | collective-permute-start | bytes 393224 | tf_op jit(solution)/shard_map/while/body/eval_jaxpr/ppermute | solution.py:16
  136.8 5.3 %collective-permute-start = (bf16[128,512]{1,0:T(8,128)(2,1)S(1)}, bf16[128,512]{1,0:T(8,128)(2,1)S(1)}, u32[]{:S(2)}, u32[]{:S(2)}) collective-permute-start(bf16[128,512]{1,0:T(8,128)(2,1)S(1)} %convolution_convert_fusion.5), channel_id=1, source_target_pairs={{0,4},{4,8},{8,12},{12,16},{16,20},{20,24},{24,28},{1,5},{5,9},{9,... | collective-permute-start | bytes 393224 | tf_op jit(solution)/shard_map/while/body/eval_jaxpr/ppermute | solution.py:16
  143.9 5.3 %collective-permute-start = (bf16[128,512]{1,0:T(8,128)(2,1)S(1)}, bf16[128,512]{1,0:T(8,128)(2,1)S(1)}, u32[]{:S(2)}, u32[]{:S(2)}) collective-permute-start(bf16[128,512]{1,0:T(8,128)(2,1)S(1)} %convolution_convert_fusion.5), channel_id=1, source_target_pairs={{0,4},{4,8},{8,12},{12,16},{16,20},{20,24},{24,28},{1,5},{5,9},{9,... | collective-permute-start | bytes 393224 | tf_op jit(solution)/shard_map/while/body/eval_jaxpr/ppermute | solution.py:16
  151.0 5.3 %collective-permute-start = (bf16[128,512]{1,0:T(8,128)(2,1)S(1)}, bf16[128,512]{1,0:T(8,128)(2,1)S(1)}, u32[]{:S(2)}, u32[]{:S(2)}) collective-permute-start(bf16[128,512]{1,0:T(8,128)(2,1)S(1)} %convolution_convert_fusion.5), channel_id=1, source_target_pairs={{0,4},{4,8},{8,12},{12,16},{16,20},{20,24},{24,28},{1,5},{5,9},{9,... | collective-permute-start | bytes 393224 | tf_op jit(solution)/shard_map/while/body/eval_jaxpr/ppermute | solution.py:16
  158.1 6.1 %collective-permute-start = (bf16[128,512]{1,0:T(8,128)(2,1)S(1)}, bf16[128,512]{1,0:T(8,128)(2,1)S(1)}, u32[]{:S(2)}, u32[]{:S(2)}) collective-permute-start(bf16[128,512]{1,0:T(8,128)(2,1)S(1)} %convolution_convert_fusion.5), channel_id=1, source_target_pairs={{0,4},{4,8},{8,12},{12,16},{16,20},{20,24},{24,28},{1,5},{5,9},{9,... | collective-permute-start | bytes 393224 | tf_op jit(solution)/shard_map/while/body/eval_jaxpr/ppermute | solution.py:16
  172.0 4.2 multiply_reduce_fusion.6
  181.6 5.7 %collective-permute-done.6 = bf16[128,512]{1,0:T(8,128)(2,1)S(1)} collective-permute-done((bf16[128,512]{1,0:T(8,128)(2,1)S(1)}, bf16[128,512]{1,0:T(8,128)(2,1)S(1)}, u32[]{:S(2)}, u32[]{:S(2)}) %collective-permute-start.6) | collective-permute-done | bytes 131104 | tf_op jit(solution)/shard_map/ppermute | solution.py:16
  187.4 4.2 multiply_reduce_fusion.4
  191.7 4.3 multiply_reduce_fusion.3
  197.4 6.6 %collective-permute-done.7 = bf16[128,512]{1,0:T(8,128)(2,1)S(1)} collective-permute-done((bf16[128,512]{1,0:T(8,128)(2,1)S(1)}, bf16[128,512]{1,0:T(8,128)(2,1)S(1)}, u32[]{:S(2)}, u32[]{:S(2)}) %collective-permute-start.7) | collective-permute-done | bytes 131104 | tf_op jit(solution)/shard_map/ppermute | solution.py:16
  207.1 4.8 %multiply_reduce_fusion.2 = (f32[128]{0:T(128)S(1)}, f32[128,512]{1,0:T(8,128)}) fusion(f32[128,512]{1,0:T(8,128)S(1)} %get-tuple-element.122, f32[128]{0:T(128)S(1)} %add_rsqrt_fusion, bf16[2,512,2048]{2,1,0:T(8,128)(2,1)} %param.11, f32[128,2048]{1,0:T(8,128)} %fusion.43, bf16[2,2048,512]{2,1,0:T(8,128)(2,1)} %param.12, ...), kind=kOutput, calls=%fused_computation.173 | convolution fusion | flops 539688832 | bytes 6030337 | tf_op jit(solution)/shard_map/dot_general | solution.py:36
  213.0 4.2 multiply_reduce_fusion.1
  226.9 56.5 %while.23 = (s32[]{:T(128)}, f32[128,512]{1,0:T(8,128)S(1)}, f32[128,512]{1,0:T(8,128)S(1)}, f32[512,512]{1,0:T(8,128)S(1)}, s32[]{:T(128)}, /*index=5*/s32[]{:T(128)}) while((s32[]{:T(128)}, f32[128,512]{1,0:T(8,128)S(1)}, f32[128,512]{1,0:T(8,128)S(1)}, f32[512,512]{1,0:T(8,128)S(1)}, s32[]{:T(128)}, ...), condition=%wide.region_18.19_spmd.clone, body=%wide.region_17.18_spmd.clone.sunk | while | flops 402915328 | bytes 2621559 | solution.py:114
  228.9 6.6 %collective-permute-done.1 = bf16[128,512]{1,0:T(8,128)(2,1)S(1)} collective-permute-done((bf16[128,512]{1,0:T(8,128)(2,1)S(1)}, bf16[128,512]{1,0:T(8,128)(2,1)S(1)}, u32[]{:S(2)}, u32[]{:S(2)}) %collective-permute-start.1) | collective-permute-done | bytes 131104 | tf_op jit(solution)/shard_map/while/body/eval_jaxpr/ppermute | solution.py:16
  237.6 5.9 %collective-permute-done.1 = bf16[128,512]{1,0:T(8,128)(2,1)S(1)} collective-permute-done((bf16[128,512]{1,0:T(8,128)(2,1)S(1)}, bf16[128,512]{1,0:T(8,128)(2,1)S(1)}, u32[]{:S(2)}, u32[]{:S(2)}) %collective-permute-start.1) | collective-permute-done | bytes 131104 | tf_op jit(solution)/shard_map/while/body/eval_jaxpr/ppermute | solution.py:16
  245.6 5.9 %collective-permute-done.1 = bf16[128,512]{1,0:T(8,128)(2,1)S(1)} collective-permute-done((bf16[128,512]{1,0:T(8,128)(2,1)S(1)}, bf16[128,512]{1,0:T(8,128)(2,1)S(1)}, u32[]{:S(2)}, u32[]{:S(2)}) %collective-permute-start.1) | collective-permute-done | bytes 131104 | tf_op jit(solution)/shard_map/while/body/eval_jaxpr/ppermute | solution.py:16
  253.5 5.9 %collective-permute-done.1 = bf16[128,512]{1,0:T(8,128)(2,1)S(1)} collective-permute-done((bf16[128,512]{1,0:T(8,128)(2,1)S(1)}, bf16[128,512]{1,0:T(8,128)(2,1)S(1)}, u32[]{:S(2)}, u32[]{:S(2)}) %collective-permute-start.1) | collective-permute-done | bytes 131104 | tf_op jit(solution)/shard_map/while/body/eval_jaxpr/ppermute | solution.py:16
  261.5 5.9 %collective-permute-done.1 = bf16[128,512]{1,0:T(8,128)(2,1)S(1)} collective-permute-done((bf16[128,512]{1,0:T(8,128)(2,1)S(1)}, bf16[128,512]{1,0:T(8,128)(2,1)S(1)}, u32[]{:S(2)}, u32[]{:S(2)}) %collective-permute-start.1) | collective-permute-done | bytes 131104 | tf_op jit(solution)/shard_map/while/body/eval_jaxpr/ppermute | solution.py:16
  269.5 5.9 %collective-permute-done.1 = bf16[128,512]{1,0:T(8,128)(2,1)S(1)} collective-permute-done((bf16[128,512]{1,0:T(8,128)(2,1)S(1)}, bf16[128,512]{1,0:T(8,128)(2,1)S(1)}, u32[]{:S(2)}, u32[]{:S(2)}) %collective-permute-start.1) | collective-permute-done | bytes 131104 | tf_op jit(solution)/shard_map/while/body/eval_jaxpr/ppermute | solution.py:16
  277.4 5.9 %collective-permute-done.1 = bf16[128,512]{1,0:T(8,128)(2,1)S(1)} collective-permute-done((bf16[128,512]{1,0:T(8,128)(2,1)S(1)}, bf16[128,512]{1,0:T(8,128)(2,1)S(1)}, u32[]{:S(2)}, u32[]{:S(2)}) %collective-permute-start.1) | collective-permute-done | bytes 131104 | tf_op jit(solution)/shard_map/while/body/eval_jaxpr/ppermute | solution.py:16
  296.1 4.6 %all-to-all-start = ((bf16[2,128,512]{1,0,2:T(2,128)(2,1)}), bf16[2,128,512]{1,0,2:T(2,128)(2,1)}, u32[]{:S(2)}, u32[]{:S(2)}) async-start(bf16[2,128,512]{1,0,2:T(2,128)(2,1)} %copy.10), calls=%async_computation | async-start | bytes 524288 | tf_op jit(solution)/shard_map/all_to_all | solution.py:129
  303.4 4.2 all-to-all-done
  313.1 37.0 %all-to-all-done.1 = bf16[2,128,2048]{1,0,2:T(2,128)(2,1)S(1)} async-done(((bf16[2,128,2048]{1,0,2:T(2,128)(2,1)}), bf16[2,128,2048]{1,0,2:T(2,128)(2,1)S(1)}, u32[]{:S(2)}, u32[]{:S(2)}) %all-to-all-start.1) | async-done | bytes 1048608 | tf_op jit(solution)/shard_map/all_to_all | solution.py:130
  354.8 72.0 %all-gather.3.cloned.1.call-done = bf16[2,512,2048]{2,1,0:T(8,128)(2,1)} async-done(((bf16[2,128,2048]{2,1,0:T(8,128)(2,1)}), bf16[2,512,2048]{2,1,0:T(8,128)(2,1)}) %all-gather.3.cloned.1.call-update) | async-done | bytes 4194320 | tf_op jit(solution)/shard_map/all_gather | solution.py:133
  426.8 4.2 fusion.291
  (158 shorter events, 116.3 us)
Async XLA Ops:
  7.2 60.6 %all-reduce.2.cloned.1.call-start = ((), (), s32[]{:S(2)}) async-start(), calls=%async_computation.2 | async-start | bytes 262144 | tf_op jit(solution)/shard_map/psum | solution.py:61
  10.1 341.2 %all-gather.5.cloned.1.call-start = ((), (), s32[]{:S(2)}) async-start(), calls=%async_computation.4 | async-start | bytes 1310720 | tf_op jit(solution)/shard_map/all_gather | solution.py:134
  75.0 5.9 %collective-permute-start.2 = (f32[128,512]{1,0:T(8,128)S(1)}, f32[128,512]{1,0:T(8,128)S(1)}, u32[]{:S(2)}, u32[]{:S(2)}) collective-permute-start(f32[128,512]{1,0:T(8,128)S(1)} %fusion.115), channel_id=1, source_target_pairs={{0,4},{4,8},{8,12},{12,16},{16,20},{20,24},{24,28},{1,5},{5,9},{9,... | collective-permute-start | bytes 786440 | tf_op jit(solution)/shard_map/ppermute | solution.py:16
  87.8 7.2 %collective-permute-start.3 = (f32[128,512]{1,0:T(8,128)}, f32[128,512]{1,0:T(8,128)S(1)}, u32[]{:S(2)}, u32[]{:S(2)}) collective-permute-start(f32[128,512]{1,0:T(8,128)} %fusion.118), channel_id=1, source_target_pairs={{0,4},{4,8},{8,12},{12,16},{16,20},{20,24},{24,28},{1,5},{5,9},{9,... | collective-permute-start | bytes 786440 | tf_op jit(solution)/shard_map/ppermute | solution.py:16
  95.0 12.6 %copy-start.1 = (f32[512,512]{1,0:T(8,128)}, f32[512,512]{1,0:T(8,128)S(1)}, u32[]{:S(2)}) copy-start(f32[512,512]{1,0:T(8,128)S(1)} %get-tuple-element.120) | copy-start | bytes 3145732
  103.6 10.0 %collective-permute-start.4 = (f32[128,512]{1,0:T(8,128)}, f32[128,512]{1,0:T(8,128)}, u32[]{:S(2)}, u32[]{:S(2)}) collective-permute-start(f32[128,512]{1,0:T(8,128)} %fusion.121), channel_id=1, source_target_pairs={{0,4},{4,8},{8,12},{12,16},{16,20},{20,24},{24,28},{1,5},{5,9},{9,... | collective-permute-start | bytes 786440 | tf_op jit(solution)/shard_map/ppermute | solution.py:16
  109.1 5.7 %collective-permute-start.5 = (f32[128,512]{1,0:T(8,128)}, f32[128,512]{1,0:T(8,128)S(1)}, u32[]{:S(2)}, u32[]{:S(2)}) collective-permute-start(f32[128,512]{1,0:T(8,128)} %fusion.244), channel_id=1, source_target_pairs={{0,4},{4,8},{8,12},{12,16},{16,20},{20,24},{24,28},{1,5},{5,9},{9,... | collective-permute-start | bytes 786440 | tf_op jit(solution)/shard_map/ppermute | solution.py:16
  115.6 6.4 %collective-permute-start = (bf16[128,512]{1,0:T(8,128)(2,1)S(1)}, bf16[128,512]{1,0:T(8,128)(2,1)S(1)}, u32[]{:S(2)}, u32[]{:S(2)}) collective-permute-start(bf16[128,512]{1,0:T(8,128)(2,1)S(1)} %convolution_convert_fusion.5), channel_id=1, source_target_pairs={{0,4},{4,8},{8,12},{12,16},{16,20},{20,24},{24,28},{1,5},{5,9},{9,... | collective-permute-start | bytes 393224 | tf_op jit(solution)/shard_map/while/body/eval_jaxpr/ppermute | solution.py:16
  122.8 6.2 %collective-permute-start = (bf16[128,512]{1,0:T(8,128)(2,1)S(1)}, bf16[128,512]{1,0:T(8,128)(2,1)S(1)}, u32[]{:S(2)}, u32[]{:S(2)}) collective-permute-start(bf16[128,512]{1,0:T(8,128)(2,1)S(1)} %convolution_convert_fusion.5), channel_id=1, source_target_pairs={{0,4},{4,8},{8,12},{12,16},{16,20},{20,24},{24,28},{1,5},{5,9},{9,... | collective-permute-start | bytes 393224 | tf_op jit(solution)/shard_map/while/body/eval_jaxpr/ppermute | solution.py:16
  129.8 6.3 %collective-permute-start = (bf16[128,512]{1,0:T(8,128)(2,1)S(1)}, bf16[128,512]{1,0:T(8,128)(2,1)S(1)}, u32[]{:S(2)}, u32[]{:S(2)}) collective-permute-start(bf16[128,512]{1,0:T(8,128)(2,1)S(1)} %convolution_convert_fusion.5), channel_id=1, source_target_pairs={{0,4},{4,8},{8,12},{12,16},{16,20},{20,24},{24,28},{1,5},{5,9},{9,... | collective-permute-start | bytes 393224 | tf_op jit(solution)/shard_map/while/body/eval_jaxpr/ppermute | solution.py:16
  136.8 6.3 %collective-permute-start = (bf16[128,512]{1,0:T(8,128)(2,1)S(1)}, bf16[128,512]{1,0:T(8,128)(2,1)S(1)}, u32[]{:S(2)}, u32[]{:S(2)}) collective-permute-start(bf16[128,512]{1,0:T(8,128)(2,1)S(1)} %convolution_convert_fusion.5), channel_id=1, source_target_pairs={{0,4},{4,8},{8,12},{12,16},{16,20},{20,24},{24,28},{1,5},{5,9},{9,... | collective-permute-start | bytes 393224 | tf_op jit(solution)/shard_map/while/body/eval_jaxpr/ppermute | solution.py:16
  143.9 6.3 %collective-permute-start = (bf16[128,512]{1,0:T(8,128)(2,1)S(1)}, bf16[128,512]{1,0:T(8,128)(2,1)S(1)}, u32[]{:S(2)}, u32[]{:S(2)}) collective-permute-start(bf16[128,512]{1,0:T(8,128)(2,1)S(1)} %convolution_convert_fusion.5), channel_id=1, source_target_pairs={{0,4},{4,8},{8,12},{12,16},{16,20},{20,24},{24,28},{1,5},{5,9},{9,... | collective-permute-start | bytes 393224 | tf_op jit(solution)/shard_map/while/body/eval_jaxpr/ppermute | solution.py:16
  151.0 6.3 %collective-permute-start = (bf16[128,512]{1,0:T(8,128)(2,1)S(1)}, bf16[128,512]{1,0:T(8,128)(2,1)S(1)}, u32[]{:S(2)}, u32[]{:S(2)}) collective-permute-start(bf16[128,512]{1,0:T(8,128)(2,1)S(1)} %convolution_convert_fusion.5), channel_id=1, source_target_pairs={{0,4},{4,8},{8,12},{12,16},{16,20},{20,24},{24,28},{1,5},{5,9},{9,... | collective-permute-start | bytes 393224 | tf_op jit(solution)/shard_map/while/body/eval_jaxpr/ppermute | solution.py:16
  158.1 7.1 %collective-permute-start = (bf16[128,512]{1,0:T(8,128)(2,1)S(1)}, bf16[128,512]{1,0:T(8,128)(2,1)S(1)}, u32[]{:S(2)}, u32[]{:S(2)}) collective-permute-start(bf16[128,512]{1,0:T(8,128)(2,1)S(1)} %convolution_convert_fusion.5), channel_id=1, source_target_pairs={{0,4},{4,8},{8,12},{12,16},{16,20},{20,24},{24,28},{1,5},{5,9},{9,... | collective-permute-start | bytes 393224 | tf_op jit(solution)/shard_map/while/body/eval_jaxpr/ppermute | solution.py:16
  168.0 12.1 %copy-start.3 = (f32[128,2048]{1,0:T(8,128)}, f32[128,2048]{1,0:T(8,128)S(1)}, u32[]{:S(2)}) copy-start(f32[128,2048]{1,0:T(8,128)S(1)} %fusion.72) | copy-start | bytes 3145732
  180.3 7.0 %collective-permute-start.6 = (bf16[128,512]{1,0:T(8,128)(2,1)S(1)}, bf16[128,512]{1,0:T(8,128)(2,1)S(1)}, u32[]{:S(2)}, u32[]{:S(2)}) collective-permute-start(bf16[128,512]{1,0:T(8,128)(2,1)S(1)} %add_convert_fusion.3), channel_id=1, source_target_pairs={{4,0},{8,4},{12,8},{16,12},{20,16},{24,20},{28,24},{5,1},{9,5},{13... | collective-permute-start | bytes 393224 | tf_op jit(solution)/shard_map/ppermute | solution.py:16
  191.7 12.3 %copy-start.2 = (f32[512,512]{1,0:T(8,128)S(1)}, f32[512,512]{1,0:T(8,128)}, u32[]{:S(2)}) copy-start(f32[512,512]{1,0:T(8,128)} %copy-done.1) | copy-start | bytes 3145732
  196.1 7.9 %collective-permute-start.7 = (bf16[128,512]{1,0:T(8,128)(2,1)S(1)}, bf16[128,512]{1,0:T(8,128)(2,1)S(1)}, u32[]{:S(2)}, u32[]{:S(2)}) collective-permute-start(bf16[128,512]{1,0:T(8,128)(2,1)S(1)} %add_convert_fusion.2), channel_id=1, source_target_pairs={{4,0},{8,4},{12,8},{16,12},{20,16},{24,20},{28,24},{5,1},{9,5},{13... | collective-permute-start | bytes 393224 | tf_op jit(solution)/shard_map/ppermute | solution.py:16
  205.8 16.4 %collective-permute-start.9 = (bf16[128,512]{1,0:T(8,128)(2,1)}, bf16[128,512]{1,0:T(8,128)(2,1)}, u32[]{:S(2)}, u32[]{:S(2)}) collective-permute-start(bf16[128,512]{1,0:T(8,128)(2,1)} %convolution_convert_fusion.2), channel_id=1, source_target_pairs={{4,0},{8,4},{12,8},{16,12},{20,16},{24,20},{28,24},{5,1},{9,5},{13... | collective-permute-start | bytes 393224 | tf_op jit(solution)/shard_map/ppermute | solution.py:16
  218.0 7.9 %collective-permute-start.8 = (bf16[128,512]{1,0:T(8,128)(2,1)}, bf16[128,512]{1,0:T(8,128)(2,1)S(1)}, u32[]{:S(2)}, u32[]{:S(2)}) collective-permute-start(bf16[128,512]{1,0:T(8,128)(2,1)} %get-tuple-element.110), channel_id=1, source_target_pairs={{4,0},{8,4},{12,8},{16,12},{20,16},{24,20},{28,24},{5,1},{9,5},{13... | collective-permute-start | bytes 393224 | tf_op jit(solution)/shard_map/ppermute | solution.py:16
  227.6 7.9 %collective-permute-start.1 = (bf16[128,512]{1,0:T(8,128)(2,1)S(1)}, bf16[128,512]{1,0:T(8,128)(2,1)S(1)}, u32[]{:S(2)}, u32[]{:S(2)}) collective-permute-start(bf16[128,512]{1,0:T(8,128)(2,1)S(1)} %convolution_convert_fusion.6), channel_id=1, source_target_pairs={{4,0},{8,4},{12,8},{16,12},{20,16},{24,20},{28,24},{5,1},{9,5},{13... | collective-permute-start | bytes 393224 | tf_op jit(solution)/shard_map/while/body/eval_jaxpr/ppermute | solution.py:16
  236.3 7.2 %collective-permute-start.1 = (bf16[128,512]{1,0:T(8,128)(2,1)S(1)}, bf16[128,512]{1,0:T(8,128)(2,1)S(1)}, u32[]{:S(2)}, u32[]{:S(2)}) collective-permute-start(bf16[128,512]{1,0:T(8,128)(2,1)S(1)} %convolution_convert_fusion.6), channel_id=1, source_target_pairs={{4,0},{8,4},{12,8},{16,12},{20,16},{24,20},{28,24},{5,1},{9,5},{13... | collective-permute-start | bytes 393224 | tf_op jit(solution)/shard_map/while/body/eval_jaxpr/ppermute | solution.py:16
  244.3 7.2 %collective-permute-start.1 = (bf16[128,512]{1,0:T(8,128)(2,1)S(1)}, bf16[128,512]{1,0:T(8,128)(2,1)S(1)}, u32[]{:S(2)}, u32[]{:S(2)}) collective-permute-start(bf16[128,512]{1,0:T(8,128)(2,1)S(1)} %convolution_convert_fusion.6), channel_id=1, source_target_pairs={{4,0},{8,4},{12,8},{16,12},{20,16},{24,20},{28,24},{5,1},{9,5},{13... | collective-permute-start | bytes 393224 | tf_op jit(solution)/shard_map/while/body/eval_jaxpr/ppermute | solution.py:16
  252.2 7.2 %collective-permute-start.1 = (bf16[128,512]{1,0:T(8,128)(2,1)S(1)}, bf16[128,512]{1,0:T(8,128)(2,1)S(1)}, u32[]{:S(2)}, u32[]{:S(2)}) collective-permute-start(bf16[128,512]{1,0:T(8,128)(2,1)S(1)} %convolution_convert_fusion.6), channel_id=1, source_target_pairs={{4,0},{8,4},{12,8},{16,12},{20,16},{24,20},{28,24},{5,1},{9,5},{13... | collective-permute-start | bytes 393224 | tf_op jit(solution)/shard_map/while/body/eval_jaxpr/ppermute | solution.py:16
  260.2 7.2 %collective-permute-start.1 = (bf16[128,512]{1,0:T(8,128)(2,1)S(1)}, bf16[128,512]{1,0:T(8,128)(2,1)S(1)}, u32[]{:S(2)}, u32[]{:S(2)}) collective-permute-start(bf16[128,512]{1,0:T(8,128)(2,1)S(1)} %convolution_convert_fusion.6), channel_id=1, source_target_pairs={{4,0},{8,4},{12,8},{16,12},{20,16},{24,20},{28,24},{5,1},{9,5},{13... | collective-permute-start | bytes 393224 | tf_op jit(solution)/shard_map/while/body/eval_jaxpr/ppermute | solution.py:16
  268.2 7.2 %collective-permute-start.1 = (bf16[128,512]{1,0:T(8,128)(2,1)S(1)}, bf16[128,512]{1,0:T(8,128)(2,1)S(1)}, u32[]{:S(2)}, u32[]{:S(2)}) collective-permute-start(bf16[128,512]{1,0:T(8,128)(2,1)S(1)} %convolution_convert_fusion.6), channel_id=1, source_target_pairs={{4,0},{8,4},{12,8},{16,12},{20,16},{24,20},{28,24},{5,1},{9,5},{13... | collective-permute-start | bytes 393224 | tf_op jit(solution)/shard_map/while/body/eval_jaxpr/ppermute | solution.py:16
  276.1 7.2 %collective-permute-start.1 = (bf16[128,512]{1,0:T(8,128)(2,1)S(1)}, bf16[128,512]{1,0:T(8,128)(2,1)S(1)}, u32[]{:S(2)}, u32[]{:S(2)}) collective-permute-start(bf16[128,512]{1,0:T(8,128)(2,1)S(1)} %convolution_convert_fusion.6), channel_id=1, source_target_pairs={{4,0},{8,4},{12,8},{16,12},{20,16},{24,20},{28,24},{5,1},{9,5},{13... | collective-permute-start | bytes 393224 | tf_op jit(solution)/shard_map/while/body/eval_jaxpr/ppermute | solution.py:16
  289.0 137.8 %all-gather.3.cloned.1.call-start = ((), (), s32[]{:S(2)}) async-start(), calls=%async_computation.3 | async-start | bytes 5242880 | tf_op jit(solution)/shard_map/all_gather | solution.py:133
  291.6 9.2 %copy-start.5 = (f32[128,2048]{1,0:T(8,128)S(1)}, f32[128,2048]{1,0:T(8,128)}, u32[]{:S(2)}) copy-start(f32[128,2048]{1,0:T(8,128)} %fusion.43) | copy-start | bytes 3145732
  296.1 11.5 %all-to-all-start = ((bf16[2,128,512]{1,0,2:T(2,128)(2,1)}), bf16[2,128,512]{1,0,2:T(2,128)(2,1)}, u32[]{:S(2)}, u32[]{:S(2)}) async-start(bf16[2,128,512]{1,0,2:T(2,128)(2,1)} %copy.10), calls=%async_computation | async-start | bytes 524288 | tf_op jit(solution)/shard_map/all_to_all | solution.py:129
  307.6 42.5 %all-to-all-start.1 = ((bf16[2,128,2048]{1,0,2:T(2,128)(2,1)}), bf16[2,128,2048]{1,0,2:T(2,128)(2,1)S(1)}, u32[]{:S(2)}, u32[]{:S(2)}) async-start(bf16[2,128,2048]{1,0,2:T(2,128)(2,1)} %copy.13), calls=%async_computation.1 | async-start | bytes 2097152 | tf_op jit(solution)/shard_map/all_to_all | solution.py:130
  351.3 75.4 %copy-start.8 = (bf16[2,512,128]{1,2,0:T(8,128)(2,1)S(1)}, bf16[2,512,128]{1,2,0:T(8,128)(2,1)}, u32[]{:S(2)}) copy-start(bf16[2,512,128]{1,2,0:T(8,128)(2,1)} %all_to_all.29) | copy-start | bytes 786436
  (11 other events, 31.0 us)
Sparse Core Ops, SparseCore 0:
  11.6 56.1 all-reduce.1
  289.1 52.3 all-gather.4
  343.7 83.0 all-gather.2
where the time goes:
time: 439 us; the launch traced here: 438 us
  waiting for transfers between devices  237 us (54%)
  matrix products  86.1 us (20%)
  starting transfers between devices  74.1 us (17%)
  between operations  14.2 us (3%)
  local copies, waits for them, and re-layouts  13.4 us (3%)
  other arithmetic  12.5 us (3%)
    all_gather x1, waiting for transfers between devices, shards(): lax.all_gather(delta_all, 'dp', axis=1, tiled=True)  72 us
    ppermute x22, starting transfers between devices, shifted(): return lax.ppermute(block, axis, route)  65.9 us
    ppermute x22, waiting for transfers between devices, shifted(): return lax.ppermute(block, axis, route)  65.8 us
    psum x1, waiting for transfers between devices, shards(): start = lax.psum(picked.astype(jnp.bfloat16), 'depth').astype(jnp.float32)  57.6 us
    all_to_all x1, waiting for transfers between devices, shards(): lax.all_to_all(hidden_all, 'dp', split_axis=2, concat_axis=1, tiled=True)  37 us
    dot_general x7, matrix products, layer_adjoint(): lax.dot_general(delta, weight_up, (((1,), (1,)), ((), ())), preferred_ele...  26.4 us
    dot_general x7, matrix products, layer_forward(): jnp.dot(hidden, weight_down, preferred_element_type=jnp.float32)  21.2 us
  transfers between devices with their start and end apart: 27, of which 22 were waited for; matrix products, arithmetic and copies ran while one was open for 9% of the time, Pallas kernels for 0%

commit v1 on v0

v1 whole, which is shorter than its diff:
```python
import jax
import jax.numpy as jnp
from jax import lax
from jax.sharding import PartitionSpec as P

RELAX = 3


EPSILON = 1e-06
GAMMA = 0.05
CHUNK = 512


def swapped(block, axis, mask):
    devices = range(lax.axis_size(axis))
    return lax.ppermute(block, axis, [(i, i ^ mask) for i in devices])


def rotated(block, axis, distance):
    size = lax.axis_size(axis)
    return lax.ppermute(block, axis, [(i, (i + distance) % size) for i in range(size)])


def times(left, right):
    return jnp.dot(
        left.astype(jnp.bfloat16), right.astype(jnp.bfloat16), preferred_element_type=jnp.float32
    )


def times_transposed(left, right):
    return lax.dot_general(
        left.astype(jnp.bfloat16),
        right.astype(jnp.bfloat16),
        (((1,), (1,)), ((), ())),
        preferred_element_type=jnp.float32,
    )


def layer_forward(state, weight_up, weight_down):
    scale = lax.rsqrt(jnp.mean(state * state, axis=-1, keepdims=True) + EPSILON)
    normed = (state * scale).astype(jnp.bfloat16)
    before = jnp.dot(normed, weight_up, preferred_element_type=jnp.float32)
    hidden = jax.nn.silu(before).astype(jnp.bfloat16)
    output = state + jnp.dot(hidden, weight_down, preferred_element_type=jnp.float32)
    return (output, (scale, normed, before, hidden))


def layer_adjoint(state, saved, adjoint, weight_up, weight_down):
    scale, normed, before, hidden = saved
    adjoint_low = adjoint.astype(jnp.bfloat16)
    toward_hidden = times_transposed(adjoint_low, weight_down)
    sigma = jax.nn.sigmoid(before)
    delta = (toward_hidden * sigma * (1.0 + before * (1.0 - sigma))).astype(jnp.bfloat16)
    toward_normed = times_transposed(delta, weight_up)
    unit = state * scale
    inner = jnp.mean(toward_normed * unit, axis=-1, keepdims=True)
    return (adjoint + scale * (toward_normed - unit * inner), adjoint_low, delta)


def coarse_part(w_up, w_down):
    total = jnp.dot(w_up[0], w_down[0], preferred_element_type=jnp.float32)
    for layer in range(1, w_up.shape[0]):
        total = total + jnp.dot(w_up[layer], w_down[layer], preferred_element_type=jnp.float32)
    return GAMMA * total


def joined(left, right):
    return left + right + times(left, right)


def matrix_scan(own, position, bits):
    whole = own
    prefix = jnp.zeros_like(own)
    suffix = jnp.zeros_like(own)
    steps = []
    for bit in range(bits):
        upper = ((position >> bit) & 1) == 1
        low = high = None
        if bit < bits - 1:
            other = swapped(whole.astype(jnp.bfloat16), "depth", 1 << bit).astype(jnp.float32)
            low = jnp.where(upper, other, whole)
            high = jnp.where(upper, whole, other)
        steps.append((prefix, suffix, low, high))
        if bit < bits - 1:
            prefix = jnp.where(upper, joined(low, prefix), prefix)
            suffix = jnp.where(upper, suffix, joined(suffix, high))
            if bit < bits - 2:
                whole = joined(low, high)
    return steps


def gathered(block, axis):
    size = lax.axis_size(axis)
    index = lax.axis_index(axis)
    rows = block.shape[0]
    whole = jnp.zeros((size * rows,) + block.shape[1:], block.dtype)
    for distance in range(size):
        piece = rotated(block, axis, distance) if distance else block
        source = lax.rem(index + size - distance, size)
        whole = lax.dynamic_update_slice_in_dim(whole, piece, source * rows, 0)
    return whole


def shards(token_ids, embedding, w_up, w_down, cotangent):
    depth = lax.axis_size("depth")
    bits = depth.bit_length() - 1
    assert depth == 1 << bits
    position = lax.axis_index("depth")
    first = position == 0
    final_block = position == depth - 1
    layers = w_up.shape[0]
    vocab_rows = embedding.shape[0]
    local_ids = token_ids - position * vocab_rows
    inside = (local_ids >= 0) & (local_ids < vocab_rows)
    picked = jnp.take(embedding, jnp.clip(local_ids, 0, vocab_rows - 1), axis=0)
    picked = jnp.where(inside[:, None], picked, jnp.zeros_like(picked))
    picked = picked + swapped(picked, "depth", 1)
    arrivals = [swapped(picked, "depth", mask) for mask in range(2, depth, 2)]
    for arrival in arrivals:
        picked = picked + arrival
    start = picked.astype(jnp.float32)
    own = coarse_part(w_up, w_down)
    steps = matrix_scan(own, position, bits)

    def run_forward(state):
        for layer in range(layers):
            state, unused = layer_forward(state, w_up[layer], w_down[layer])
        return state

    coarse = start
    for sweep in range(RELAX - 1):
        arrived = rotated(run_forward(coarse).astype(jnp.bfloat16), "depth", 1)
        coarse = jnp.where(first, start, arrived.astype(jnp.float32))
    ended = run_forward(coarse)
    value = jnp.where(first, ended, ended - coarse - times(coarse, own))
    corrected = jnp.zeros_like(start)
    for bit in range(bits):
        prefix, suffix, low, high = steps[bit]
        upper = ((position >> bit) & 1) == 1
        other = swapped(value.astype(jnp.bfloat16), "depth", 1 << bit).astype(jnp.float32)
        lower_value = jnp.where(upper, other, value)
        corrected = corrected + jnp.where(upper, lower_value + times(lower_value, prefix), 0.0)
        if bit < bits - 1:
            upper_value = jnp.where(upper, value, other)
            value = upper_value + lower_value + times(lower_value, high)
    corrected = jnp.where(first, start, corrected)
    corrected_low = corrected.astype(jnp.bfloat16)
    corrected = corrected_low.astype(jnp.float32)

    def block_saves(state):
        states = []
        saves = []
        for layer in range(layers):
            states.append(state)
            state, saved = layer_forward(state, w_up[layer], w_down[layer])
            saves.append(saved)
        return states, saves

    states, saves = block_saves(corrected)

    def run_adjoint(adjoint):
        for layer in reversed(range(layers)):
            adjoint, low, delta = layer_adjoint(
                states[layer], saves[layer], adjoint, w_up[layer], w_down[layer]
            )
        return adjoint

    final = cotangent.astype(jnp.float32)
    adjoint_state = final
    for sweep in range(RELAX - 1):
        arrived = rotated(run_adjoint(adjoint_state).astype(jnp.bfloat16), "depth", -1)
        adjoint_state = jnp.where(final_block, final, arrived.astype(jnp.float32))
    begun = run_adjoint(adjoint_state)
    value = jnp.where(
        final_block, begun, begun - adjoint_state - times_transposed(adjoint_state, own)
    )
    adjoint = jnp.zeros_like(final)
    for bit in range(bits):
        prefix, suffix, low, high = steps[bit]
        upper = ((position >> bit) & 1) == 1
        other = swapped(value.astype(jnp.bfloat16), "depth", 1 << bit).astype(jnp.float32)
        upper_value = jnp.where(upper, value, other)
        adjoint = adjoint + jnp.where(
            upper, 0.0, upper_value + times_transposed(upper_value, suffix)
        )
        if bit < bits - 1:
            lower_value = jnp.where(upper, other, value)
            value = lower_value + upper_value + times_transposed(upper_value, low)
    adjoint = jnp.where(final_block, final, adjoint)

    parts = lax.axis_size("dp")
    part = lax.axis_index("dp")

    def own_columns(block):
        width = block.shape[1] // parts
        return lax.dynamic_slice_in_dim(block, part * width, width, 1)

    def over_tokens(left, right):
        return lax.dot_general(
            left, right, (((0,), (0,)), ((), ())), preferred_element_type=jnp.float32
        )

    def chunk_grads(state_low, adjoint_low):
        inputs, saves = block_saves(state_low.astype(jnp.float32))
        adjoint = adjoint_low.astype(jnp.float32)
        grads_up = [None] * layers
        grads_down = [None] * layers
        for layer in reversed(range(layers)):
            scale, normed, before, hidden = saves[layer]
            adjoint, low, delta = layer_adjoint(
                inputs[layer], saves[layer], adjoint, w_up[layer], w_down[layer]
            )
            grads_down[layer] = over_tokens(own_columns(hidden), low)
            grads_up[layer] = over_tokens(own_columns(normed), delta)
        return (jnp.stack(grads_up, 0), jnp.stack(grads_down, 0))

    all_corrected = gathered(corrected_low, "dp")
    all_adjoint = gathered(adjoint.astype(jnp.bfloat16), "dp")
    tokens = all_corrected.shape[0]
    chunk = min(tokens, CHUNK)
    if tokens == chunk:
        return chunk_grads(all_corrected, all_adjoint)

    def add_chunk(turn, grads):
        rows = lambda block: lax.dynamic_slice_in_dim(block, turn * chunk, chunk, 0)
        more = chunk_grads(rows(all_corrected), rows(all_adjoint))
        return (grads[0] + more[0], grads[1] + more[1])

    shapes = jax.eval_shape(chunk_grads, all_corrected[:chunk], all_adjoint[:chunk])
    zeros = tuple(jnp.zeros(shape.shape, shape.dtype) for shape in shapes)
    return lax.fori_loop(0, tokens // chunk, add_chunk, zeros)


def solution(mesh):
    in_specs = (
        P("dp"),
        P("depth", None),
        P("depth", None, None),
        P("depth", None, None),
        P("dp", None),
    )
    out_specs = (P("depth", "dp", None), P("depth", "dp", None))
    return jax.shard_map(shards, mesh=mesh, in_specs=in_specs, out_specs=out_specs, check_vma=False)
```

time: 439 us -> 222 us (0.51)
  waiting for transfers between devices: 237 us -> 39.2 us
  starting transfers between devices: 74.1 us -> 22.8 us
  matrix products: 86.1 us -> 120 us
  between operations: 14.2 us -> 1.17 us
  other arithmetic: 12.5 us -> 18.7 us
  local copies, waits for them, and re-layouts: 13.4 us -> 19.1 us
    all_gather x2 -> x0, waiting for transfers between devices: 72 us -> none  [the longest x1 72 us: shards(): lax.all_gather(delta_all, 'dp', axis=1, tiled=True)]
    psum x1 -> x0, waiting for transfers between devices: 57.6 us -> none  [shards(): start = lax.psum(picked.astype(jnp.bfloat16), 'depth').astype(jnp.float32)]
    ppermute x22, starting transfers between devices: 65.9 us -> 22.8 us  [the longest x12 11.6 us: swapped(): return lax.ppermute(block, axis, [(i, i ^ mask) for i in devices])]
    all_to_all x2 -> x0, waiting for transfers between devices: 41.2 us -> none  [the longest x1 37 us: shards(): lax.all_to_all(hidden_all, 'dp', split_axis=2, concat_axis=1, tiled=True)]
    ppermute x22, waiting for transfers between devices: 65.8 us -> 39.2 us  [the longest x12 29.6 us: swapped(): return lax.ppermute(block, axis, [(i, i ^ mask) for i in devices])]
    dot_general x29, matrix products: 61.1 us -> 77.7 us  [the longest x14 44.7 us: times_transposed(): lax.dot_general(left.astype(jnp.bfloat16), right.astype(jnp.bfloat16), ((...]
    dot_general x2 -> x4, matrix products: 3.7 us -> 15.9 us  [layer_forward(): before = jnp.dot(normed, weight_up, preferred_element_type=jnp.float32)]
    all_to_all x2 -> x0, starting transfers between devices: 8.11 us -> none  [the longest x1 4.59 us: shards(): lax.all_to_all(normed_all, 'dp', split_axis=2, concat_axis=1, tiled=True)]
  transfers between devices with their start and end apart: 27 -> 22, of which waited for: 22 -> 13; matrix products, arithmetic and copies ran while one was open for 9% -> 34% of each run, Pallas kernels for 0% -> 0%
where the time goes in v1:
time: 222 us; the launch traced here: 221 us
  matrix products  120 us (54%)
  waiting for transfers between devices  39.2 us (18%)
  starting transfers between devices  22.8 us (10%)
  local copies, waits for them, and re-layouts  19.1 us (9%)
  other arithmetic  18.7 us (8%)
    dot_general x14, matrix products, times_transposed(): lax.dot_general(left.astype(jnp.bfloat16), right.astype(jnp.bfloat16), ((...  44.7 us
    ppermute x12, waiting for transfers between devices, swapped(): return lax.ppermute(block, axis, [(i, i ^ mask) for i in devices])  29.6 us
    dot_general x8, matrix products, layer_forward(): jnp.dot(hidden, weight_down, preferred_element_type=jnp.float32)  26.4 us
    dot_general x4, matrix products, layer_forward(): before = jnp.dot(normed, weight_up, preferred_element_type=jnp.float32)  15.9 us
    dot_general x4, matrix products, over_tokens(): lax.dot_general(left, right, (((0,), (0,)), ((), ())), preferred_element_...  12.4 us
    dot_general x9, matrix products, times(): jnp.dot(left.astype(jnp.bfloat16), right.astype(jnp.bfloat16), preferred_...  12.4 us
    ppermute x12, starting transfers between devices, swapped(): return lax.ppermute(block, axis, [(i, i ^ mask) for i in devices])  11.6 us
    ppermute x10, starting transfers between devices, rotated(): lax.ppermute(block, axis, [(i, (i + distance) % size) for i in range(size)])  11.2 us
  transfers between devices with their start and end apart: 22, of which 13 were waited for; matrix products, arithmetic and copies ran while one was open for 34% of the time, Pallas kernels for 0%

profile of v1, /device:TPU:0, one launch (start us, length us, event | category | flops | bytes accessed | tf_op | source)
XLA Modules:
  0.0 221.1 jit_solution(17866771391503795746)
XLA Ops:
  4.6 3.9 %collective-permute-start.3 = (bf16[128,512]{1,0:T(8,128)(2,1)S(1)}, bf16[128,512]{1,0:T(8,128)(2,1)S(1)}, u32[]{:S(2)}, u32[]{:S(2)}) collective-permute-start(bf16[128,512]{1,0:T(8,128)(2,1)S(1)} %fusion.461), channel_id=1, source_target_pairs={{0,24},{4,28},{8,16},{12,20},{16,8},{20,12},{24,0},{28,4},{1,25},{... | collective-permute-start | bytes 393224 | tf_op jit(solution)/shard_map/ppermute | solution.py:16
  9.1 3.3 %collective-permute-done.3 = bf16[128,512]{1,0:T(8,128)(2,1)S(1)} collective-permute-done((bf16[128,512]{1,0:T(8,128)(2,1)S(1)}, bf16[128,512]{1,0:T(8,128)(2,1)S(1)}, u32[]{:S(2)}, u32[]{:S(2)}) %collective-permute-start.3) | collective-permute-done | bytes 131104 | tf_op jit(solution)/shard_map/ppermute | solution.py:16
  12.4 2.6 %collective-permute-done.2 = bf16[128,512]{1,0:T(8,128)(2,1)S(1)} collective-permute-done((bf16[128,512]{1,0:T(8,128)(2,1)S(1)}, bf16[128,512]{1,0:T(8,128)(2,1)S(1)}, u32[]{:S(2)}, u32[]{:S(2)}) %collective-permute-start.2) | collective-permute-done | bytes 131104 | tf_op jit(solution)/shard_map/ppermute | solution.py:16
  15.5 3.1 %multiply_reduce_fusion.10 = (f32[128]{0:T(128)S(1)}, f32[128,512]{1,0:T(8,128)S(1)}) fusion(bf16[2,2048,512]{2,1,0:T(8,128)(2,1)} %param.8, bf16[128,512]{1,0:T(8,128)(2,1)S(1)} %get-tuple-element.3, f32[128]{0:T(128)S(1)} %add_rsqrt_fusion.9, bf16[2,512,2048]{2,1,0:T(8,128)(2,1)} %param.7), kind=kOutput, calls=%fused_computation.266 | convolution fusion | flops 538640256 | bytes 4719616 | tf_op jit(solution)/shard_map/dot_general | solution.py:44
  18.6 3.0 %fusion.138 = bf16[128,512]{1,0:T(8,128)(2,1)S(1)} fusion(f32[128,512]{1,0:T(8,128)S(1)} %get-tuple-element.14, bf16[2,2048,512]{2,1,0:T(8,128)(2,1)} %param.8, f32[128]{0:T(128)S(1)} %add_rsqrt_fusion.8, bf16[2,512,2048]{2,1,0:T(8,128)(2,1)} %param.7), kind=kOutput, calls=%fused_computation.133 | convolution fusion | flops 538443776 | bytes 4850176 | tf_op jit(solution)/shard_map/dot_general | solution.py:44
  21.7 4.4 %fusion.16 = f32[512,512]{1,0:T(8,128)} fusion(bf16[2,2048,512]{2,1,0:T(8,128)(2,1)} %param.8, bf16[2,512,2048]{2,1,0:T(8,128)(2,1)} %param.7), kind=kOutput, calls=%fused_computation.32 | convolution fusion | flops 1073741824 | bytes 5242880 | tf_op jit(solution)/shard_map/dot_general | solution.py:63
  27.1 3.1 %multiply_reduce_fusion.8 = (f32[128]{0:T(128)S(1)}, f32[128,512]{1,0:T(8,128)S(1)}) fusion(bf16[2,2048,512]{2,1,0:T(8,128)(2,1)} %param.8, bf16[128,512]{1,0:T(8,128)(2,1)S(1)} %get-tuple-element.3, bf16[128,512]{1,0:T(8,128)(2,1)S(1)} %collective-permute-done.4, f32[128]{0:T(128)S(1)} %add_rsqrt_fusion.7, pred[]{:T(512)S(6)} %eq.20, ...), kind=kOutput, calls=%fused_computation.262 | convolution fusion | flops 538902400 | bytes 4982784 | tf_op jit(solution)/shard_map/dot_general | solution.py:44
  30.2 3.7 %fusion.135 = bf16[128,512]{1,0:T(8,128)(2,1)} fusion(f32[128,512]{1,0:T(8,128)S(1)} %get-tuple-element.16, bf16[2,2048,512]{2,1,0:T(8,128)(2,1)} %param.8, f32[128]{0:T(128)S(1)} %add_rsqrt_fusion.6, bf16[2,512,2048]{2,1,0:T(8,128)(2,1)} %param.7), kind=kOutput, calls=%fused_computation.132 | convolution fusion | flops 538443776 | bytes 4850176 | tf_op jit(solution)/shard_map/dot_general | solution.py:44
  34.7 3.7 %fusion.407 = (bf16[512,512]{1,0:T(8,128)(2,1)S(1)}, f32[512,512]{1,0:T(8,128)S(1)}) fusion(f32[512,512]{1,0:T(8,128)} %fusion.16, bf16[2,2048,512]{2,1,0:T(8,128)(2,1)} %param.8, bf16[2,512,2048]{2,1,0:T(8,128)(2,1)} %param.7), kind=kOutput, calls=%fused_computation.389 | convolution fusion | flops 1074528256 | bytes 6815744 | tf_op jit(solution)/shard_map/dot_general | solution.py:61
  40.5 3.8 %multiply_reduce_fusion.6 = (f32[128]{0:T(128)S(1)}, f32[128,512]{1,0:T(8,128)}) fusion(bf16[2,2048,512]{2,1,0:T(8,128)(2,1)} %param.8, bf16[128,512]{1,0:T(8,128)(2,1)S(1)} %get-tuple-element.3, bf16[128,512]{1,0:T(8,128)(2,1)} %collective-permute-done.5, f32[128]{0:T(128)S(1)} %add_rsqrt_fusion.5, pred[]{:T(512)S(6)} %eq.20, bf16[2,512,2048]{2,1,0:T(8,128)(2,1)} %param.7), kind=kOutput, calls=%fused_computation.258 | convolution fusion | flops 538902400 | bytes 4982784 | tf_op jit(solution)/shard_map/dot_general | solution.py:44
  44.3 3.8 %fusion.120 = f32[128,512]{1,0:T(8,128)} fusion(f32[128,512]{1,0:T(8,128)} %get-tuple-element.18, bf16[2,2048,512]{2,1,0:T(8,128)(2,1)} %param.8, f32[128]{0:T(128)S(1)} %add_rsqrt_fusion.4, bf16[2,512,2048]{2,1,0:T(8,128)(2,1)} %param.7), kind=kOutput, calls=%fused_computation.113 | convolution fusion | flops 538378240 | bytes 4981248 | tf_op jit(solution)/shard_map/dot_general | solution.py:44
  56.7 10.5 %collective-permute-done.9 = bf16[512,512]{1,0:T(8,128)(2,1)S(1)} collective-permute-done((bf16[512,512]{1,0:T(8,128)(2,1)S(1)}, bf16[512,512]{1,0:T(8,128)(2,1)S(1)}, u32[]{:S(2)}, u32[]{:S(2)}) %collective-permute-start.9) | collective-permute-done | bytes 524320 | tf_op jit(solution)/shard_map/ppermute | solution.py:16
  72.9 2.6 %collective-permute-done.10 = bf16[128,512]{1,0:T(8,128)(2,1)S(1)} collective-permute-done((bf16[128,512]{1,0:T(8,128)(2,1)S(1)}, bf16[128,512]{1,0:T(8,128)(2,1)S(1)}, u32[]{:S(2)}, u32[]{:S(2)}) %collective-permute-start.10) | collective-permute-done | bytes 131104 | tf_op jit(solution)/shard_map/ppermute | solution.py:16
  75.6 3.3 %fusion.125 = f32[128,512]{1,0:T(8,128)} fusion(f32[512,512]{1,0:T(8,128)} %copy-done.7, f32[512,512]{1,0:T(8,128)S(1)} %get-tuple-element.12, bf16[512,512]{1,0:T(8,128)(2,1)} %copy-done.5, pred[]{:T(512)S(6)} %eq.22, bf16[512,512]{1,0:T(8,128)(2,1)} %get-tuple-element.7, f32[128,512]{1,0:T(8,128)} %get-tuple-element.24, ...), kind=kOutput, calls=%fused_computation.122 | convolution fusion | flops 337838080 | bytes 3801090 | tf_op jit(solution)/shard_map/dot_general | solution.py:25
  81.3 3.6 %collective-permute-start.13 = (bf16[128,512]{1,0:T(8,128)(2,1)S(1)}, bf16[128,512]{1,0:T(8,128)(2,1)}, u32[]{:S(2)}, u32[]{:S(2)}) collective-permute-start(bf16[128,512]{1,0:T(8,128)(2,1)S(1)} %get-tuple-element.30), channel_id=1, source_target_pairs={{0,3},{1,0},{2,1},{3,2},{4,7},{5,4},{6,5},{7,6},{8,11},{9,8},{10,9... | collective-permute-start | bytes 393224 | tf_op jit(solution)/shard_map/ppermute | solution.py:21
  93.5 4.8 %multiply_reduce_fusion.4 = (f32[128]{0:T(128)S(1)}, f32[128,512]{1,0:T(8,128)}) fusion(f32[128,512]{1,0:T(8,128)} %copy-done.8, f32[128]{0:T(128)S(1)} %add_rsqrt_fusion.2, bf16[2,512,2048]{2,1,0:T(8,128)(2,1)} %param.7, bf16[128,512]{1,0:T(8,128)(2,1)} %param.9, f32[128,2048]{1,0:T(8,128)} %fusion.34, bf16[2,2048,512]{2,1,0:T(8,128)(2,1)} %param.8), kind=kOutput, calls=%fused_computation.250 | convolution fusion | flops 539426688 | bytes 5899264 | tf_op jit(solution)/shard_map/dot_general | solution.py:31
  98.4 5.0 %fusion.225 = (f32[128]{0:T(128)S(1)}, f32[128,512]{1,0:T(8,128)}) fusion(bf16[128,512]{1,0:T(8,128)(2,1)S(1)} %get-tuple-element.30, f32[128]{0:T(128)S(1)} %add_rsqrt_fusion.3, bf16[2,512,2048]{2,1,0:T(8,128)(2,1)} %param.7, f32[128,2048]{1,0:T(8,128)} %copy-done.19, bf16[128,512]{1,0:T(8,128)(2,1)} %param.9, f32[128,512]{1,0:T(8,128)} %get-tuple-element.34, ...), kind=kOutput, calls=%fused_computation.224 | convolution fusion | flops 539950976 | bytes 6293504 | tf_op jit(solution)/shard_map/dot_general | solution.py:31
  120.8 4.9 %multiply_reduce_fusion.3 = (f32[128]{0:T(128)S(1)}, f32[128,512]{1,0:T(8,128)}) fusion(f32[128,512]{1,0:T(8,128)} %copy-done.8, f32[128]{0:T(128)S(1)} %add_rsqrt_fusion.2, bf16[2,512,2048]{2,1,0:T(8,128)(2,1)} %param.7, f32[128,2048]{1,0:T(8,128)} %fusion.34, bf16[2,2048,512]{2,1,0:T(8,128)(2,1)} %param.8, bf16[128,512]{1,0:T(8,128)(2,1)} %collective-permute-done.14, ...), kind=kOutput, calls=%fused_computation.249 | convolution fusion | flops 539688832 | bytes 6030337 | tf_op jit(solution)/shard_map/dot_general | solution.py:31
  127.7 4.9 %fusion.230 = (f32[128]{0:T(128)S(1)}, f32[128,512]{1,0:T(8,128)}) fusion(bf16[128,512]{1,0:T(8,128)(2,1)S(1)} %get-tuple-element.30, f32[128]{0:T(128)S(1)} %add_rsqrt_fusion.3, bf16[2,512,2048]{2,1,0:T(8,128)(2,1)} %param.7, f32[128,2048]{1,0:T(8,128)} %copy-done.19, f32[128,512]{1,0:T(8,128)} %multiply_add_fusion.9, bf16[2,2048,512]{2,1,0:T(8,128)(2,1)} %param.8), kind=kOutput, calls=%fused_computation.229 | convolution fusion | flops 539557760 | bytes 5899264 | tf_op jit(solution)/shard_map/dot_general | solution.py:31
  135.2 5.5 %multiply_convert_fusion.2 = (bf16[512,2048]{1,0:T(8,128)(2,1)S(1)}, f32[512,2048]{1,0:T(8,128)}) fusion(bf16[512,512]{0,1:T(8,128)(2,1)} %fusion.144, bf16[2,512,2048]{2,1,0:T(8,128)(2,1)} %param.7), kind=kOutput, calls=%fused_computation.4 | convolution fusion | flops 1078984704 | bytes 8912896 | tf_op jit(solution)/shard_map/dot_general | solution.py:42
  140.8 3.7 %multiply_reduce_fusion.1 = (f32[512]{0:T(512)S(1)}, f32[512,512]{0,1:T(8,128)}) fusion(bf16[512,2048]{1,0:T(8,128)(2,1)S(1)} %get-tuple-element.25, bf16[2,2048,512]{2,1,0:T(8,128)(2,1)S(1)} %copy-done.24, bf16[512,512]{0,1:T(8,128)(2,1)} %constant_dynamic-update-slice_fusion.4), kind=kOutput, calls=%fused_computation.142 | convolution fusion | flops 1074789888 | bytes 5769216 | tf_op jit(solution)/shard_map/dot_general | solution.py:44
  144.5 5.4 %multiply_reduce_fusion.2 = (f32[128]{0:T(128)}, f32[128,512]{1,0:T(8,128)}) fusion(f32[128,512]{1,0:T(8,128)} %copy-done.8, f32[128]{0:T(128)S(1)} %add_rsqrt_fusion.2, bf16[2,512,2048]{2,1,0:T(8,128)(2,1)} %param.7, f32[128,2048]{1,0:T(8,128)} %fusion.34, bf16[2,2048,512]{2,1,0:T(8,128)(2,1)} %param.8, bf16[128,512]{1,0:T(8,128)(2,1)} %collective-permute-done.15, ...), kind=kOutput, calls=%fused_computation.247 | convolution fusion | flops 539688832 | bytes 6030337 | tf_op jit(solution)/shard_map/dot_general | solution.py:31
  150.5 5.7 %fusion.235 = (f32[128]{0:T(128)}, f32[128,512]{1,0:T(8,128)}) fusion(bf16[128,512]{1,0:T(8,128)(2,1)S(1)} %get-tuple-element.30, f32[128]{0:T(128)S(1)} %add_rsqrt_fusion.3, bf16[2,512,2048]{2,1,0:T(8,128)(2,1)} %param.7, f32[128,2048]{1,0:T(8,128)} %copy-done.19, f32[128,512]{1,0:T(8,128)} %get-tuple-element.42, ...), kind=kOutput, calls=%fused_computation.234 | convolution fusion | flops 540082048 | bytes 6424577 | tf_op jit(solution)/shard_map/dot_general | solution.py:31
  163.7 3.6 %collective-permute-done.17 = bf16[128,512]{1,0:T(8,128)(2,1)S(1)} collective-permute-done((bf16[128,512]{1,0:T(8,128)(2,1)S(1)}, bf16[128,512]{1,0:T(8,128)(2,1)S(1)}, u32[]{:S(2)}, u32[]{:S(2)}) %collective-permute-start.17) | collective-permute-done | bytes 131104 | tf_op jit(solution)/shard_map/ppermute | solution.py:16
  169.6 3.0 %collective-permute-done.18 = bf16[128,512]{1,0:T(8,128)(2,1)S(1)} collective-permute-done((bf16[128,512]{1,0:T(8,128)(2,1)S(1)}, bf16[128,512]{1,0:T(8,128)(2,1)S(1)}, u32[]{:S(2)}, u32[]{:S(2)}) %collective-permute-start.18) | collective-permute-done | bytes 131104 | tf_op jit(solution)/shard_map/ppermute | solution.py:16
  173.3 2.7 %fusion.128 = f32[128,512]{1,0:T(8,128)S(1)} fusion(f32[512,512]{1,0:T(8,128)} %fusion.77, f32[512,512]{1,0:T(8,128)S(1)} %get-tuple-element.12, bf16[512,512]{1,0:T(8,128)(2,1)} %copy-done.5, pred[]{:T(512)S(6)} %eq.22, bf16[512,512]{1,0:T(8,128)(2,1)} %copy-done.3, f32[128,512]{1,0:T(8,128)S(1)} %get-tuple-element.50, bf16[128,512]{1,0:T(8,128)(2,1)} %copy-done.23, ...), kind=kOutput, calls=%fused_computation.125 | convolution fusion | flops 337838080 | bytes 3801090 | tf_op jit(solution)/shard_map/dot_general | solution.py:31
  179.7 6.9 %add_divide_fusion = (f32[512,2048]{1,0:T(8,128)}, f32[512,2048]{1,0:T(8,128)}) fusion(bf16[512,512]{0,1:T(8,128)(2,1)} %multiply_convert_fusion.10, bf16[2,512,2048]{2,1,0:T(8,128)(2,1)} %param.7), kind=kOutput, calls=%fused_computation.3 | convolution fusion | flops 1076887552 | bytes 11010048 | tf_op jit(solution)/shard_map/dot_general | solution.py:42
  188.7 7.8 %collective-permute-done.20 = bf16[128,512]{1,0:T(8,128)(2,1)S(1)} collective-permute-done((bf16[128,512]{1,0:T(8,128)(2,1)S(1)}, bf16[128,512]{1,0:T(8,128)(2,1)S(1)}, u32[]{:S(2)}, u32[]{:S(2)}) %collective-permute-start.20) | collective-permute-done | bytes 131104 | tf_op jit(solution)/shard_map/ppermute | solution.py:21
  196.9 5.0 %multiply_convert_fusion.1 = bf16[512,2048]{1,0:T(8,128)(2,1)S(1)} fusion(f32[512,2048]{1,0:T(8,128)} %get-tuple-element.54, bf16[512,512]{0,1:T(8,128)(2,1)S(1)} %constant_dynamic-update-slice_fusion, bf16[2,2048,512]{2,1,0:T(8,128)(2,1)} %param.8), kind=kOutput, calls=%fused_computation.2 | convolution fusion | flops 1083179008 | bytes 8912896 | tf_op jit(solution)/shard_map/dot_general | solution.py:31
  204.6 3.1 %convolution_bitcast_fusion.2 = f32[1,512,512]{2,1,0:T(8,128)} fusion(bf16[512,512]{0,1:T(8,128)(2,1)S(1)} %constant_dynamic-update-slice_fusion, f32[512,2048]{1,0:T(8,128)} %get-tuple-element.53, s32[]{:T(128)S(6)} %select_n.234, f32[512,2048]{1,0:T(8,128)} %get-tuple-element.54), kind=kOutput, calls=%fused_computation.95 | convolution fusion | flops 268959744 | bytes 3670020 | tf_op jit(solution)/shard_map/dot_general | solution.py:199
  210.3 6.4 %convolution_bitcast_fusion.1 = f32[1,128,2048]{2,1,0:T(8,128)} fusion(f32[512,2048]{1,0:T(8,128)} %get-tuple-element.26, bf16[512,512]{0,1:T(8,128)(2,1)} %copy-done.18, bf16[512,512]{0,1:T(8,128)(2,1)} %fusion.144, s32[]{:T(128)S(6)} %select_n.218, bf16[2,2048,512]{2,1,0:T(8,128)(2,1)} %param.8), kind=kOutput, calls=%fused_computation.19 | convolution fusion | flops 1351614464 | bytes 7995396 | tf_op jit(solution)/shard_map/dot_general | solution.py:199
  216.8 2.8 %pad_maximum_fusion.1 = f32[2,512,512]{2,1,0:T(8,128)} fusion(f32[1,512,512]{2,1,0:T(8,128)} %convolution_bitcast_fusion.2, f32[1,512,512]{2,1,0:T(8,128)S(1)} %convolution_bitcast_fusion.3), kind=kLoop, calls=%fused_computation.27 | loop fusion | flops 524288 | bytes 4194304 | tf_op jit(solution)/shard_map/stack | solution.py:215
  (156 shorter events, 80.1 us)
Async XLA Ops:
  2.9 1.5 collective-permute-start
  4.6 7.8 %collective-permute-start.3 = (bf16[128,512]{1,0:T(8,128)(2,1)S(1)}, bf16[128,512]{1,0:T(8,128)(2,1)S(1)}, u32[]{:S(2)}, u32[]{:S(2)}) collective-permute-start(bf16[128,512]{1,0:T(8,128)(2,1)S(1)} %fusion.461), channel_id=1, source_target_pairs={{0,24},{4,28},{8,16},{12,20},{16,8},{20,12},{24,0},{28,4},{1,25},{... | collective-permute-start | bytes 393224 | tf_op jit(solution)/shard_map/ppermute | solution.py:16
  8.4 6.6 %collective-permute-start.2 = (bf16[128,512]{1,0:T(8,128)(2,1)S(1)}, bf16[128,512]{1,0:T(8,128)(2,1)S(1)}, u32[]{:S(2)}, u32[]{:S(2)}) collective-permute-start(bf16[128,512]{1,0:T(8,128)(2,1)S(1)} %fusion.461), channel_id=1, source_target_pairs={{0,16},{4,20},{8,24},{12,28},{16,0},{20,4},{24,8},{28,12},{1,17},{... | collective-permute-start | bytes 393224 | tf_op jit(solution)/shard_map/ppermute | solution.py:16
  8.9 6.4 %collective-permute-start.1 = (bf16[128,512]{1,0:T(8,128)(2,1)S(1)}, bf16[128,512]{1,0:T(8,128)(2,1)S(1)}, u32[]{:S(2)}, u32[]{:S(2)}) collective-permute-start(bf16[128,512]{1,0:T(8,128)(2,1)S(1)} %fusion.461), channel_id=1, source_target_pairs={{0,8},{4,12},{8,0},{12,4},{16,24},{20,28},{24,16},{28,20},{1,9},{5... | collective-permute-start | bytes 393224 | tf_op jit(solution)/shard_map/ppermute | solution.py:16
  15.5 32.6 %copy-start.13 = (bf16[128,512]{1,0:T(8,128)(2,1)}, bf16[128,512]{1,0:T(8,128)(2,1)S(1)}, u32[]{:S(2)}) copy-start(bf16[128,512]{1,0:T(8,128)(2,1)S(1)} %get-tuple-element.3) | copy-start | bytes 393220
  21.7 5.3 %collective-permute-start.4 = (bf16[128,512]{1,0:T(8,128)(2,1)S(1)}, bf16[128,512]{1,0:T(8,128)(2,1)S(1)}, u32[]{:S(2)}, u32[]{:S(2)}) collective-permute-start(bf16[128,512]{1,0:T(8,128)(2,1)S(1)} %fusion.138), channel_id=1, source_target_pairs={{0,4},{4,8},{8,12},{12,16},{16,20},{20,24},{24,28},{28,0},{1,5},{5... | collective-permute-start | bytes 393224 | tf_op jit(solution)/shard_map/ppermute | solution.py:21
  33.9 5.6 %collective-permute-start.5 = (bf16[128,512]{1,0:T(8,128)(2,1)}, bf16[128,512]{1,0:T(8,128)(2,1)}, u32[]{:S(2)}, u32[]{:S(2)}) collective-permute-start(bf16[128,512]{1,0:T(8,128)(2,1)} %fusion.135), channel_id=1, source_target_pairs={{0,4},{4,8},{8,12},{12,16},{16,20},{20,24},{24,28},{28,0},{1,5},{5... | collective-permute-start | bytes 393224 | tf_op jit(solution)/shard_map/ppermute | solution.py:21
  38.4 9.7 %copy-start.17 = (bf16[512,512]{1,0:T(8,128)(2,1)}, bf16[512,512]{1,0:T(8,128)(2,1)S(1)}, u32[]{:S(2)}) copy-start(bf16[512,512]{1,0:T(8,128)(2,1)S(1)} %get-tuple-element.9) | copy-start | bytes 1572868
  38.4 11.0 %collective-permute-start.7 = (bf16[512,512]{1,0:T(8,128)(2,1)S(1)}, bf16[512,512]{1,0:T(8,128)(2,1)S(1)}, u32[]{:S(2)}, u32[]{:S(2)}) collective-permute-start(bf16[512,512]{1,0:T(8,128)(2,1)S(1)} %get-tuple-element.9), channel_id=1, source_target_pairs={{0,4},{4,0},{8,12},{12,8},{16,20},{20,16},{24,28},{28,24},{1,5},{5... | collective-permute-start | bytes 1572872 | tf_op jit(solution)/shard_map/ppermute | solution.py:16
  49.4 23.5 %copy-start.15 = (f32[128,512]{1,0:T(8,128)}, f32[128,512]{1,0:T(8,128)S(1)}, u32[]{:S(2)}) copy-start(f32[128,512]{1,0:T(8,128)S(1)} %get-tuple-element.20) | copy-start | bytes 786436
  49.4 6.3 %collective-permute-start.6 = (bf16[128,512]{1,0:T(8,128)(2,1)S(1)}, bf16[128,512]{1,0:T(8,128)(2,1)S(1)}, u32[]{:S(2)}, u32[]{:S(2)}) collective-permute-start(bf16[128,512]{1,0:T(8,128)(2,1)S(1)} %get-tuple-element.19), channel_id=1, source_target_pairs={{0,4},{4,0},{8,12},{12,8},{16,20},{20,16},{24,28},{28,24},{1,5},{5... | collective-permute-start | bytes 393224 | tf_op jit(solution)/shard_map/ppermute | solution.py:16
  52.4 14.9 %collective-permute-start.9 = (bf16[512,512]{1,0:T(8,128)(2,1)S(1)}, bf16[512,512]{1,0:T(8,128)(2,1)S(1)}, u32[]{:S(2)}, u32[]{:S(2)}) collective-permute-start(bf16[512,512]{1,0:T(8,128)(2,1)S(1)} %get-tuple-element.11), channel_id=1, source_target_pairs={{0,8},{4,12},{8,0},{12,4},{16,24},{20,28},{24,16},{28,20},{1,9},{5... | collective-permute-start | bytes 1572872 | tf_op jit(solution)/shard_map/ppermute | solution.py:16
  54.2 17.8 %copy-start.7 = (f32[512,512]{1,0:T(8,128)}, f32[512,512]{1,0:T(8,128)S(1)}, u32[]{:S(2)}) copy-start(f32[512,512]{1,0:T(8,128)S(1)} %fusion.76) | copy-start | bytes 3145732
  55.7 19.9 %copy-start.21 = (bf16[128,512]{1,0:T(8,128)(2,1)}, bf16[128,512]{1,0:T(8,128)(2,1)S(1)}, u32[]{:S(2)}) copy-start(bf16[128,512]{1,0:T(8,128)(2,1)S(1)} %collective-permute-done.6) | copy-start | bytes 393220
  56.0 13.6 %collective-permute-start.8 = (bf16[128,512]{1,0:T(8,128)(2,1)S(1)}, bf16[128,512]{1,0:T(8,128)(2,1)S(1)}, u32[]{:S(2)}, u32[]{:S(2)}) collective-permute-start(bf16[128,512]{1,0:T(8,128)(2,1)S(1)} %get-tuple-element.21), channel_id=1, source_target_pairs={{0,8},{4,12},{8,0},{12,4},{16,24},{20,28},{24,16},{28,20},{1,9},{5... | collective-permute-start | bytes 393224 | tf_op jit(solution)/shard_map/ppermute | solution.py:16
  70.5 5.0 %collective-permute-start.10 = (bf16[128,512]{1,0:T(8,128)(2,1)S(1)}, bf16[128,512]{1,0:T(8,128)(2,1)S(1)}, u32[]{:S(2)}, u32[]{:S(2)}) collective-permute-start(bf16[128,512]{1,0:T(8,128)(2,1)S(1)} %get-tuple-element.23), channel_id=1, source_target_pairs={{0,16},{4,20},{8,24},{12,28},{16,0},{20,4},{24,8},{28,12},{1,17},{... | collective-permute-start | bytes 393224 | tf_op jit(solution)/shard_map/ppermute | solution.py:16
  81.3 33.1 %collective-permute-start.13 = (bf16[128,512]{1,0:T(8,128)(2,1)S(1)}, bf16[128,512]{1,0:T(8,128)(2,1)}, u32[]{:S(2)}, u32[]{:S(2)}) collective-permute-start(bf16[128,512]{1,0:T(8,128)(2,1)S(1)} %get-tuple-element.30), channel_id=1, source_target_pairs={{0,3},{1,0},{2,1},{3,2},{4,7},{5,4},{6,5},{7,6},{8,11},{9,8},{10,9... | collective-permute-start | bytes 393224 | tf_op jit(solution)/shard_map/ppermute | solution.py:21
  84.9 26.2 %collective-permute-start.12 = (bf16[128,512]{1,0:T(8,128)(2,1)S(1)}, bf16[128,512]{1,0:T(8,128)(2,1)}, u32[]{:S(2)}, u32[]{:S(2)}) collective-permute-start(bf16[128,512]{1,0:T(8,128)(2,1)S(1)} %get-tuple-element.30), channel_id=1, source_target_pairs={{0,2},{1,3},{2,0},{3,1},{4,6},{5,7},{6,4},{7,5},{8,10},{9,11},{10,... | collective-permute-start | bytes 393224 | tf_op jit(solution)/shard_map/ppermute | solution.py:21
  84.9 22.9 %collective-permute-start.11 = (bf16[128,512]{1,0:T(8,128)(2,1)S(1)}, bf16[128,512]{1,0:T(8,128)(2,1)}, u32[]{:S(2)}, u32[]{:S(2)}) collective-permute-start(bf16[128,512]{1,0:T(8,128)(2,1)S(1)} %get-tuple-element.30), channel_id=1, source_target_pairs={{0,1},{1,2},{2,3},{3,0},{4,5},{5,6},{6,7},{7,4},{8,9},{9,10},{10,1... | collective-permute-start | bytes 393224 | tf_op jit(solution)/shard_map/ppermute | solution.py:21
  105.4 15.4 %collective-permute-start.14 = (bf16[128,512]{1,0:T(8,128)(2,1)}, bf16[128,512]{1,0:T(8,128)(2,1)}, u32[]{:S(2)}, u32[]{:S(2)}) collective-permute-start(bf16[128,512]{1,0:T(8,128)(2,1)} %fusion.229), channel_id=1, source_target_pairs={{0,28},{4,0},{8,4},{12,8},{16,12},{20,16},{24,20},{28,24},{1,29},{... | collective-permute-start | bytes 393224 | tf_op jit(solution)/shard_map/ppermute | solution.py:21
  133.8 7.0 %copy-start.24 = (bf16[2,2048,512]{2,1,0:T(8,128)(2,1)S(1)}, bf16[2,2048,512]{2,1,0:T(8,128)(2,1)}, u32[]{:S(2)}) copy-start(bf16[2,2048,512]{2,1,0:T(8,128)(2,1)} %param.8) | copy-start | bytes 12582916
  133.8 10.7 %collective-permute-start.15 = (bf16[128,512]{1,0:T(8,128)(2,1)S(1)}, bf16[128,512]{1,0:T(8,128)(2,1)}, u32[]{:S(2)}, u32[]{:S(2)}) collective-permute-start(bf16[128,512]{1,0:T(8,128)(2,1)S(1)} %fusion.234), channel_id=1, source_target_pairs={{0,28},{4,0},{8,4},{12,8},{16,12},{20,16},{24,20},{28,24},{1,29},{... | collective-permute-start | bytes 393224 | tf_op jit(solution)/shard_map/ppermute | solution.py:21
  156.2 11.1 %copy-start.4 = (bf16[512,512]{1,0:T(8,128)(2,1)S(1)}, bf16[512,512]{1,0:T(8,128)(2,1)}, u32[]{:S(2)}) copy-start(bf16[512,512]{1,0:T(8,128)(2,1)} %get-tuple-element.7) | copy-start | bytes 1572868
  156.2 13.0 %copy-start.6 = (f32[512,512]{1,0:T(8,128)S(1)}, f32[512,512]{1,0:T(8,128)}, u32[]{:S(2)}) copy-start(f32[512,512]{1,0:T(8,128)} %fusion.77) | copy-start | bytes 3145732
  158.8 10.7 %copy-start.14 = (f32[128,512]{1,0:T(8,128)}, f32[128,512]{1,0:T(8,128)S(1)}, u32[]{:S(2)}) copy-start(f32[128,512]{1,0:T(8,128)S(1)} %get-tuple-element.46) | copy-start | bytes 786436
  158.9 1.4 collective-permute-start.16
  161.6 5.6 %collective-permute-start.17 = (bf16[128,512]{1,0:T(8,128)(2,1)S(1)}, bf16[128,512]{1,0:T(8,128)(2,1)S(1)}, u32[]{:S(2)}, u32[]{:S(2)}) collective-permute-start(bf16[128,512]{1,0:T(8,128)(2,1)S(1)} %get-tuple-element.47), channel_id=1, source_target_pairs={{0,8},{4,12},{8,0},{12,4},{16,24},{20,28},{24,16},{28,20},{1,9},{5... | collective-permute-start | bytes 393224 | tf_op jit(solution)/shard_map/ppermute | solution.py:16
  162.7 13.2 %copy-start.16 = (bf16[128,512]{1,0:T(8,128)(2,1)S(1)}, bf16[128,512]{1,0:T(8,128)(2,1)}, u32[]{:S(2)}) copy-start(bf16[128,512]{1,0:T(8,128)(2,1)} %param.9) | copy-start | bytes 393220
  167.6 5.0 %collective-permute-start.18 = (bf16[128,512]{1,0:T(8,128)(2,1)S(1)}, bf16[128,512]{1,0:T(8,128)(2,1)S(1)}, u32[]{:S(2)}, u32[]{:S(2)}) collective-permute-start(bf16[128,512]{1,0:T(8,128)(2,1)S(1)} %get-tuple-element.49), channel_id=1, source_target_pairs={{0,16},{4,20},{8,24},{12,28},{16,0},{20,4},{24,8},{28,12},{1,17},{... | collective-permute-start | bytes 393224 | tf_op jit(solution)/shard_map/ppermute | solution.py:16
  177.1 11.4 %collective-permute-start.19 = (bf16[128,512]{1,0:T(8,128)(2,1)S(1)}, bf16[128,512]{1,0:T(8,128)(2,1)S(1)}, u32[]{:S(2)}, u32[]{:S(2)}) collective-permute-start(bf16[128,512]{1,0:T(8,128)(2,1)S(1)} %fusion.142), channel_id=1, source_target_pairs={{0,1},{1,2},{2,3},{3,0},{4,5},{5,6},{6,7},{7,4},{8,9},{9,10},{10,1... | collective-permute-start | bytes 393224 | tf_op jit(solution)/shard_map/ppermute | solution.py:21
  186.7 10.0 %collective-permute-start.21 = (bf16[128,512]{1,0:T(8,128)(2,1)S(1)}, bf16[128,512]{1,0:T(8,128)(2,1)S(1)}, u32[]{:S(2)}, u32[]{:S(2)}) collective-permute-start(bf16[128,512]{1,0:T(8,128)(2,1)S(1)} %fusion.142), channel_id=1, source_target_pairs={{0,3},{1,0},{2,1},{3,2},{4,7},{5,4},{6,5},{7,6},{8,11},{9,8},{10,9... | collective-permute-start | bytes 393224 | tf_op jit(solution)/shard_map/ppermute | solution.py:21
  188.3 8.2 %collective-permute-start.20 = (bf16[128,512]{1,0:T(8,128)(2,1)S(1)}, bf16[128,512]{1,0:T(8,128)(2,1)S(1)}, u32[]{:S(2)}, u32[]{:S(2)}) collective-permute-start(bf16[128,512]{1,0:T(8,128)(2,1)S(1)} %fusion.142), channel_id=1, source_target_pairs={{0,2},{1,3},{2,0},{3,1},{4,6},{5,7},{6,4},{7,5},{8,10},{9,11},{10,... | collective-permute-start | bytes 393224 | tf_op jit(solution)/shard_map/ppermute | solution.py:21
  (15 other events, 39.6 us)

commit v2 on v0

v2 whole, which is shorter than its diff:
```python
import functools

import jax
import jax.numpy as jnp
from jax import lax
from jax.experimental import pallas as pl
from jax.experimental.pallas import tpu as pltpu
from jax.sharding import PartitionSpec as P

RELAX = 3


EPSILON = 1e-06
GAMMA = 0.05
CHUNK = 512
MIB = 1 << 20

LOW = jnp.bfloat16
FULL = jnp.float32


def swapped(block, axis, mask):
    devices = range(lax.axis_size(axis))
    return lax.ppermute(block, axis, [(i, i ^ mask) for i in devices])


def rotated(block, axis, distance):
    size = lax.axis_size(axis)
    return lax.ppermute(block, axis, [(i, (i + distance) % size) for i in range(size)])


def dot(left, right):
    return jnp.dot(left.astype(LOW), right.astype(LOW), preferred_element_type=FULL)


def dot_transposed(left, right):
    return lax.dot_general(
        left.astype(LOW), right.astype(LOW), (((1,), (1,)), ((), ())), preferred_element_type=FULL
    )


def call(body, name, flops, limit, out_shapes, position, *args):
    whole = pl.BlockSpec(memory_space=pltpu.VMEM)
    moved = sum(a.size * a.dtype.itemsize for a in args)
    return pl.pallas_call(
        body,
        out_shape=out_shapes,
        in_specs=[pl.BlockSpec(memory_space=pltpu.SMEM)] + [whole] * len(args),
        out_specs=jax.tree.map(lambda unused: whole, out_shapes),
        name=name,
        compiler_params=pltpu.CompilerParams(vmem_limit_bytes=limit * MIB),
        cost_estimate=pl.CostEstimate(flops=flops, bytes_accessed=moved // 4, transcendentals=0),
    )(position, *args)


def shape(dims, kind):
    return jax.ShapeDtypeStruct(dims, kind)


def row_scale(state):
    return lax.rsqrt(jnp.mean(state * state, axis=-1, keepdims=True) + EPSILON)


def block_forward(state, up_ref, down_ref):
    for layer in range(up_ref.shape[0]):
        normed = (state * row_scale(state)).astype(LOW)
        before = dot(normed, up_ref[layer])
        hidden = (before / (1.0 + jnp.exp(-before))).astype(LOW)
        state = state + dot(hidden, down_ref[layer])
    return state


def block_adjoint(adjoint, slope_ref, unit_ref, scale_ref, up_ref, down_ref):
    for layer in reversed(range(up_ref.shape[0])):
        toward_hidden = dot_transposed(adjoint, down_ref[layer])
        delta = (toward_hidden * slope_ref[layer]).astype(LOW)
        toward_normed = dot_transposed(delta, up_ref[layer])
        unit = unit_ref[layer]
        inner = jnp.mean(toward_normed * unit, axis=-1, keepdims=True)
        adjoint = adjoint + scale_ref[layer] * (toward_normed - unit * inner)
    return adjoint


def save_forward(state, up_ref, down_ref, slope_ref, unit_ref, scale_ref, normed_ref, hidden_ref):
    layers = up_ref.shape[0]
    for layer in range(layers):
        scale = row_scale(state)
        unit = state * scale
        normed = unit.astype(LOW)
        before = dot(normed, up_ref[layer])
        sigma = 1.0 / (1.0 + jnp.exp(-before))
        slope_ref[layer] = sigma * (1.0 + before * (1.0 - sigma))
        unit_ref[layer] = unit
        scale_ref[layer] = scale
        if normed_ref is not None:
            normed_ref[layer] = normed
        if hidden_ref is not None or layer < layers - 1:
            hidden = (before * sigma).astype(LOW)
            if hidden_ref is not None:
                hidden_ref[layer] = hidden
            if layer < layers - 1:
                state = state + dot(hidden, down_ref[layer])


def coarse_kernel(position_ref, up_ref, down_ref, out_ref):
    total = dot(up_ref[0], down_ref[0])
    for layer in range(1, up_ref.shape[0]):
        total = total + dot(up_ref[layer], down_ref[layer])
    out_ref[...] = (GAMMA * total).astype(LOW)


def joined(left, right):
    return left.astype(FULL) + right.astype(FULL) + dot(left, right)


def join_kernel(bit, last, position_ref, whole_ref, other_ref, *refs):
    upper = ((position_ref[0] >> bit) & 1) == 1
    whole, other = whole_ref[...], other_ref[...]
    low = jnp.where(upper, other, whole)
    high = jnp.where(upper, whole, other)
    refs = list(refs)
    zeros = jnp.zeros_like(low)
    if bit > 0:
        before, after = refs.pop(0)[...], refs.pop(0)[...]
        prefix = jnp.where(upper, joined(low, before).astype(LOW), before)
        suffix = jnp.where(upper, after, joined(after, high).astype(LOW))
    else:
        prefix = jnp.where(upper, low, zeros)
        suffix = jnp.where(upper, zeros, high)
    refs[0][...] = low
    refs[1][...] = high
    refs[2][...] = prefix
    refs[3][...] = suffix
    if not last:
        refs[4][...] = joined(low, high).astype(LOW)


def matrix_scan(own, position, bits):
    width = own.shape[0]
    square = shape(own.shape, LOW)
    whole, prefix, suffix = own, None, None
    steps = []
    for bit in range(bits - 1):
        last = bit == bits - 2
        other = swapped(whole, "depth", 1 << bit)
        args = (whole, other) if bit == 0 else (whole, other, prefix, suffix)
        outs = call(
            functools.partial(join_kernel, bit, last),
            f"join_{bit}",
            6 * width**3,
            12,
            [square] * (4 if last else 5),
            position,
            *args,
        )
        steps.append((prefix, suffix, outs[0], outs[1]))
        prefix, suffix = outs[2], outs[3]
        whole = None if last else outs[4]
    steps.append((prefix, suffix, None, None))
    return steps


def scan_values(forward, bit, position_ref, value_ref, other_ref):
    upper = ((position_ref[0] >> bit) & 1) == 1
    value, other = value_ref[...].astype(FULL), other_ref[...].astype(FULL)
    lower_value = jnp.where(upper, other, value)
    upper_value = jnp.where(upper, value, other)
    if forward:
        return upper, lower_value, upper_value
    return jnp.logical_not(upper), upper_value, lower_value


def scan_kernel(forward, bit, position_ref, value_ref, other_ref, matrix_ref, *refs):
    receives, donor, keep = scan_values(forward, bit, position_ref, value_ref, other_ref)
    times = dot if forward else dot_transposed
    if bit == 0:
        out_ref, next_ref = refs
        total = jnp.where(receives, donor, jnp.zeros_like(donor))
    else:
        total_ref, part_ref, out_ref, next_ref = refs
        more = donor + times(donor, part_ref[...])
        total = total_ref[...] + jnp.where(receives, more, jnp.zeros_like(more))
    out_ref[...] = total
    next_ref[...] = (keep + donor + times(donor, matrix_ref[...])).astype(LOW)


def scan_end(forward, bit, position_ref, value_ref, other_ref, total_ref, part_ref):
    receives, donor, unused = scan_values(forward, bit, position_ref, value_ref, other_ref)
    times = dot if forward else dot_transposed
    more = donor + times(donor, part_ref[...])
    return total_ref[...] + jnp.where(receives, more, jnp.zeros_like(more))


def shards(token_ids, embedding, w_up, w_down, cotangent):
    depth = lax.axis_size("depth")
    bits = depth.bit_length() - 1
    assert depth == 1 << bits and bits >= 2
    position = lax.axis_index("depth")
    place = position.reshape(1).astype(jnp.int32)
    layers, width, inner_width = w_up.shape
    rows = token_ids.shape[0]
    layer_flops = 4 * rows * width * inner_width
    vocab_rows = embedding.shape[0]
    local_ids = token_ids - position * vocab_rows
    inside = (local_ids >= 0) & (local_ids < vocab_rows)
    picked = jnp.take(embedding, jnp.clip(local_ids, 0, vocab_rows - 1), axis=0)
    picked = jnp.where(inside[:, None], picked, jnp.zeros_like(picked))
    picked = picked + swapped(picked, "depth", 1)
    arrivals = [swapped(picked, "depth", mask) for mask in range(2, depth, 2)]
    for arrival in arrivals:
        picked = picked + arrival
    start = picked

    own = call(
        coarse_kernel,
        "coarse",
        4 * width * width * inner_width,
        12,
        shape((width, width), LOW),
        place,
        w_up,
        w_down,
    )
    steps = matrix_scan(own, place, bits)
    state_low = shape((rows, width), LOW)
    state_full = shape((rows, width), FULL)

    def forward_kernel(position_ref, start_ref, arrived_ref, up_ref, down_ref, out_ref):
        state = jnp.where(position_ref[0] == 0, start_ref[...], arrived_ref[...]).astype(FULL)
        out_ref[...] = block_forward(state, up_ref, down_ref).astype(LOW)

    def value_kernel(position_ref, start_ref, arrived_ref, own_ref, up_ref, down_ref, out_ref):
        state = jnp.where(position_ref[0] == 0, start_ref[...], arrived_ref[...]).astype(FULL)
        ended = block_forward(state, up_ref, down_ref)
        change = ended - state - dot(state, own_ref[...])
        out_ref[...] = jnp.where(position_ref[0] == 0, ended, change).astype(LOW)

    arrived = start
    for sweep in range(RELAX - 1):
        ended = call(
            forward_kernel,
            f"forward_{sweep}",
            layers * layer_flops,
            12,
            state_low,
            place,
            start,
            arrived,
            w_up,
            w_down,
        )
        arrived = rotated(ended, "depth", 1)
    value = call(
        value_kernel,
        "forward_value",
        layers * layer_flops,
        12,
        state_low,
        place,
        start,
        arrived,
        own,
        w_up,
        w_down,
    )

    def scanned(forward, value):
        total = None
        for bit in range(bits - 1):
            prefix, suffix, low, high = steps[bit]
            other = swapped(value, "depth", 1 << bit)
            args = (value, other, high if forward else low)
            if bit > 0:
                args = args + (total, prefix if forward else suffix)
            total, value = call(
                functools.partial(scan_kernel, forward, bit),
                f"scan_{int(forward)}_{bit}",
                4 * rows * width * width,
                8,
                [state_full, state_low],
                place,
                *args,
            )
        other = swapped(value, "depth", 1 << (bits - 1))
        prefix, suffix, unused, unused = steps[-1]
        return (value, other, total, prefix if forward else suffix)

    saved_shapes = lambda count: [
        shape((layers, count, inner_width), FULL),
        shape((layers, count, width), FULL),
        shape((layers, count, 1), FULL),
    ]

    def states_kernel(
        position_ref, value_ref, other_ref, total_ref, part_ref, start_ref, up_ref, down_ref,
        low_ref, slope_ref, unit_ref, scale_ref,
    ):
        corrected = scan_end(
            True, bits - 1, position_ref, value_ref, other_ref, total_ref, part_ref
        )
        corrected = jnp.where(position_ref[0] == 0, start_ref[...], corrected.astype(LOW))
        low_ref[...] = corrected
        save_forward(
            corrected.astype(FULL), up_ref, down_ref, slope_ref, unit_ref, scale_ref, None, None
        )

    corrected, slope, unit, scale = call(
        states_kernel,
        "states",
        layers * layer_flops,
        12,
        [state_low] + saved_shapes(rows),
        place,
        *scanned(True, value),
        start,
        w_up,
        w_down,
    )

    def adjoint_kernel(
        position_ref, final_ref, arrived_ref, slope_ref, unit_ref, scale_ref, up_ref, down_ref,
        out_ref,
    ):
        ends = position_ref[0] == depth - 1
        adjoint = jnp.where(ends, final_ref[...], arrived_ref[...]).astype(FULL)
        out_ref[...] = block_adjoint(
            adjoint, slope_ref, unit_ref, scale_ref, up_ref, down_ref
        ).astype(LOW)

    def adjoint_value_kernel(
        position_ref, final_ref, arrived_ref, own_ref, slope_ref, unit_ref, scale_ref, up_ref,
        down_ref, out_ref,
    ):
        ends = position_ref[0] == depth - 1
        adjoint = jnp.where(ends, final_ref[...], arrived_ref[...]).astype(FULL)
        begun = block_adjoint(adjoint, slope_ref, unit_ref, scale_ref, up_ref, down_ref)
        change = begun - adjoint - dot_transposed(adjoint, own_ref[...])
        out_ref[...] = jnp.where(ends, begun, change).astype(LOW)

    arrived = cotangent
    for sweep in range(RELAX - 1):
        begun = call(
            adjoint_kernel,
            f"adjoint_{sweep}",
            layers * layer_flops,
            12,
            state_low,
            place,
            cotangent,
            arrived,
            slope,
            unit,
            scale,
            w_up,
            w_down,
        )
        arrived = rotated(begun, "depth", -1)
    value = call(
        adjoint_value_kernel,
        "adjoint_value",
        layers * layer_flops,
        12,
        state_low,
        place,
        cotangent,
        arrived,
        own,
        slope,
        unit,
        scale,
        w_up,
        w_down,
    )

    def end_kernel(
        position_ref, value_ref, other_ref, total_ref, part_ref, final_ref, out_ref
    ):
        adjoint = scan_end(
            False, bits - 1, position_ref, value_ref, other_ref, total_ref, part_ref
        )
        ends = position_ref[0] == depth - 1
        out_ref[...] = jnp.where(ends, final_ref[...], adjoint.astype(LOW))

    adjoint = call(
        end_kernel,
        "scan_end",
        2 * rows * width * width,
        8,
        state_low,
        place,
        *scanned(False, value),
        cotangent,
    )

    parts = lax.axis_size("dp")
    part = lax.axis_index("dp")
    pieces = lambda block: [block] + [rotated(block, "dp", d) for d in range(1, parts)]
    corrected_pieces = pieces(corrected)
    adjoint_pieces = pieces(adjoint)

    def own_rows(block):
        size = block.shape[2] // parts
        return jnp.swapaxes(lax.dynamic_slice_in_dim(block, part * size, size, 2), 1, 2)

    def recompute_kernel(count, position_ref, *refs):
        state = jnp.concatenate([ref[...] for ref in refs[:count]], axis=0).astype(FULL)
        save_forward(state, *refs[count:])

    def grads_kernel(count, position_ref, *refs):
        adjoint = jnp.concatenate([ref[...] for ref in refs[:count]], axis=0).astype(FULL)
        slope_ref, unit_ref, scale_ref, normed_ref, hidden_ref = refs[count : count + 5]
        up_ref, down_ref, grad_up_ref, grad_down_ref = refs[count + 5 :]
        for layer in reversed(range(layers)):
            low = adjoint.astype(LOW)
            grad_down_ref[layer] = dot(hidden_ref[layer], low)
            toward_hidden = dot_transposed(low, down_ref[layer])
            delta = (toward_hidden * slope_ref[layer]).astype(LOW)
            grad_up_ref[layer] = dot(normed_ref[layer], delta)
            if layer > 0:
                toward_normed = dot_transposed(delta, up_ref[layer])
                unit = unit_ref[layer]
                inner = jnp.mean(toward_normed * unit, axis=-1, keepdims=True)
                adjoint = adjoint + scale_ref[layer] * (toward_normed - unit * inner)

    group = max(1, min(parts, CHUNK // rows))
    grads = None
    for begin in range(0, parts, group):
        chosen = slice(begin, min(begin + group, parts))
        count = len(range(parts)[chosen])
        tokens = count * rows
        inputs = corrected_pieces[chosen]
        if grads is not None:
            inputs, grads = lax.optimization_barrier((inputs, grads))
        slope, unit, scale, normed, hidden = call(
            functools.partial(recompute_kernel, count),
            f"recompute_{begin}",
            layers * layer_flops * count,
            24,
            saved_shapes(tokens)
            + [shape((layers, tokens, width), LOW), shape((layers, tokens, inner_width), LOW)],
            place,
            *inputs,
            w_up,
            w_down,
        )
        more = call(
            functools.partial(grads_kernel, count),
            f"grads_{begin}",
            layers * layer_flops * count,
            24,
            [
                shape((layers, width // parts, inner_width), FULL),
                shape((layers, inner_width // parts, width), FULL),
            ],
            place,
            *adjoint_pieces[chosen],
            slope,
            unit,
            scale,
            own_rows(normed),
            own_rows(hidden),
            w_up,
            w_down,
        )
        grads = more if grads is None else [a + b for a, b in zip(grads, more)]
    return tuple(grads)


def solution(mesh):
    in_specs = (
        P("dp"),
        P("depth", None),
        P("depth", None, None),
        P("depth", None, None),
        P("dp", None),
    )
    out_specs = (P("depth", "dp", None), P("depth", "dp", None))
    return jax.shard_map(shards, mesh=mesh, in_specs=in_specs, out_specs=out_specs, check_vma=False)
```

time: 439 us -> 153 us (0.35)
  waiting for transfers between devices: 237 us -> 46.1 us
  matrix products: 86.1 us -> 0 us
  starting transfers between devices: 74.1 us -> 24.8 us
  Pallas kernels: 0 us -> 35 us
  local copies, waits for them, and re-layouts: 13.4 us -> 44 us
  between operations: 14.2 us -> 0.95 us
  other arithmetic: 12.5 us -> 1.01 us
    dot_general x38 -> x0, matrix products: 86.1 us -> none  [the longest x7 26.4 us: layer_adjoint(): lax.dot_general(delta, weight_up, (((1,), (1,)), ((), ())), preferred_ele...]
    all_gather x2 -> x0, waiting for transfers between devices: 72 us -> none  [the longest x1 72 us: shards(): lax.all_gather(delta_all, 'dp', axis=1, tiled=True)]
    psum x1 -> x0, waiting for transfers between devices: 57.6 us -> none  [shards(): start = lax.psum(picked.astype(jnp.bfloat16), 'depth').astype(jnp.float32)]
    all_to_all x2 -> x0, waiting for transfers between devices: 41.2 us -> none  [the longest x1 37 us: shards(): lax.all_to_all(hidden_all, 'dp', split_axis=2, concat_axis=1, tiled=True)]
    ppermute x22, starting transfers between devices: 65.9 us -> 24.8 us  [the longest x12 12.6 us: swapped(): return lax.ppermute(block, axis, [(i, i ^ mask) for i in devices])]
    pallas_call x0 -> x17, Pallas kernels: none -> 35 us  [call(): pl.pallas_call(body, out_shape=out_shapes, in_specs=[pl.BlockSpec(memory_...]
    unnamed x33 -> x54, local copies, waits for them, and re-layouts: 5.5 us -> 32.3 us
    ppermute x22, waiting for transfers between devices: 65.8 us -> 46.1 us  [the longest x10 34.4 us: rotated(): lax.ppermute(block, axis, [(i, (i + distance) % size) for i in range(size)])]
  transfers between devices with their start and end apart: 27 -> 22, of which waited for: 22 -> 13; matrix products, arithmetic and copies ran while one was open for 9% -> 7% of each run, Pallas kernels for 0% -> 10%
where the time goes in v2:
time: 153 us; the launch traced here: 152 us
  waiting for transfers between devices  46.1 us (30%)
  local copies, waits for them, and re-layouts  44 us (29%)
  Pallas kernels  35 us (23%)
  starting transfers between devices  24.8 us (16%)
    pallas_call x17, Pallas kernels, call(): pl.pallas_call(body, out_shape=out_shapes, in_specs=[pl.BlockSpec(memory_...  35 us
    ppermute x10, waiting for transfers between devices, rotated(): lax.ppermute(block, axis, [(i, (i + distance) % size) for i in range(size)])  34.4 us
    unnamed x54, local copies, waits for them, and re-layouts  32.3 us
    ppermute x12, starting transfers between devices, swapped(): return lax.ppermute(block, axis, [(i, i ^ mask) for i in devices])  12.6 us
    ppermute x10, starting transfers between devices, rotated(): lax.ppermute(block, axis, [(i, (i + distance) % size) for i in range(size)])  12.2 us
    ppermute x12, waiting for transfers between devices, swapped(): return lax.ppermute(block, axis, [(i, i ^ mask) for i in devices])  11.6 us
    pallas_call x2, local copies, waits for them, and re-layouts, call(): pl.pallas_call(body, out_shape=out_shapes, in_specs=[pl.BlockSpec(memory_...  8.54 us
  transfers between devices with their start and end apart: 22, of which 13 were waited for; matrix products, arithmetic and copies ran while one was open for 7% of the time, Pallas kernels for 10%

profile of v2, /device:TPU:0, one launch (start us, length us, event | category | flops | bytes accessed | tf_op | source)
XLA Modules:
  0.0 151.8 jit_solution(9343037911834560653)
XLA Ops:
  4.6 3.9 %collective-permute-start.3 = (bf16[128,512]{1,0:T(8,128)(2,1)S(1)}, bf16[128,512]{1,0:T(8,128)(2,1)S(1)}, u32[]{:S(2)}, u32[]{:S(2)}) collective-permute-start(bf16[128,512]{1,0:T(8,128)(2,1)S(1)} %fusion), channel_id=1, source_target_pairs={{0,24},{4,28},{8,16},{12,20},{16,8},{20,12},{24,0},{28,4},{1,25},{... | collective-permute-start | bytes 393224 | tf_op jit(solution)/shard_map/ppermute | solution.py:24
  9.1 2.2 %copy-done.1 = bf16[2,512,2048]{2,1,0:T(8,128)(2,1)S(1)} copy-done((bf16[2,512,2048]{2,1,0:T(8,128)(2,1)S(1)}, bf16[2,512,2048]{2,1,0:T(8,128)(2,1)}, u32[]{:S(2)}) %copy-start.1) | copy-done | bytes 4194328
  11.3 2.2 %copy-done.5 = bf16[2,2048,512]{2,1,0:T(8,128)(2,1)S(1)} copy-done((bf16[2,2048,512]{2,1,0:T(8,128)(2,1)S(1)}, bf16[2,2048,512]{2,1,0:T(8,128)(2,1)}, u32[]{:S(2)}) %copy-start.5) | copy-done | bytes 4194328
  13.5 2.3 %coarse.1.own_ref.whole_ref = bf16[512,512]{1,0:T(8,128)(2,1)S(1)} custom-call(s32[1]{0:T(128)} %bitcast.position_ref, bf16[2,512,2048]{2,1,0:T(8,128)(2,1)S(1)} %copy-done.1, bf16[2,2048,512]{2,1,0:T(8,128)(2,1)S(1)} %copy-done.5), custom_call_target="tpu_custom_call" | custom-call | flops 2147483648 | bytes 2097152 | tf_op jit(solution)/shard_map/coarse/pallas_call | solution.py:45
  18.6 2.0 %collective-permute-start.9 = (bf16[512,512]{1,0:T(8,128)(2,1)S(1)}, bf16[512,512]{1,0:T(8,128)(2,1)S(1)}, u32[]{:S(2)}, u32[]{:S(2)}) collective-permute-start(bf16[512,512]{1,0:T(8,128)(2,1)S(1)} %get-tuple-element.30.whole_ref), channel_id=1, source_target_pairs={{0,8},{4,12},{8,0},{12,4},{16,24},{20,28},{24,16},{28,20},{1,9},{5... | collective-permute-start | bytes 1572872 | tf_op jit(solution)/shard_map/ppermute | solution.py:24
  20.6 2.7 %collective-permute-done.4.arrived_ref = bf16[128,512]{1,0:T(8,128)(2,1)S(1)} collective-permute-done((bf16[128,512]{1,0:T(8,128)(2,1)S(1)}, bf16[128,512]{1,0:T(8,128)(2,1)S(1)}, u32[]{:S(2)}, u32[]{:S(2)}) %collective-permute-start.4) | collective-permute-done | bytes 131104 | tf_op jit(solution)/shard_map/ppermute | solution.py:29
  24.9 11.3 %collective-permute-done.5.arrived_ref = bf16[128,512]{1,0:T(8,128)(2,1)S(1)} collective-permute-done((bf16[128,512]{1,0:T(8,128)(2,1)S(1)}, bf16[128,512]{1,0:T(8,128)(2,1)S(1)}, u32[]{:S(2)}, u32[]{:S(2)}) %collective-permute-start.5) | collective-permute-done | bytes 131104 | tf_op jit(solution)/shard_map/ppermute | solution.py:29
  41.0 4.3 %collective-permute-done.8.other_ref = bf16[128,512]{1,0:T(8,128)(2,1)S(1)} collective-permute-done((bf16[128,512]{1,0:T(8,128)(2,1)S(1)}, bf16[128,512]{1,0:T(8,128)(2,1)S(1)}, u32[]{:S(2)}, u32[]{:S(2)}) %collective-permute-start.8) | collective-permute-done | bytes 131104 | tf_op jit(solution)/shard_map/ppermute | solution.py:24
  46.9 3.7 %collective-permute-done.10.other_ref = bf16[128,512]{1,0:T(8,128)(2,1)S(1)} collective-permute-done((bf16[128,512]{1,0:T(8,128)(2,1)S(1)}, bf16[128,512]{1,0:T(8,128)(2,1)S(1)}, u32[]{:S(2)}, u32[]{:S(2)}) %collective-permute-start.10) | collective-permute-done | bytes 131104 | tf_op jit(solution)/shard_map/ppermute | solution.py:24
  50.6 1.8 %states.1 = (bf16[128,512]{1,0:T(8,128)(2,1)S(1)}, f32[2,128,2048]{2,1,0:T(8,128)S(1)}, f32[2,128,512]{2,1,0:T(8,128)S(1)}, f32[2,128,1]{2,1,0:T(8,128)S(1)}) custom-call(s32[1]{0:T(128)} %bitcast.position_ref, bf16[128,512]{1,0:T(8,128)(2,1)S(1)} %get-tuple-element.35.value_ref, bf16[128,512]{1,0:T(8,128)(2,1)S(1)} %collective-permute-done.10.other_ref, ...), custom_call_target="tpu_custom_call" | custom-call | flops 1073741824 | bytes 2392064 | tf_op jit(solution)/shard_map/states/pallas_call | solution.py:45
  52.5 3.1 %adjoint_0.1 = bf16[128,512]{1,0:T(8,128)(2,1)S(1)} custom-call(s32[1]{0:T(128)} %bitcast.position_ref, bf16[128,512]{1,0:T(8,128)(2,1)S(1)} %copy-done.11, bf16[128,512]{1,0:T(8,128)(2,1)S(1)} %copy-done.11, f32[2,128,2048]{2,1,0:T(8,128)S(1)} %get-tuple-element.38.slope_ref, f32[2,128,512]{2,1,0:T(8,128)S(1)} %get-tuple-element.39.unit_ref, ...), custom_call_target="tpu_custom_call" | custom-call | flops 1073741824 | bytes 2818304 | tf_op jit(solution)/shard_map/adjoint_0/pallas_call | solution.py:45
  55.8 2.5 %collective-permute-done.11.arrived_ref = bf16[128,512]{1,0:T(8,128)(2,1)S(1)} collective-permute-done((bf16[128,512]{1,0:T(8,128)(2,1)S(1)}, bf16[128,512]{1,0:T(8,128)(2,1)S(1)}, u32[]{:S(2)}, u32[]{:S(2)}) %collective-permute-start.11) | collective-permute-done | bytes 131104 | tf_op jit(solution)/shard_map/ppermute | solution.py:29
  58.3 3.1 %adjoint_1.1 = bf16[128,512]{1,0:T(8,128)(2,1)S(1)} custom-call(s32[1]{0:T(128)} %bitcast.position_ref, bf16[128,512]{1,0:T(8,128)(2,1)S(1)} %copy-done.11, bf16[128,512]{1,0:T(8,128)(2,1)S(1)} %collective-permute-done.11.arrived_ref, f32[2,128,2048]{2,1,0:T(8,128)S(1)} %get-tuple-element.38.slope_ref, f32[2,128,512]{2,1,0:T(8,128)S(1)} %get-tuple-element.39.unit_ref, ...), custom_call_target="tpu_custom_call" | custom-call | flops 1073741824 | bytes 2818304 | tf_op jit(solution)/shard_map/adjoint_1/pallas_call | solution.py:45
  61.4 2.8 %collective-permute-start.12 = (bf16[128,512]{1,0:T(8,128)(2,1)S(1)}, bf16[128,512]{1,0:T(8,128)(2,1)S(1)}, u32[]{:S(2)}, u32[]{:S(2)}) collective-permute-start(bf16[128,512]{1,0:T(8,128)(2,1)S(1)} %adjoint_1.1), channel_id=1, source_target_pairs={{0,28},{4,0},{8,4},{12,8},{16,12},{20,16},{24,20},{28,24},{1,29},{... | collective-permute-start | bytes 393224 | tf_op jit(solution)/shard_map/ppermute | solution.py:29
  64.2 2.5 %collective-permute-done.12.arrived_ref = bf16[128,512]{1,0:T(8,128)(2,1)S(1)} collective-permute-done((bf16[128,512]{1,0:T(8,128)(2,1)S(1)}, bf16[128,512]{1,0:T(8,128)(2,1)S(1)}, u32[]{:S(2)}, u32[]{:S(2)}) %collective-permute-start.12) | collective-permute-done | bytes 131104 | tf_op jit(solution)/shard_map/ppermute | solution.py:29
  66.7 3.1 %adjoint_value.1.value_ref = bf16[128,512]{1,0:T(8,128)(2,1)S(1)} custom-call(s32[1]{0:T(128)} %bitcast.position_ref, bf16[128,512]{1,0:T(8,128)(2,1)S(1)} %copy-done.11, bf16[128,512]{1,0:T(8,128)(2,1)S(1)} %collective-permute-done.12.arrived_ref, bf16[512,512]{1,0:T(8,128)(2,1)S(1)} %coarse.1.own_ref.whole_ref, ...), custom_call_target="tpu_custom_call" | custom-call | flops 1073741824 | bytes 2949376 | tf_op jit(solution)/shard_map/adjoint_value/pallas_call | solution.py:45
  71.6 2.7 %collective-permute-start.14 = (bf16[128,512]{1,0:T(8,128)(2,1)S(1)}, bf16[128,512]{1,0:T(8,128)(2,1)S(1)}, u32[]{:S(2)}, u32[]{:S(2)}) collective-permute-start(bf16[128,512]{1,0:T(8,128)(2,1)S(1)} %get-tuple-element.42.value_ref), channel_id=1, source_target_pairs={{0,8},{4,12},{8,0},{12,4},{16,24},{20,28},{24,16},{28,20},{1,9},{5... | collective-permute-start | bytes 393224 | tf_op jit(solution)/shard_map/ppermute | solution.py:24
  74.3 3.6 %collective-permute-start.21 = (bf16[128,512]{1,0:T(8,128)(2,1)S(1)}, bf16[128,512]{1,0:T(8,128)(2,1)S(1)}, u32[]{:S(2)}, u32[]{:S(2)}) collective-permute-start(bf16[128,512]{1,0:T(8,128)(2,1)S(1)} %get-tuple-element.48.refs_0_), channel_id=1, source_target_pairs={{0,3},{1,0},{2,1},{3,2},{4,7},{5,4},{6,5},{7,6},{8,11},{9,8},{10,9... | collective-permute-start | bytes 393224 | tf_op jit(solution)/shard_map/ppermute | solution.py:29
  82.5 7.0 %collective-permute-done.20.refs_2_ = bf16[128,512]{1,0:T(8,128)(2,1)S(1)} collective-permute-done((bf16[128,512]{1,0:T(8,128)(2,1)S(1)}, bf16[128,512]{1,0:T(8,128)(2,1)S(1)}, u32[]{:S(2)}, u32[]{:S(2)}) %collective-permute-start.20) | collective-permute-done | bytes 131104 | tf_op jit(solution)/shard_map/ppermute | solution.py:29
  90.8 2.2 %copy-done.3 = bf16[2,512,2048]{2,1,0:T(8,128)(2,1)S(1)} copy-done((bf16[2,512,2048]{2,1,0:T(8,128)(2,1)S(1)}, bf16[2,512,2048]{2,1,0:T(8,128)(2,1)}, u32[]{:S(2)}) %copy-start.3) | copy-done | bytes 4194328
  93.0 2.2 %copy-done.6 = bf16[2,2048,512]{2,1,0:T(8,128)(2,1)S(1)} copy-done((bf16[2,2048,512]{2,1,0:T(8,128)(2,1)S(1)}, bf16[2,2048,512]{2,1,0:T(8,128)(2,1)}, u32[]{:S(2)}) %copy-start.6) | copy-done | bytes 4194328
  98.8 5.3 %recompute_0.1 = (f32[2,512,2048]{2,1,0:T(8,128)S(1)}, f32[2,512,512]{2,1,0:T(8,128)S(1)}, f32[2,512,1]{2,1,0:T(8,128)S(1)}, bf16[2,512,512]{2,1,0:T(8,128)(2,1)S(1)}, bf16[2,512,2048]{2,1,0:T(8,128)(2,1)S(1)}) custom-call(s32[1]{0:T(128)} %bitcast.position_ref, bf16[128,512]{1,0:T(8,128)(2,1)S(1)} %copy-done.20, bf16[128,512]{1,0:T(8,128)(2,1)S(1)} %copy-done.26, ...), custom_call_target="tpu_custom_call" | custom-call | flops 4294967296 | bytes 2228224 | tf_op jit(solution)/shard_map/recompute_0/pallas_call | solution.py:45
  104.1 3.3 %copy-done.8 = f32[2,512,2048]{2,1,0:T(8,128)} copy-done((f32[2,512,2048]{2,1,0:T(8,128)}, f32[2,512,2048]{2,1,0:T(8,128)S(1)}, u32[]{:S(2)}) %copy-start.8) | copy-done | bytes 8388632
  107.4 1.9 %copy-done.10 = bf16[2,512,2048]{2,1,0:T(8,128)(2,1)} copy-done((bf16[2,512,2048]{2,1,0:T(8,128)(2,1)}, bf16[2,512,2048]{2,1,0:T(8,128)(2,1)S(1)}, u32[]{:S(2)}) %copy-start.10) | copy-done | bytes 4194328
  111.1 2.3 %copy.7 = bf16[2,512,512]{1,2,0:T(8,128)(2,1)} copy(bf16[2,512,512]{2,1,0:T(8,128)(2,1)} %copy-done.12) | data formatting | bytes 2097152 | tf_op jit(solution)/shard_map/recompute_0/pallas_call | solution.py:45
  113.4 6.3 %copy.8 = bf16[2,512,2048]{1,2,0:T(8,128)(2,1)} copy(bf16[2,512,2048]{2,1,0:T(8,128)(2,1)} %copy-done.10) | data formatting | bytes 8388608 | tf_op jit(solution)/shard_map/recompute_0/pallas_call | solution.py:45
  125.9 1.9 %collective-permute-start.16 = (bf16[128,512]{1,0:T(8,128)(2,1)S(1)}, bf16[128,512]{1,0:T(8,128)(2,1)S(1)}, u32[]{:S(2)}, u32[]{:S(2)}) collective-permute-start(bf16[128,512]{1,0:T(8,128)(2,1)S(1)} %scan_end.1.refs_0_), channel_id=1, source_target_pairs={{0,1},{1,2},{2,3},{3,0},{4,5},{5,6},{6,7},{7,4},{8,9},{9,10},{10,1... | collective-permute-start | bytes 393224 | tf_op jit(solution)/shard_map/ppermute | solution.py:29
  129.7 7.6 %collective-permute-done.17.refs_2_ = bf16[128,512]{1,0:T(8,128)(2,1)S(1)} collective-permute-done((bf16[128,512]{1,0:T(8,128)(2,1)S(1)}, bf16[128,512]{1,0:T(8,128)(2,1)S(1)}, u32[]{:S(2)}, u32[]{:S(2)}) %collective-permute-start.17) | collective-permute-done | bytes 131104 | tf_op jit(solution)/shard_map/ppermute | solution.py:29
  137.3 2.2 %copy-done.4 = bf16[2,512,2048]{2,1,0:T(8,128)(2,1)S(1)} copy-done((bf16[2,512,2048]{2,1,0:T(8,128)(2,1)S(1)}, bf16[2,512,2048]{2,1,0:T(8,128)(2,1)}, u32[]{:S(2)}) %copy-start.4) | copy-done | bytes 4194328
  139.5 2.2 %copy-done.7 = bf16[2,2048,512]{2,1,0:T(8,128)(2,1)S(1)} copy-done((bf16[2,2048,512]{2,1,0:T(8,128)(2,1)S(1)}, bf16[2,2048,512]{2,1,0:T(8,128)(2,1)}, u32[]{:S(2)}) %copy-start.7) | copy-done | bytes 4194328
  141.7 3.4 %copy-done.9 = f32[2,512,2048]{2,1,0:T(8,128)S(1)} copy-done((f32[2,512,2048]{2,1,0:T(8,128)S(1)}, f32[2,512,2048]{2,1,0:T(8,128)}, u32[]{:S(2)}) %copy-start.9) | copy-done | bytes 8388632
  145.0 6.7 %grads_0.1 = (f32[2,128,2048]{2,1,0:T(8,128)}, f32[2,512,512]{2,1,0:T(8,128)}) custom-call(s32[1]{0:T(128)} %bitcast.position_ref, bf16[128,512]{1,0:T(8,128)(2,1)S(1)} %scan_end.1.refs_0_, bf16[128,512]{1,0:T(8,128)(2,1)S(1)} %collective-permute-done.16.refs_1_, bf16[128,512]{1,0:T(8,128)(2,1)S(1)} %collective-permute-done.17.refs_2_, ...), custom_call_target="tpu_custom_call" | custom-call | flops 4294967296 | bytes 5178368 | tf_op jit(solution)/shard_map/grads_0/pallas_call | solution.py:45
  (93 shorter events, 36.8 us)
Async XLA Ops:
  2.9 1.5 %collective-permute-start = (bf16[128,512]{1,0:T(8,128)(2,1)S(1)}, bf16[128,512]{1,0:T(8,128)(2,1)S(1)}, u32[]{:S(2)}, u32[]{:S(2)}) collective-permute-start(bf16[128,512]{1,0:T(8,128)(2,1)S(1)} %select_select_fusion), channel_id=1, source_target_pairs={{0,4},{4,0},{8,12},{12,8},{16,20},{20,16},{24,28},{28,24},{1,5},{5... | collective-permute-start | bytes 393224 | tf_op jit(solution)/shard_map/ppermute | solution.py:24
  4.6 11.3 %collective-permute-start.3 = (bf16[128,512]{1,0:T(8,128)(2,1)S(1)}, bf16[128,512]{1,0:T(8,128)(2,1)S(1)}, u32[]{:S(2)}, u32[]{:S(2)}) collective-permute-start(bf16[128,512]{1,0:T(8,128)(2,1)S(1)} %fusion), channel_id=1, source_target_pairs={{0,24},{4,28},{8,16},{12,20},{16,8},{20,12},{24,0},{28,4},{1,25},{... | collective-permute-start | bytes 393224 | tf_op jit(solution)/shard_map/ppermute | solution.py:24
  8.4 7.4 %collective-permute-start.2 = (bf16[128,512]{1,0:T(8,128)(2,1)S(1)}, bf16[128,512]{1,0:T(8,128)(2,1)S(1)}, u32[]{:S(2)}, u32[]{:S(2)}) collective-permute-start(bf16[128,512]{1,0:T(8,128)(2,1)S(1)} %fusion), channel_id=1, source_target_pairs={{0,16},{4,20},{8,24},{12,28},{16,0},{20,4},{24,8},{28,12},{1,17},{... | collective-permute-start | bytes 393224 | tf_op jit(solution)/shard_map/ppermute | solution.py:24
  8.9 6.9 %collective-permute-start.1 = (bf16[128,512]{1,0:T(8,128)(2,1)S(1)}, bf16[128,512]{1,0:T(8,128)(2,1)S(1)}, u32[]{:S(2)}, u32[]{:S(2)}) collective-permute-start(bf16[128,512]{1,0:T(8,128)(2,1)S(1)} %fusion), channel_id=1, source_target_pairs={{0,8},{4,12},{8,0},{12,4},{16,24},{20,28},{24,16},{28,20},{1,9},{5... | collective-permute-start | bytes 393224 | tf_op jit(solution)/shard_map/ppermute | solution.py:24
  9.1 2.2 %copy-start.1 = (bf16[2,512,2048]{2,1,0:T(8,128)(2,1)S(1)}, bf16[2,512,2048]{2,1,0:T(8,128)(2,1)}, u32[]{:S(2)}) copy-start(bf16[2,512,2048]{2,1,0:T(8,128)(2,1)} %refs_9_.1) | copy-start | bytes 12582916
  11.3 2.2 %copy-start.5 = (bf16[2,2048,512]{2,1,0:T(8,128)(2,1)S(1)}, bf16[2,2048,512]{2,1,0:T(8,128)(2,1)}, u32[]{:S(2)}) copy-start(bf16[2,2048,512]{2,1,0:T(8,128)(2,1)} %refs_10_.1) | copy-start | bytes 12582916
  13.5 2.5 %copy-start.2 = (bf16[2,512,2048]{2,1,0:T(8,128)(2,1)S(1)}, bf16[2,512,2048]{2,1,0:T(8,128)(2,1)}, u32[]{:S(2)}) copy-start(bf16[2,512,2048]{2,1,0:T(8,128)(2,1)} %refs_9_.1) | copy-start | bytes 12582916
  15.8 2.3 %collective-permute-start.7 = (bf16[512,512]{1,0:T(8,128)(2,1)S(1)}, bf16[512,512]{1,0:T(8,128)(2,1)S(1)}, u32[]{:S(2)}, u32[]{:S(2)}) collective-permute-start(bf16[512,512]{1,0:T(8,128)(2,1)S(1)} %coarse.1.own_ref.whole_ref), channel_id=1, source_target_pairs={{0,4},{4,0},{8,12},{12,8},{16,20},{20,16},{24,28},{28,24},{1,5},{5... | collective-permute-start | bytes 1572872 | tf_op jit(solution)/shard_map/ppermute | solution.py:24
  17.6 5.6 %collective-permute-start.4 = (bf16[128,512]{1,0:T(8,128)(2,1)S(1)}, bf16[128,512]{1,0:T(8,128)(2,1)S(1)}, u32[]{:S(2)}, u32[]{:S(2)}) collective-permute-start(bf16[128,512]{1,0:T(8,128)(2,1)S(1)} %forward_0.1), channel_id=1, source_target_pairs={{0,4},{4,8},{8,12},{12,16},{16,20},{20,24},{24,28},{28,0},{1,5},{5... | collective-permute-start | bytes 393224 | tf_op jit(solution)/shard_map/ppermute | solution.py:29
  18.6 21.6 %collective-permute-start.9 = (bf16[512,512]{1,0:T(8,128)(2,1)S(1)}, bf16[512,512]{1,0:T(8,128)(2,1)S(1)}, u32[]{:S(2)}, u32[]{:S(2)}) collective-permute-start(bf16[512,512]{1,0:T(8,128)(2,1)S(1)} %get-tuple-element.30.whole_ref), channel_id=1, source_target_pairs={{0,8},{4,12},{8,0},{12,4},{16,24},{20,28},{24,16},{28,20},{1,9},{5... | collective-permute-start | bytes 1572872 | tf_op jit(solution)/shard_map/ppermute | solution.py:24
  24.9 11.4 %collective-permute-start.5 = (bf16[128,512]{1,0:T(8,128)(2,1)S(1)}, bf16[128,512]{1,0:T(8,128)(2,1)S(1)}, u32[]{:S(2)}, u32[]{:S(2)}) collective-permute-start(bf16[128,512]{1,0:T(8,128)(2,1)S(1)} %forward_1.1), channel_id=1, source_target_pairs={{0,4},{4,8},{8,12},{12,16},{16,20},{20,24},{24,28},{28,0},{1,5},{5... | collective-permute-start | bytes 393224 | tf_op jit(solution)/shard_map/ppermute | solution.py:29
  38.0 1.4 collective-permute-start.6
  39.6 5.6 %collective-permute-start.8 = (bf16[128,512]{1,0:T(8,128)(2,1)S(1)}, bf16[128,512]{1,0:T(8,128)(2,1)S(1)}, u32[]{:S(2)}, u32[]{:S(2)}) collective-permute-start(bf16[128,512]{1,0:T(8,128)(2,1)S(1)} %get-tuple-element.29.value_ref), channel_id=1, source_target_pairs={{0,8},{4,12},{8,0},{12,4},{16,24},{20,28},{24,16},{28,20},{1,9},{5... | collective-permute-start | bytes 393224 | tf_op jit(solution)/shard_map/ppermute | solution.py:24
  41.0 9.6 %copy-start.13 = (bf16[512,512]{1,0:T(8,128)(2,1)}, bf16[512,512]{1,0:T(8,128)(2,1)S(1)}, u32[]{:S(2)}) copy-start(bf16[512,512]{1,0:T(8,128)(2,1)S(1)} %get-tuple-element.47.part_ref) | copy-start | bytes 1572868
  45.6 5.0 %collective-permute-start.10 = (bf16[128,512]{1,0:T(8,128)(2,1)S(1)}, bf16[128,512]{1,0:T(8,128)(2,1)S(1)}, u32[]{:S(2)}, u32[]{:S(2)}) collective-permute-start(bf16[128,512]{1,0:T(8,128)(2,1)S(1)} %get-tuple-element.35.value_ref), channel_id=1, source_target_pairs={{0,16},{4,20},{8,24},{12,28},{16,0},{20,4},{24,8},{28,12},{1,17},{... | collective-permute-start | bytes 393224 | tf_op jit(solution)/shard_map/ppermute | solution.py:24
  52.4 25.4 %copy-start.19 = (bf16[128,512]{1,0:T(8,128)(2,1)}, bf16[128,512]{1,0:T(8,128)(2,1)S(1)}, u32[]{:S(2)}) copy-start(bf16[128,512]{1,0:T(8,128)(2,1)S(1)} %get-tuple-element.48.refs_0_) | copy-start | bytes 393220
  55.5 2.8 %collective-permute-start.11 = (bf16[128,512]{1,0:T(8,128)(2,1)S(1)}, bf16[128,512]{1,0:T(8,128)(2,1)S(1)}, u32[]{:S(2)}, u32[]{:S(2)}) collective-permute-start(bf16[128,512]{1,0:T(8,128)(2,1)S(1)} %adjoint_0.1), channel_id=1, source_target_pairs={{0,28},{4,0},{8,4},{12,8},{16,12},{20,16},{24,20},{28,24},{1,29},{... | collective-permute-start | bytes 393224 | tf_op jit(solution)/shard_map/ppermute | solution.py:29
  61.4 5.3 %collective-permute-start.12 = (bf16[128,512]{1,0:T(8,128)(2,1)S(1)}, bf16[128,512]{1,0:T(8,128)(2,1)S(1)}, u32[]{:S(2)}, u32[]{:S(2)}) collective-permute-start(bf16[128,512]{1,0:T(8,128)(2,1)S(1)} %adjoint_1.1), channel_id=1, source_target_pairs={{0,28},{4,0},{8,4},{12,8},{16,12},{20,16},{24,20},{28,24},{1,29},{... | collective-permute-start | bytes 393224 | tf_op jit(solution)/shard_map/ppermute | solution.py:29
  69.9 1.4 collective-permute-start.13
  71.6 7.3 %collective-permute-start.14 = (bf16[128,512]{1,0:T(8,128)(2,1)S(1)}, bf16[128,512]{1,0:T(8,128)(2,1)S(1)}, u32[]{:S(2)}, u32[]{:S(2)}) collective-permute-start(bf16[128,512]{1,0:T(8,128)(2,1)S(1)} %get-tuple-element.42.value_ref), channel_id=1, source_target_pairs={{0,8},{4,12},{8,0},{12,4},{16,24},{20,28},{24,16},{28,20},{1,9},{5... | collective-permute-start | bytes 393224 | tf_op jit(solution)/shard_map/ppermute | solution.py:24
  74.3 7.5 %collective-permute-start.21 = (bf16[128,512]{1,0:T(8,128)(2,1)S(1)}, bf16[128,512]{1,0:T(8,128)(2,1)S(1)}, u32[]{:S(2)}, u32[]{:S(2)}) collective-permute-start(bf16[128,512]{1,0:T(8,128)(2,1)S(1)} %get-tuple-element.48.refs_0_), channel_id=1, source_target_pairs={{0,3},{1,0},{2,1},{3,2},{4,7},{5,4},{6,5},{7,6},{8,11},{9,8},{10,9... | collective-permute-start | bytes 393224 | tf_op jit(solution)/shard_map/ppermute | solution.py:29
  77.9 11.6 %collective-permute-start.20 = (bf16[128,512]{1,0:T(8,128)(2,1)S(1)}, bf16[128,512]{1,0:T(8,128)(2,1)S(1)}, u32[]{:S(2)}, u32[]{:S(2)}) collective-permute-start(bf16[128,512]{1,0:T(8,128)(2,1)S(1)} %get-tuple-element.48.refs_0_), channel_id=1, source_target_pairs={{0,2},{1,3},{2,0},{3,1},{4,6},{5,7},{6,4},{7,5},{8,10},{9,11},{10,... | collective-permute-start | bytes 393224 | tf_op jit(solution)/shard_map/ppermute | solution.py:29
  77.9 12.2 %collective-permute-start.19 = (bf16[128,512]{1,0:T(8,128)(2,1)S(1)}, bf16[128,512]{1,0:T(8,128)(2,1)S(1)}, u32[]{:S(2)}, u32[]{:S(2)}) collective-permute-start(bf16[128,512]{1,0:T(8,128)(2,1)S(1)} %get-tuple-element.48.refs_0_), channel_id=1, source_target_pairs={{0,1},{1,2},{2,3},{3,0},{4,5},{5,6},{6,7},{7,4},{8,9},{9,10},{10,1... | collective-permute-start | bytes 393224 | tf_op jit(solution)/shard_map/ppermute | solution.py:29
  80.7 39.9 %collective-permute-start.15 = (bf16[128,512]{1,0:T(8,128)(2,1)}, bf16[128,512]{1,0:T(8,128)(2,1)}, u32[]{:S(2)}, u32[]{:S(2)}) collective-permute-start(bf16[128,512]{1,0:T(8,128)(2,1)} %get-tuple-element.45.value_ref), channel_id=1, source_target_pairs={{0,16},{4,20},{8,24},{12,28},{16,0},{20,4},{24,8},{28,12},{1,17},{... | collective-permute-start | bytes 393224 | tf_op jit(solution)/shard_map/ppermute | solution.py:24
  90.8 2.2 %copy-start.3 = (bf16[2,512,2048]{2,1,0:T(8,128)(2,1)S(1)}, bf16[2,512,2048]{2,1,0:T(8,128)(2,1)}, u32[]{:S(2)}) copy-start(bf16[2,512,2048]{2,1,0:T(8,128)(2,1)} %refs_9_.1) | copy-start | bytes 12582916
  104.1 3.3 %copy-start.8 = (f32[2,512,2048]{2,1,0:T(8,128)}, f32[2,512,2048]{2,1,0:T(8,128)S(1)}, u32[]{:S(2)}) copy-start(f32[2,512,2048]{2,1,0:T(8,128)S(1)} %get-tuple-element.49.refs_4_) | copy-start | bytes 25165828
  119.6 17.7 %copy-start.16 = (f32[2,512,1]{2,1,0:T(8,128)S(1)}, f32[2,512,1]{2,1,0:T(8,128)}, u32[]{:S(2)}) copy-start(f32[2,512,1]{2,1,0:T(8,128)} %copy-done.15) | copy-start | bytes 12292
  124.0 5.8 %collective-permute-start.18 = (bf16[128,512]{1,0:T(8,128)(2,1)S(1)}, bf16[128,512]{1,0:T(8,128)(2,1)S(1)}, u32[]{:S(2)}, u32[]{:S(2)}) collective-permute-start(bf16[128,512]{1,0:T(8,128)(2,1)S(1)} %scan_end.1.refs_0_), channel_id=1, source_target_pairs={{0,3},{1,0},{2,1},{3,2},{4,7},{5,4},{6,5},{7,6},{8,11},{9,8},{10,9... | collective-permute-start | bytes 393224 | tf_op jit(solution)/shard_map/ppermute | solution.py:29
  125.4 11.8 %collective-permute-start.17 = (bf16[128,512]{1,0:T(8,128)(2,1)S(1)}, bf16[128,512]{1,0:T(8,128)(2,1)S(1)}, u32[]{:S(2)}, u32[]{:S(2)}) collective-permute-start(bf16[128,512]{1,0:T(8,128)(2,1)S(1)} %scan_end.1.refs_0_), channel_id=1, source_target_pairs={{0,2},{1,3},{2,0},{3,1},{4,6},{5,7},{6,4},{7,5},{8,10},{9,11},{10,... | collective-permute-start | bytes 393224 | tf_op jit(solution)/shard_map/ppermute | solution.py:29
  125.9 11.3 %collective-permute-start.16 = (bf16[128,512]{1,0:T(8,128)(2,1)S(1)}, bf16[128,512]{1,0:T(8,128)(2,1)S(1)}, u32[]{:S(2)}, u32[]{:S(2)}) collective-permute-start(bf16[128,512]{1,0:T(8,128)(2,1)S(1)} %scan_end.1.refs_0_), channel_id=1, source_target_pairs={{0,1},{1,2},{2,3},{3,0},{4,5},{5,6},{6,7},{7,4},{8,9},{9,10},{10,1... | collective-permute-start | bytes 393224 | tf_op jit(solution)/shard_map/ppermute | solution.py:29
  137.3 2.2 %copy-start.4 = (bf16[2,512,2048]{2,1,0:T(8,128)(2,1)S(1)}, bf16[2,512,2048]{2,1,0:T(8,128)(2,1)}, u32[]{:S(2)}) copy-start(bf16[2,512,2048]{2,1,0:T(8,128)(2,1)} %refs_9_.1) | copy-start | bytes 12582916
  141.7 3.4 %copy-start.9 = (f32[2,512,2048]{2,1,0:T(8,128)S(1)}, f32[2,512,2048]{2,1,0:T(8,128)}, u32[]{:S(2)}) copy-start(f32[2,512,2048]{2,1,0:T(8,128)} %copy-done.8) | copy-start | bytes 25165828
  (17 other events, 19.5 us)

commit v3 on v2

--- a/solution.py
+++ b/solution.py
@@ -7,6 +7,7 @@
 from jax.experimental.pallas import tpu as pltpu
 from jax.sharding import PartitionSpec as P
 
+
 RELAX = 3
 
 
@@ -39,7 +40,7 @@
     )
 
 
-def call(body, name, flops, limit, out_shapes, position, *args):
+def call(body, flops, limit, out_shapes, position, *args):
     whole = pl.BlockSpec(memory_space=pltpu.VMEM)
     moved = sum(a.size * a.dtype.itemsize for a in args)
     return pl.pallas_call(
@@ -47,7 +48,6 @@
         out_shape=out_shapes,
         in_specs=[pl.BlockSpec(memory_space=pltpu.SMEM)] + [whole] * len(args),
         out_specs=jax.tree.map(lambda unused: whole, out_shapes),
-        name=name,
         compiler_params=pltpu.CompilerParams(vmem_limit_bytes=limit * MIB),
         cost_estimate=pl.CostEstimate(flops=flops, bytes_accessed=moved // 4, transcendentals=0),
     )(position, *args)
@@ -81,7 +81,7 @@
     return adjoint
 
 
-def save_forward(state, up_ref, down_ref, slope_ref, unit_ref, scale_ref, normed_ref, hidden_ref):
+def save_forward(state, up_ref, down_ref, slope_ref, unit_ref, scale_ref, keep=None):
     layers = up_ref.shape[0]
     for layer in range(layers):
         scale = row_scale(state)
@@ -92,14 +92,19 @@
         slope_ref[layer] = sigma * (1.0 + before * (1.0 - sigma))
         unit_ref[layer] = unit
         scale_ref[layer] = scale
-        if normed_ref is not None:
-            normed_ref[layer] = normed
-        if hidden_ref is not None or layer < layers - 1:
+        if keep is not None or layer < layers - 1:
             hidden = (before * sigma).astype(LOW)
-            if hidden_ref is not None:
-                hidden_ref[layer] = hidden
+            if keep is not None:
+                keep(layer, normed, hidden)
             if layer < layers - 1:
                 state = state + dot(hidden, down_ref[layer])
+
+
+def own_columns(values, part, count):
+    dims = (count, values.shape[1])
+    columns = lax.broadcasted_iota(jnp.int32, dims, 1)
+    chosen = lax.broadcasted_iota(jnp.int32, dims, 0) + part * count
+    return dot_transposed((columns == chosen).astype(LOW), values).astype(LOW)
 
 
 def coarse_kernel(position_ref, up_ref, down_ref, out_ref):
@@ -113,12 +118,19 @@
     return left.astype(FULL) + right.astype(FULL) + dot(left, right)
 
 
-def join_kernel(bit, last, position_ref, whole_ref, other_ref, *refs):
+def join_kernel(bit, last, position_ref, whole_ref, *refs):
     upper = ((position_ref[0] >> bit) & 1) == 1
-    whole, other = whole_ref[...], other_ref[...]
+    odd = (position_ref[0] & 1) == 1
+    refs = list(refs)
+    whole = whole_ref[...]
+    half = whole.shape[0] // 2
+    if bit > 0:
+        near, far = refs.pop(0)[...], refs.pop(0)[...]
+        other = jnp.concatenate([jnp.where(odd, far, near), jnp.where(odd, near, far)], axis=0)
+    else:
+        other = refs.pop(0)[...]
     low = jnp.where(upper, other, whole)
     high = jnp.where(upper, whole, other)
-    refs = list(refs)
     zeros = jnp.zeros_like(low)
     if bit > 0:
         before, after = refs.pop(0)[...], refs.pop(0)[...]
@@ -132,30 +144,35 @@
     refs[2][...] = prefix
     refs[3][...] = suffix
     if not last:
-        refs[4][...] = joined(low, high).astype(LOW)
+        both = joined(low, high).astype(LOW)
+        refs[4][...] = both
+        refs[5][...] = jnp.where(odd, both[half:], both[:half])
 
 
 def matrix_scan(own, position, bits):
     width = own.shape[0]
     square = shape(own.shape, LOW)
-    whole, prefix, suffix = own, None, None
+    half = shape((width // 2, width), LOW)
+    whole, part, prefix, suffix = own, None, None, None
     steps = []
     for bit in range(bits - 1):
         last = bit == bits - 2
-        other = swapped(whole, "depth", 1 << bit)
-        args = (whole, other) if bit == 0 else (whole, other, prefix, suffix)
+        if bit == 0:
+            args = (whole, swapped(whole, "depth", 1))
+        else:
+            near = swapped(part, "depth", 1 << bit)
+            args = (whole, near, swapped(near, "depth", 1), prefix, suffix)
         outs = call(
             functools.partial(join_kernel, bit, last),
-            f"join_{bit}",
             6 * width**3,
             12,
-            [square] * (4 if last else 5),
+            [square] * 4 + ([] if last else [square, half]),
             position,
             *args,
         )
         steps.append((prefix, suffix, outs[0], outs[1]))
         prefix, suffix = outs[2], outs[3]
-        whole = None if last else outs[4]
+        whole, part = (None, None) if last else outs[4:]
     steps.append((prefix, suffix, None, None))
     return steps
 
@@ -185,18 +202,19 @@
 
 
 def scan_end(forward, bit, position_ref, value_ref, other_ref, total_ref, part_ref):
-    receives, donor, unused = scan_values(forward, bit, position_ref, value_ref, other_ref)
+    receives, donor, _ = scan_values(forward, bit, position_ref, value_ref, other_ref)
     times = dot if forward else dot_transposed
     more = donor + times(donor, part_ref[...])
     return total_ref[...] + jnp.where(receives, more, jnp.zeros_like(more))
 
 
-def shards(token_ids, embedding, w_up, w_down, cotangent):
+def block_pass(token_ids, embedding, w_up, w_down, cotangent):
     depth = lax.axis_size("depth")
     bits = depth.bit_length() - 1
     assert depth == 1 << bits and bits >= 2
     position = lax.axis_index("depth")
-    place = position.reshape(1).astype(jnp.int32)
+    parts = lax.axis_size("dp")
+    place = jnp.stack([position, lax.axis_index("dp")]).astype(jnp.int32)
     layers, width, inner_width = w_up.shape
     rows = token_ids.shape[0]
     layer_flops = 4 * rows * width * inner_width
@@ -206,14 +224,15 @@
     picked = jnp.take(embedding, jnp.clip(local_ids, 0, vocab_rows - 1), axis=0)
     picked = jnp.where(inside[:, None], picked, jnp.zeros_like(picked))
     picked = picked + swapped(picked, "depth", 1)
-    arrivals = [swapped(picked, "depth", mask) for mask in range(2, depth, 2)]
+    arrivals = []
+    for mask in range(2, depth, 2):
+        arrivals.append(swapped(picked, "depth", mask))
     for arrival in arrivals:
         picked = picked + arrival
     start = picked
 
     own = call(
         coarse_kernel,
-        "coarse",
         4 * width * width * inner_width,
         12,
         shape((width, width), LOW),
@@ -236,32 +255,13 @@
         out_ref[...] = jnp.where(position_ref[0] == 0, ended, change).astype(LOW)
 
     arrived = start
-    for sweep in range(RELAX - 1):
+    for _ in range(RELAX - 1):
         ended = call(
-            forward_kernel,
-            f"forward_{sweep}",
-            layers * layer_flops,
-            12,
-            state_low,
-            place,
-            start,
-            arrived,
-            w_up,
-            w_down,
+            forward_kernel, layers * layer_flops, 12, state_low, place, start, arrived, w_up, w_down
         )
         arrived = rotated(ended, "depth", 1)
     value = call(
-        value_kernel,
-        "forward_value",
-        layers * layer_flops,
-        12,
-        state_low,
-        place,
-        start,
-        arrived,
-        own,
-        w_up,
-        w_down,
+        value_kernel, layers * layer_flops, 12, state_low, place, start, arrived, own, w_up, w_down
     )
 
     def scanned(forward, value):
@@ -274,7 +274,6 @@
                 args = args + (total, prefix if forward else suffix)
             total, value = call(
                 functools.partial(scan_kernel, forward, bit),
-                f"scan_{int(forward)}_{bit}",
                 4 * rows * width * width,
                 8,
                 [state_full, state_low],
@@ -301,12 +300,11 @@
         corrected = jnp.where(position_ref[0] == 0, start_ref[...], corrected.astype(LOW))
         low_ref[...] = corrected
         save_forward(
-            corrected.astype(FULL), up_ref, down_ref, slope_ref, unit_ref, scale_ref, None, None
+            corrected.astype(FULL), up_ref, down_ref, slope_ref, unit_ref, scale_ref
         )
 
     corrected, slope, unit, scale = call(
         states_kernel,
-        "states",
         layers * layer_flops,
         12,
         [state_low] + saved_shapes(rows),
@@ -337,11 +335,11 @@
         change = begun - adjoint - dot_transposed(adjoint, own_ref[...])
         out_ref[...] = jnp.where(ends, begun, change).astype(LOW)
 
+    pieces = lambda block: [block] + [rotated(block, "dp", d) for d in range(1, parts)]
     arrived = cotangent
     for sweep in range(RELAX - 1):
         begun = call(
             adjoint_kernel,
-            f"adjoint_{sweep}",
             layers * layer_flops,
             12,
             state_low,
@@ -354,10 +352,13 @@
             w_up,
             w_down,
         )
+        if sweep == 0:
+            begun, corrected = lax.optimization_barrier((begun, corrected))
+            corrected_pieces = pieces(corrected)
         arrived = rotated(begun, "depth", -1)
+    arrived, corrected_pieces = lax.optimization_barrier((arrived, corrected_pieces))
     value = call(
         adjoint_value_kernel,
-        "adjoint_value",
         layers * layer_flops,
         12,
         state_low,
@@ -382,29 +383,21 @@
         out_ref[...] = jnp.where(ends, final_ref[...], adjoint.astype(LOW))
 
     adjoint = call(
-        end_kernel,
-        "scan_end",
-        2 * rows * width * width,
-        8,
-        state_low,
-        place,
-        *scanned(False, value),
-        cotangent,
-    )
-
-    parts = lax.axis_size("dp")
-    part = lax.axis_index("dp")
-    pieces = lambda block: [block] + [rotated(block, "dp", d) for d in range(1, parts)]
-    corrected_pieces = pieces(corrected)
+        end_kernel, 2 * rows * width * width, 8, state_low, place, *scanned(False, value), cotangent
+    )
+
+    corrected_pieces, adjoint = lax.optimization_barrier((corrected_pieces, adjoint))
     adjoint_pieces = pieces(adjoint)
-
-    def own_rows(block):
-        size = block.shape[2] // parts
-        return jnp.swapaxes(lax.dynamic_slice_in_dim(block, part * size, size, 2), 1, 2)
 
     def recompute_kernel(count, position_ref, *refs):
         state = jnp.concatenate([ref[...] for ref in refs[:count]], axis=0).astype(FULL)
-        save_forward(state, *refs[count:])
+        normed_ref, hidden_ref = refs[-2:]
+
+        def keep(layer, normed, hidden):
+            normed_ref[layer] = own_columns(normed, position_ref[1], width // parts)
+            hidden_ref[layer] = own_columns(hidden, position_ref[1], inner_width // parts)
+
+        save_forward(state, *refs[count:-2], keep)
 
     def grads_kernel(count, position_ref, *refs):
         adjoint = jnp.concatenate([ref[...] for ref in refs[:count]], axis=0).astype(FULL)
@@ -433,11 +426,13 @@
             inputs, grads = lax.optimization_barrier((inputs, grads))
         slope, unit, scale, normed, hidden = call(
             functools.partial(recompute_kernel, count),
-            f"recompute_{begin}",
             layers * layer_flops * count,
             24,
             saved_shapes(tokens)
-            + [shape((layers, tokens, width), LOW), shape((layers, tokens, inner_width), LOW)],
+            + [
+                shape((layers, width // parts, tokens), LOW),
+                shape((layers, inner_width // parts, tokens), LOW),
+            ],
             place,
             *inputs,
             w_up,
@@ -445,7 +440,6 @@
         )
         more = call(
             functools.partial(grads_kernel, count),
-            f"grads_{begin}",
             layers * layer_flops * count,
             24,
             [
@@ -457,8 +451,8 @@
             slope,
             unit,
             scale,
-            own_rows(normed),
-            own_rows(hidden),
+            normed,
+            hidden,
             w_up,
             w_down,
         )
@@ -475,4 +469,4 @@
         P("dp", None),
     )
     out_specs = (P("depth", "dp", None), P("depth", "dp", None))
-    return jax.shard_map(shards, mesh=mesh, in_specs=in_specs, out_specs=out_specs, check_vma=False)
+    return jax.shard_map(block_pass, mesh=mesh, in_specs=in_specs, out_specs=out_specs, check_vma=False)

time: 153 us -> 114 us (0.75)
  local copies, waits for them, and re-layouts: 44 us -> 5.78 us
  Pallas kernels: 35 us -> 45.4 us
  waiting for transfers between devices: 46.1 us -> 37.8 us
  starting transfers between devices: 24.8 us -> 23 us
    unnamed x54 -> x12, local copies, waits for them, and re-layouts: 32.3 us -> 4.93 us
    ppermute x10, waiting for transfers between devices: 34.4 us -> 11.6 us  [rotated(): lax.ppermute(block, axis, [(i, (i + distance) % size) for i in range(size)])]
    ppermute x12 -> x13, waiting for transfers between devices: 11.6 us -> 26.2 us  [swapped(): return lax.ppermute(block, axis, [(i, i ^ mask) for i in devices])]
    pallas_call x17, Pallas kernels: 35 us -> 45.4 us  [call(): pl.pallas_call(body, out_shape=out_shapes, in_specs=[pl.BlockSpec(memory_...]
    pallas_call x2 -> x0, local copies, waits for them, and re-layouts: 8.54 us -> none  [call(): pl.pallas_call(body, out_shape=out_shapes, in_specs=[pl.BlockSpec(memory_...]
    transpose x2 -> x0, local copies, waits for them, and re-layouts: 2.32 us -> none  [own_rows(): jnp.swapaxes(lax.dynamic_slice_in_dim(block, part * size, size, 2), 1, 2)]
    ppermute x10, starting transfers between devices: 12.2 us -> 10.3 us  [rotated(): lax.ppermute(block, axis, [(i, (i + distance) % size) for i in range(size)])]
    ppermute x12 -> x13, starting transfers between devices: 12.6 us -> 12.6 us  [swapped(): return lax.ppermute(block, axis, [(i, i ^ mask) for i in devices])]
  transfers between devices with their start and end apart: 22 -> 23, of which waited for: 13 -> 14; matrix products, arithmetic and copies ran while one was open for 7% -> 0% of each run, Pallas kernels for 10% -> 22%
where the time goes in v3:
time: 114 us
  Pallas kernels  45.4 us (40%)
  waiting for transfers between devices  37.8 us (33%)
  starting transfers between devices  23 us (20%)
  local copies, waits for them, and re-layouts  5.78 us (5%)
    pallas_call x17, Pallas kernels, call(): pl.pallas_call(body, out_shape=out_shapes, in_specs=[pl.BlockSpec(memory_...  45.4 us
    ppermute x13, waiting for transfers between devices, swapped(): return lax.ppermute(block, axis, [(i, i ^ mask) for i in devices])  26.2 us
    ppermute x13, starting transfers between devices, swapped(): return lax.ppermute(block, axis, [(i, i ^ mask) for i in devices])  12.6 us
    ppermute x10, waiting for transfers between devices, rotated(): lax.ppermute(block, axis, [(i, (i + distance) % size) for i in range(size)])  11.6 us
    ppermute x10, starting transfers between devices, rotated(): lax.ppermute(block, axis, [(i, (i + distance) % size) for i in range(size)])  10.3 us
    unnamed x12, local copies, waits for them, and re-layouts  4.93 us
  transfers between devices with their start and end apart: 23, of which 14 were waited for; matrix products, arithmetic and copies ran while one was open for 0% of the time, Pallas kernels for 22%

profile of v3, /device:TPU:0, one launch (start us, length us, event | category | flops | bytes accessed | tf_op | source)
XLA Modules:
  0.0 113.9 jit_solution(18225331326616201770)
XLA Ops:
  3.6 2.2 %copy-done.1 = bf16[2,512,2048]{2,1,0:T(8,128)(2,1)S(1)} copy-done((bf16[2,512,2048]{2,1,0:T(8,128)(2,1)S(1)}, bf16[2,512,2048]{2,1,0:T(8,128)(2,1)}, u32[]{:S(2)}) %copy-start.1) | copy-done | bytes 4194328
  5.8 2.2 %copy-done.3 = bf16[2,2048,512]{2,1,0:T(8,128)(2,1)S(1)} copy-done((bf16[2,2048,512]{2,1,0:T(8,128)(2,1)S(1)}, bf16[2,2048,512]{2,1,0:T(8,128)(2,1)}, u32[]{:S(2)}) %copy-start.3) | copy-done | bytes 4194328
  7.9 2.9 %shard_map.70.own_ref.whole_ref = bf16[512,512]{1,0:T(8,128)(2,1)S(1)} custom-call(s32[2]{0:T(128)S(1)} %pad_add_fusion.position_ref, bf16[2,512,2048]{2,1,0:T(8,128)(2,1)S(1)} %copy-done.1, bf16[2,2048,512]{2,1,0:T(8,128)(2,1)S(1)} %copy-done.3), custom_call_target="tpu_custom_call" | custom-call | flops 2147483648 | bytes 2097152 | tf_op jit(solution)/shard_map/pallas_call | solution.py:46
  11.0 4.0 %collective-permute-start.3 = (bf16[128,512]{1,0:T(8,128)(2,1)S(1)}, bf16[128,512]{1,0:T(8,128)(2,1)S(1)}, u32[]{:S(2)}, u32[]{:S(2)}) collective-permute-start(bf16[128,512]{1,0:T(8,128)(2,1)S(1)} %fusion), channel_id=1, source_target_pairs={{0,24},{4,28},{8,16},{12,20},{16,8},{20,12},{24,0},{28,4},{1,25},{... | collective-permute-start | bytes 393224 | tf_op jit(solution)/shard_map/ppermute | solution.py:25
  15.6 3.3 %collective-permute-done.3 = bf16[128,512]{1,0:T(8,128)(2,1)S(1)} collective-permute-done((bf16[128,512]{1,0:T(8,128)(2,1)S(1)}, bf16[128,512]{1,0:T(8,128)(2,1)S(1)}, u32[]{:S(2)}, u32[]{:S(2)}) %collective-permute-start.3) | collective-permute-done | bytes 131104 | tf_op jit(solution)/shard_map/ppermute | solution.py:25
  18.9 2.6 %collective-permute-done.2 = bf16[128,512]{1,0:T(8,128)(2,1)S(1)} collective-permute-done((bf16[128,512]{1,0:T(8,128)(2,1)S(1)}, bf16[128,512]{1,0:T(8,128)(2,1)S(1)}, u32[]{:S(2)}, u32[]{:S(2)}) %collective-permute-start.2) | collective-permute-done | bytes 131104 | tf_op jit(solution)/shard_map/ppermute | solution.py:25
  21.8 2.3 %shard_map.68 = bf16[128,512]{1,0:T(8,128)(2,1)S(1)} custom-call(s32[2]{0:T(128)S(1)} %pad_add_fusion.position_ref, bf16[128,512]{1,0:T(8,128)(2,1)S(1)} %add_add_fusion.start_ref.arrived_ref, bf16[128,512]{1,0:T(8,128)(2,1)S(1)} %add_add_fusion.start_ref.arrived_ref, bf16[2,512,2048]{2,1,0:T(8,128)(2,1)S(1)} %copy-done.2, bf16[2,2048,512]{2,1,0:T(8,128)(2,1)S(1)} %copy-done.3), custom_call_target="tpu_custom_call" | custom-call | flops 1073741824 | bytes 2162688 | tf_op jit(solution)/shard_map/pallas_call | solution.py:46
  25.2 1.6 %collective-permute-start.9 = (bf16[256,512]{1,0:T(8,128)(2,1)S(1)}, bf16[256,512]{1,0:T(8,128)(2,1)S(1)}, u32[]{:S(2)}, u32[]{:S(2)}) collective-permute-start(bf16[256,512]{1,0:T(8,128)(2,1)S(1)} %get-tuple-element.44), channel_id=1, source_target_pairs={{0,8},{4,12},{8,0},{12,4},{16,24},{20,28},{24,16},{28,20},{1,9},{5... | collective-permute-start | bytes 786440 | tf_op jit(solution)/shard_map/ppermute | solution.py:25
  26.8 2.6 %collective-permute-done.4.arrived_ref = bf16[128,512]{1,0:T(8,128)(2,1)S(1)} collective-permute-done((bf16[128,512]{1,0:T(8,128)(2,1)S(1)}, bf16[128,512]{1,0:T(8,128)(2,1)S(1)}, u32[]{:S(2)}, u32[]{:S(2)}) %collective-permute-start.4) | collective-permute-done | bytes 131104 | tf_op jit(solution)/shard_map/ppermute | solution.py:30
  29.4 2.3 %shard_map.69 = bf16[128,512]{1,0:T(8,128)(2,1)S(1)} custom-call(s32[2]{0:T(128)S(1)} %pad_add_fusion.position_ref, bf16[128,512]{1,0:T(8,128)(2,1)S(1)} %add_add_fusion.start_ref.arrived_ref, bf16[128,512]{1,0:T(8,128)(2,1)S(1)} %collective-permute-done.4.arrived_ref, bf16[2,512,2048]{2,1,0:T(8,128)(2,1)S(1)} %copy-done.2, bf16[2,2048,512]{2,1,0:T(8,128)(2,1)S(1)} %copy-done.3), custom_call_target="tpu_custom_call" | custom-call | flops 1073741824 | bytes 2162688 | tf_op jit(solution)/shard_map/pallas_call | solution.py:46
  31.7 2.7 %collective-permute-done.9.refs_0_ = bf16[256,512]{1,0:T(8,128)(2,1)S(1)} collective-permute-done((bf16[256,512]{1,0:T(8,128)(2,1)S(1)}, bf16[256,512]{1,0:T(8,128)(2,1)S(1)}, u32[]{:S(2)}, u32[]{:S(2)}) %collective-permute-start.9) | collective-permute-done | bytes 262176 | tf_op jit(solution)/shard_map/ppermute | solution.py:25
  34.8 2.2 %collective-permute-done.5.arrived_ref = bf16[128,512]{1,0:T(8,128)(2,1)S(1)} collective-permute-done((bf16[128,512]{1,0:T(8,128)(2,1)S(1)}, bf16[128,512]{1,0:T(8,128)(2,1)S(1)}, u32[]{:S(2)}, u32[]{:S(2)}) %collective-permute-start.5) | collective-permute-done | bytes 131104 | tf_op jit(solution)/shard_map/ppermute | solution.py:30
  37.0 2.3 %shard_map.71.value_ref = bf16[128,512]{1,0:T(8,128)(2,1)S(1)} custom-call(s32[2]{0:T(128)S(1)} %pad_add_fusion.position_ref, bf16[128,512]{1,0:T(8,128)(2,1)S(1)} %add_add_fusion.start_ref.arrived_ref, bf16[128,512]{1,0:T(8,128)(2,1)S(1)} %collective-permute-done.5.arrived_ref, bf16[512,512]{1,0:T(8,128)(2,1)S(1)} %shard_map.70.own_ref.whole_ref, ...), custom_call_target="tpu_custom_call" | custom-call | flops 1073741824 | bytes 2293760 | tf_op jit(solution)/shard_map/pallas_call | solution.py:46
  39.4 1.3 %collective-permute-done.6.other_ref = bf16[128,512]{1,0:T(8,128)(2,1)S(1)} collective-permute-done((bf16[128,512]{1,0:T(8,128)(2,1)S(1)}, bf16[128,512]{1,0:T(8,128)(2,1)S(1)}, u32[]{:S(2)}, u32[]{:S(2)}) %collective-permute-start.6) | collective-permute-done | bytes 131104 | tf_op jit(solution)/shard_map/ppermute | solution.py:25
  42.0 1.4 %shard_map.74 = (bf16[512,512]{1,0:T(8,128)(2,1)S(1)}, bf16[512,512]{1,0:T(8,128)(2,1)S(1)}, bf16[512,512]{1,0:T(8,128)(2,1)S(1)}, bf16[512,512]{1,0:T(8,128)(2,1)S(1)}) custom-call(s32[2]{0:T(128)S(1)} %pad_add_fusion.position_ref, bf16[512,512]{1,0:T(8,128)(2,1)S(1)} %get-tuple-element.43.whole_ref, bf16[256,512]{1,0:T(8,128)(2,1)S(1)} %collective-permute-done.9.refs_0_, ...), custom_call_target="tpu_custom_call" | custom-call | flops 805306368 | bytes 524288 | tf_op jit(solution)/shard_map/pallas_call | solution.py:46
  43.3 3.8 %collective-permute-done.8.other_ref = bf16[128,512]{1,0:T(8,128)(2,1)S(1)} collective-permute-done((bf16[128,512]{1,0:T(8,128)(2,1)S(1)}, bf16[128,512]{1,0:T(8,128)(2,1)S(1)}, u32[]{:S(2)}, u32[]{:S(2)}) %collective-permute-start.8) | collective-permute-done | bytes 131104 | tf_op jit(solution)/shard_map/ppermute | solution.py:25
  48.0 2.1 %collective-permute-start.11 = (bf16[128,512]{1,0:T(8,128)(2,1)S(1)}, bf16[128,512]{1,0:T(8,128)(2,1)S(1)}, u32[]{:S(2)}, u32[]{:S(2)}) collective-permute-start(bf16[128,512]{1,0:T(8,128)(2,1)S(1)} %get-tuple-element.49.value_ref), channel_id=1, source_target_pairs={{0,16},{4,20},{8,24},{12,28},{16,0},{20,4},{24,8},{28,12},{1,17},{... | collective-permute-start | bytes 393224 | tf_op jit(solution)/shard_map/ppermute | solution.py:25
  50.1 3.0 %collective-permute-done.11.other_ref = bf16[128,512]{1,0:T(8,128)(2,1)S(1)} collective-permute-done((bf16[128,512]{1,0:T(8,128)(2,1)S(1)}, bf16[128,512]{1,0:T(8,128)(2,1)S(1)}, u32[]{:S(2)}, u32[]{:S(2)}) %collective-permute-start.11) | collective-permute-done | bytes 131104 | tf_op jit(solution)/shard_map/ppermute | solution.py:25
  53.1 2.5 %shard_map.76 = (bf16[128,512]{1,0:T(8,128)(2,1)S(1)}, f32[2,128,2048]{2,1,0:T(8,128)S(1)}, f32[2,128,512]{2,1,0:T(8,128)S(1)}, f32[2,128,1]{2,1,0:T(8,128)S(1)}) custom-call(s32[2]{0:T(128)S(1)} %pad_add_fusion.position_ref, bf16[128,512]{1,0:T(8,128)(2,1)S(1)} %get-tuple-element.49.value_ref, bf16[128,512]{1,0:T(8,128)(2,1)S(1)} %collective-permute-done.11.other_ref, ...), custom_call_target="tpu_custom_call" | custom-call | flops 1073741824 | bytes 2392064 | tf_op jit(solution)/shard_map/pallas_call | solution.py:46
  55.6 3.6 %shard_map.77 = bf16[128,512]{1,0:T(8,128)(2,1)S(1)} custom-call(s32[2]{0:T(128)S(1)} %pad_add_fusion.position_ref, bf16[128,512]{1,0:T(8,128)(2,1)S(1)} %copy-done.5, bf16[128,512]{1,0:T(8,128)(2,1)S(1)} %copy-done.5, f32[2,128,2048]{2,1,0:T(8,128)S(1)} %get-tuple-element.52.slope_ref, f32[2,128,512]{2,1,0:T(8,128)S(1)} %get-tuple-element.53.unit_ref, ...), custom_call_target="tpu_custom_call" | custom-call | flops 1073741824 | bytes 2818304 | tf_op jit(solution)/shard_map/pallas_call | solution.py:46
  59.3 3.6 %collective-permute-start.16 = (bf16[128,512]{1,0:T(8,128)(2,1)S(1)}, bf16[128,512]{1,0:T(8,128)(2,1)S(1)}, u32[]{:S(2)}, u32[]{:S(2)}) collective-permute-start(bf16[128,512]{1,0:T(8,128)(2,1)S(1)} %get-tuple-element.71.refs_0_), channel_id=1, source_target_pairs={{0,3},{1,0},{2,1},{3,2},{4,7},{5,4},{6,5},{7,6},{8,11},{9,8},{10,9... | collective-permute-start | bytes 393224 | tf_op jit(solution)/shard_map/ppermute | solution.py:30
  63.9 3.6 %shard_map.78 = bf16[128,512]{1,0:T(8,128)(2,1)S(1)} custom-call(s32[2]{0:T(128)S(1)} %pad_add_fusion.position_ref, bf16[128,512]{1,0:T(8,128)(2,1)S(1)} %copy-done.5, bf16[128,512]{1,0:T(8,128)(2,1)S(1)} %collective-permute-done.12.arrived_ref, f32[2,128,2048]{2,1,0:T(8,128)S(1)} %get-tuple-element.52.slope_ref, ...), custom_call_target="tpu_custom_call" | custom-call | flops 1073741824 | bytes 2818304 | tf_op jit(solution)/shard_map/pallas_call | solution.py:46
  68.6 6.4 %collective-permute-done.15.refs_2_ = bf16[128,512]{1,0:T(8,128)(2,1)S(1)} collective-permute-done((bf16[128,512]{1,0:T(8,128)(2,1)S(1)}, bf16[128,512]{1,0:T(8,128)(2,1)S(1)}, u32[]{:S(2)}, u32[]{:S(2)}) %collective-permute-start.15) | collective-permute-done | bytes 131104 | tf_op jit(solution)/shard_map/ppermute | solution.py:30
  75.0 3.7 %shard_map.79.value_ref = bf16[128,512]{1,0:T(8,128)(2,1)S(1)} custom-call(s32[2]{0:T(128)S(1)} %pad_add_fusion.position_ref, bf16[128,512]{1,0:T(8,128)(2,1)S(1)} %copy-done.5, bf16[128,512]{1,0:T(8,128)(2,1)S(1)} %collective-permute-done.13.arrived_ref, bf16[512,512]{1,0:T(8,128)(2,1)S(1)} %shard_map.70.own_ref.whole_ref, ...), custom_call_target="tpu_custom_call" | custom-call | flops 1073741824 | bytes 2949376 | tf_op jit(solution)/shard_map/pallas_call | solution.py:46
  78.8 1.3 %collective-permute-done.17.other_ref = bf16[128,512]{1,0:T(8,128)(2,1)S(1)} collective-permute-done((bf16[128,512]{1,0:T(8,128)(2,1)S(1)}, bf16[128,512]{1,0:T(8,128)(2,1)S(1)}, u32[]{:S(2)}, u32[]{:S(2)}) %collective-permute-start.17) | collective-permute-done | bytes 131104 | tf_op jit(solution)/shard_map/ppermute | solution.py:25
  81.6 5.0 %collective-permute-done.18.other_ref = bf16[128,512]{1,0:T(8,128)(2,1)S(1)} collective-permute-done((bf16[128,512]{1,0:T(8,128)(2,1)S(1)}, bf16[128,512]{1,0:T(8,128)(2,1)S(1)}, u32[]{:S(2)}, u32[]{:S(2)}) %collective-permute-start.18) | collective-permute-done | bytes 131104 | tf_op jit(solution)/shard_map/ppermute | solution.py:25
  87.6 2.1 %collective-permute-start.19 = (bf16[128,512]{1,0:T(8,128)(2,1)S(1)}, bf16[128,512]{1,0:T(8,128)(2,1)S(1)}, u32[]{:S(2)}, u32[]{:S(2)}) collective-permute-start(bf16[128,512]{1,0:T(8,128)(2,1)S(1)} %get-tuple-element.67.value_ref), channel_id=1, source_target_pairs={{0,16},{4,20},{8,24},{12,28},{16,0},{20,4},{24,8},{28,12},{1,17},{... | collective-permute-start | bytes 393224 | tf_op jit(solution)/shard_map/ppermute | solution.py:25
  89.7 3.0 %collective-permute-done.19.other_ref = bf16[128,512]{1,0:T(8,128)(2,1)S(1)} collective-permute-done((bf16[128,512]{1,0:T(8,128)(2,1)S(1)}, bf16[128,512]{1,0:T(8,128)(2,1)S(1)}, u32[]{:S(2)}, u32[]{:S(2)}) %collective-permute-start.19) | collective-permute-done | bytes 131104 | tf_op jit(solution)/shard_map/ppermute | solution.py:25
  93.5 1.5 %collective-permute-start.22 = (bf16[128,512]{1,0:T(8,128)(2,1)S(1)}, bf16[128,512]{1,0:T(8,128)(2,1)S(1)}, u32[]{:S(2)}, u32[]{:S(2)}) collective-permute-start(bf16[128,512]{1,0:T(8,128)(2,1)S(1)} %shard_map.82.refs_0_), channel_id=1, source_target_pairs={{0,3},{1,0},{2,1},{3,2},{4,7},{5,4},{6,5},{7,6},{8,11},{9,8},{10,9... | collective-permute-start | bytes 393224 | tf_op jit(solution)/shard_map/ppermute | solution.py:30
  96.1 1.9 %collective-permute-start.20 = (bf16[128,512]{1,0:T(8,128)(2,1)S(1)}, bf16[128,512]{1,0:T(8,128)(2,1)S(1)}, u32[]{:S(2)}, u32[]{:S(2)}) collective-permute-start(bf16[128,512]{1,0:T(8,128)(2,1)S(1)} %shard_map.82.refs_0_), channel_id=1, source_target_pairs={{0,1},{1,2},{2,3},{3,0},{4,5},{5,6},{6,7},{7,4},{8,9},{9,10},{10,1... | collective-permute-start | bytes 393224 | tf_op jit(solution)/shard_map/ppermute | solution.py:30
  98.0 8.0 %shard_map.83 = (f32[2,512,2048]{2,1,0:T(8,128)S(1)}, f32[2,512,512]{2,1,0:T(8,128)S(1)}, f32[2,512,1]{2,1,0:T(8,128)S(1)}, bf16[2,128,512]{2,1,0:T(8,128)(2,1)S(1)}, bf16[2,512,512]{2,1,0:T(8,128)(2,1)S(1)}) custom-call(s32[2]{0:T(128)S(1)} %pad_add_fusion.position_ref, bf16[128,512]{1,0:T(8,128)(2,1)S(1)} %get-tuple-element.71.refs_0_, ...), custom_call_target="tpu_custom_call" | custom-call | flops 4294967296 | bytes 2228224 | tf_op jit(solution)/shard_map/pallas_call | solution.py:46
  106.5 7.4 %shard_map.84 = (f32[2,128,2048]{2,1,0:T(8,128)}, f32[2,512,512]{2,1,0:T(8,128)}) custom-call(s32[2]{0:T(128)S(1)} %pad_add_fusion.position_ref, bf16[128,512]{1,0:T(8,128)(2,1)S(1)} %shard_map.82.refs_0_, bf16[128,512]{1,0:T(8,128)(2,1)S(1)} %collective-permute-done.20.refs_1_, bf16[128,512]{1,0:T(8,128)(2,1)S(1)} %collective-permute-done.21.refs_2_, ...), custom_call_target="tpu_custom_call" | custom-call | flops 4294967296 | bytes 5178368 | tf_op jit(solution)/shard_map/pallas_call | solution.py:46
  (50 shorter events, 14.8 us)
Async XLA Ops:
  0.6 1.3 %copy-start = (bf16[1280,512]{1,0:T(8,128)(2,1)S(1)}, bf16[1280,512]{1,0:T(8,128)(2,1)}, u32[]{:S(2)}) copy-start(bf16[1280,512]{1,0:T(8,128)(2,1)} %param.6) | copy-start | bytes 3932164
  2.9 8.0 %collective-permute-start = (bf16[128,512]{1,0:T(8,128)(2,1)S(1)}, bf16[128,512]{1,0:T(8,128)(2,1)S(1)}, u32[]{:S(2)}, u32[]{:S(2)}) collective-permute-start(bf16[128,512]{1,0:T(8,128)(2,1)S(1)} %select_select_fusion), channel_id=1, source_target_pairs={{0,4},{4,0},{8,12},{12,8},{16,20},{20,16},{24,28},{28,24},{1,5},{5... | collective-permute-start | bytes 393224 | tf_op jit(solution)/shard_map/ppermute | solution.py:25
  3.6 2.2 %copy-start.1 = (bf16[2,512,2048]{2,1,0:T(8,128)(2,1)S(1)}, bf16[2,512,2048]{2,1,0:T(8,128)(2,1)}, u32[]{:S(2)}) copy-start(bf16[2,512,2048]{2,1,0:T(8,128)(2,1)} %refs_9_.1) | copy-start | bytes 12582916
  5.7 2.2 %copy-start.3 = (bf16[2,2048,512]{2,1,0:T(8,128)(2,1)S(1)}, bf16[2,2048,512]{2,1,0:T(8,128)(2,1)}, u32[]{:S(2)}) copy-start(bf16[2,2048,512]{2,1,0:T(8,128)(2,1)} %refs_10_.1) | copy-start | bytes 12582916
  7.9 13.9 %copy-start.2 = (bf16[2,512,2048]{2,1,0:T(8,128)(2,1)S(1)}, bf16[2,512,2048]{2,1,0:T(8,128)(2,1)}, u32[]{:S(2)}) copy-start(bf16[2,512,2048]{2,1,0:T(8,128)(2,1)} %refs_9_.1) | copy-start | bytes 12582916
  10.8 13.3 %collective-permute-start.7 = (bf16[512,512]{1,0:T(8,128)(2,1)S(1)}, bf16[512,512]{1,0:T(8,128)(2,1)S(1)}, u32[]{:S(2)}, u32[]{:S(2)}) collective-permute-start(bf16[512,512]{1,0:T(8,128)(2,1)S(1)} %shard_map.70.own_ref.whole_ref), channel_id=1, source_target_pairs={{0,4},{4,0},{8,12},{12,8},{16,20},{20,16},{24,28},{28,24},{1,5},{5... | collective-permute-start | bytes 1572872 | tf_op jit(solution)/shard_map/ppermute | solution.py:25
  11.0 7.9 %collective-permute-start.3 = (bf16[128,512]{1,0:T(8,128)(2,1)S(1)}, bf16[128,512]{1,0:T(8,128)(2,1)S(1)}, u32[]{:S(2)}, u32[]{:S(2)}) collective-permute-start(bf16[128,512]{1,0:T(8,128)(2,1)S(1)} %fusion), channel_id=1, source_target_pairs={{0,24},{4,28},{8,16},{12,20},{16,8},{20,12},{24,0},{28,4},{1,25},{... | collective-permute-start | bytes 393224 | tf_op jit(solution)/shard_map/ppermute | solution.py:25
  15.0 6.5 %collective-permute-start.2 = (bf16[128,512]{1,0:T(8,128)(2,1)S(1)}, bf16[128,512]{1,0:T(8,128)(2,1)S(1)}, u32[]{:S(2)}, u32[]{:S(2)}) collective-permute-start(bf16[128,512]{1,0:T(8,128)(2,1)S(1)} %fusion), channel_id=1, source_target_pairs={{0,16},{4,20},{8,24},{12,28},{16,0},{20,4},{24,8},{28,12},{1,17},{... | collective-permute-start | bytes 393224 | tf_op jit(solution)/shard_map/ppermute | solution.py:25
  15.5 6.3 %collective-permute-start.1 = (bf16[128,512]{1,0:T(8,128)(2,1)S(1)}, bf16[128,512]{1,0:T(8,128)(2,1)S(1)}, u32[]{:S(2)}, u32[]{:S(2)}) collective-permute-start(bf16[128,512]{1,0:T(8,128)(2,1)S(1)} %fusion), channel_id=1, source_target_pairs={{0,8},{4,12},{8,0},{12,4},{16,24},{20,28},{24,16},{28,20},{1,9},{5... | collective-permute-start | bytes 393224 | tf_op jit(solution)/shard_map/ppermute | solution.py:25
  24.1 5.3 %collective-permute-start.4 = (bf16[128,512]{1,0:T(8,128)(2,1)S(1)}, bf16[128,512]{1,0:T(8,128)(2,1)S(1)}, u32[]{:S(2)}, u32[]{:S(2)}) collective-permute-start(bf16[128,512]{1,0:T(8,128)(2,1)S(1)} %shard_map.68), channel_id=1, source_target_pairs={{0,4},{4,8},{8,12},{12,16},{16,20},{20,24},{24,28},{28,0},{1,5},{5... | collective-permute-start | bytes 393224 | tf_op jit(solution)/shard_map/ppermute | solution.py:30
  25.2 9.2 %collective-permute-start.9 = (bf16[256,512]{1,0:T(8,128)(2,1)S(1)}, bf16[256,512]{1,0:T(8,128)(2,1)S(1)}, u32[]{:S(2)}, u32[]{:S(2)}) collective-permute-start(bf16[256,512]{1,0:T(8,128)(2,1)S(1)} %get-tuple-element.44), channel_id=1, source_target_pairs={{0,8},{4,12},{8,0},{12,4},{16,24},{20,28},{24,16},{28,20},{1,9},{5... | collective-permute-start | bytes 786440 | tf_op jit(solution)/shard_map/ppermute | solution.py:25
  31.7 5.3 %collective-permute-start.5 = (bf16[128,512]{1,0:T(8,128)(2,1)S(1)}, bf16[128,512]{1,0:T(8,128)(2,1)S(1)}, u32[]{:S(2)}, u32[]{:S(2)}) collective-permute-start(bf16[128,512]{1,0:T(8,128)(2,1)S(1)} %shard_map.69), channel_id=1, source_target_pairs={{0,4},{4,8},{8,12},{12,16},{16,20},{20,24},{24,28},{28,0},{1,5},{5... | collective-permute-start | bytes 393224 | tf_op jit(solution)/shard_map/ppermute | solution.py:30
  34.4 7.5 %collective-permute-start.10 = (bf16[256,512]{1,0:T(8,128)(2,1)S(1)}, bf16[256,512]{1,0:T(8,128)(2,1)S(1)}, u32[]{:S(2)}, u32[]{:S(2)}) collective-permute-start(bf16[256,512]{1,0:T(8,128)(2,1)S(1)} %collective-permute-done.9.refs_0_), channel_id=1, source_target_pairs={{0,4},{4,0},{8,12},{12,8},{16,20},{20,16},{24,28},{28,24},{1,5},{5... | collective-permute-start | bytes 786440 | tf_op jit(solution)/shard_map/ppermute | solution.py:25
  39.4 1.4 %collective-permute-start.6 = (bf16[128,512]{1,0:T(8,128)(2,1)S(1)}, bf16[128,512]{1,0:T(8,128)(2,1)S(1)}, u32[]{:S(2)}, u32[]{:S(2)}) collective-permute-start(bf16[128,512]{1,0:T(8,128)(2,1)S(1)} %shard_map.71.value_ref), channel_id=1, source_target_pairs={{0,4},{4,0},{8,12},{12,8},{16,20},{20,16},{24,28},{28,24},{1,5},{5... | collective-permute-start | bytes 393224 | tf_op jit(solution)/shard_map/ppermute | solution.py:25
  41.5 5.6 %collective-permute-start.8 = (bf16[128,512]{1,0:T(8,128)(2,1)S(1)}, bf16[128,512]{1,0:T(8,128)(2,1)S(1)}, u32[]{:S(2)}, u32[]{:S(2)}) collective-permute-start(bf16[128,512]{1,0:T(8,128)(2,1)S(1)} %get-tuple-element.42.value_ref), channel_id=1, source_target_pairs={{0,8},{4,12},{8,0},{12,4},{16,24},{20,28},{24,16},{28,20},{1,9},{5... | collective-permute-start | bytes 393224 | tf_op jit(solution)/shard_map/ppermute | solution.py:25
  48.0 5.1 %collective-permute-start.11 = (bf16[128,512]{1,0:T(8,128)(2,1)S(1)}, bf16[128,512]{1,0:T(8,128)(2,1)S(1)}, u32[]{:S(2)}, u32[]{:S(2)}) collective-permute-start(bf16[128,512]{1,0:T(8,128)(2,1)S(1)} %get-tuple-element.49.value_ref), channel_id=1, source_target_pairs={{0,16},{4,20},{8,24},{12,28},{16,0},{20,4},{24,8},{28,12},{1,17},{... | collective-permute-start | bytes 393224 | tf_op jit(solution)/shard_map/ppermute | solution.py:25
  53.1 2.5 %copy-start.5 = (bf16[128,512]{1,0:T(8,128)(2,1)S(1)}, bf16[128,512]{1,0:T(8,128)(2,1)}, u32[]{:S(2)}) copy-start(bf16[128,512]{1,0:T(8,128)(2,1)} %final_ref.7) | copy-start | bytes 393220
  59.2 4.7 %collective-permute-start.12 = (bf16[128,512]{1,0:T(8,128)(2,1)S(1)}, bf16[128,512]{1,0:T(8,128)(2,1)S(1)}, u32[]{:S(2)}, u32[]{:S(2)}) collective-permute-start(bf16[128,512]{1,0:T(8,128)(2,1)S(1)} %shard_map.77), channel_id=1, source_target_pairs={{0,28},{4,0},{8,4},{12,8},{16,12},{20,16},{24,20},{28,24},{1,29},{... | collective-permute-start | bytes 393224 | tf_op jit(solution)/shard_map/ppermute | solution.py:30
  59.3 9.3 %collective-permute-start.16 = (bf16[128,512]{1,0:T(8,128)(2,1)S(1)}, bf16[128,512]{1,0:T(8,128)(2,1)S(1)}, u32[]{:S(2)}, u32[]{:S(2)}) collective-permute-start(bf16[128,512]{1,0:T(8,128)(2,1)S(1)} %get-tuple-element.71.refs_0_), channel_id=1, source_target_pairs={{0,3},{1,0},{2,1},{3,2},{4,7},{5,4},{6,5},{7,6},{8,11},{9,8},{10,9... | collective-permute-start | bytes 393224 | tf_op jit(solution)/shard_map/ppermute | solution.py:30
  62.9 12.1 %collective-permute-start.15 = (bf16[128,512]{1,0:T(8,128)(2,1)S(1)}, bf16[128,512]{1,0:T(8,128)(2,1)S(1)}, u32[]{:S(2)}, u32[]{:S(2)}) collective-permute-start(bf16[128,512]{1,0:T(8,128)(2,1)S(1)} %get-tuple-element.71.refs_0_), channel_id=1, source_target_pairs={{0,2},{1,3},{2,0},{3,1},{4,6},{5,7},{6,4},{7,5},{8,10},{9,11},{10,... | collective-permute-start | bytes 393224 | tf_op jit(solution)/shard_map/ppermute | solution.py:30
  62.9 12.1 %collective-permute-start.14 = (bf16[128,512]{1,0:T(8,128)(2,1)S(1)}, bf16[128,512]{1,0:T(8,128)(2,1)S(1)}, u32[]{:S(2)}, u32[]{:S(2)}) collective-permute-start(bf16[128,512]{1,0:T(8,128)(2,1)S(1)} %get-tuple-element.71.refs_0_), channel_id=1, source_target_pairs={{0,1},{1,2},{2,3},{3,0},{4,5},{5,6},{6,7},{7,4},{8,9},{9,10},{10,1... | collective-permute-start | bytes 393224 | tf_op jit(solution)/shard_map/ppermute | solution.py:30
  67.6 7.4 %collective-permute-start.13 = (bf16[128,512]{1,0:T(8,128)(2,1)S(1)}, bf16[128,512]{1,0:T(8,128)(2,1)S(1)}, u32[]{:S(2)}, u32[]{:S(2)}) collective-permute-start(bf16[128,512]{1,0:T(8,128)(2,1)S(1)} %shard_map.78), channel_id=1, source_target_pairs={{0,28},{4,0},{8,4},{12,8},{16,12},{20,16},{24,20},{28,24},{1,29},{... | collective-permute-start | bytes 393224 | tf_op jit(solution)/shard_map/ppermute | solution.py:30
  75.0 23.0 %copy-start.4 = (bf16[2,2048,512]{2,1,0:T(8,128)(2,1)S(1)}, bf16[2,2048,512]{2,1,0:T(8,128)(2,1)}, u32[]{:S(2)}) copy-start(bf16[2,2048,512]{2,1,0:T(8,128)(2,1)} %refs_10_.1) | copy-start | bytes 12582916
  78.7 1.4 %collective-permute-start.17 = (bf16[128,512]{1,0:T(8,128)(2,1)S(1)}, bf16[128,512]{1,0:T(8,128)(2,1)S(1)}, u32[]{:S(2)}, u32[]{:S(2)}) collective-permute-start(bf16[128,512]{1,0:T(8,128)(2,1)S(1)} %shard_map.79.value_ref), channel_id=1, source_target_pairs={{0,4},{4,0},{8,12},{12,8},{16,20},{20,16},{24,28},{28,24},{1,5},{5... | collective-permute-start | bytes 393224 | tf_op jit(solution)/shard_map/ppermute | solution.py:25
  81.0 5.6 %collective-permute-start.18 = (bf16[128,512]{1,0:T(8,128)(2,1)S(1)}, bf16[128,512]{1,0:T(8,128)(2,1)S(1)}, u32[]{:S(2)}, u32[]{:S(2)}) collective-permute-start(bf16[128,512]{1,0:T(8,128)(2,1)S(1)} %get-tuple-element.64.value_ref), channel_id=1, source_target_pairs={{0,8},{4,12},{8,0},{12,4},{16,24},{20,28},{24,16},{28,20},{1,9},{5... | collective-permute-start | bytes 393224 | tf_op jit(solution)/shard_map/ppermute | solution.py:25
  87.6 5.0 %collective-permute-start.19 = (bf16[128,512]{1,0:T(8,128)(2,1)S(1)}, bf16[128,512]{1,0:T(8,128)(2,1)S(1)}, u32[]{:S(2)}, u32[]{:S(2)}) collective-permute-start(bf16[128,512]{1,0:T(8,128)(2,1)S(1)} %get-tuple-element.67.value_ref), channel_id=1, source_target_pairs={{0,16},{4,20},{8,24},{12,28},{16,0},{20,4},{24,8},{28,12},{1,17},{... | collective-permute-start | bytes 393224 | tf_op jit(solution)/shard_map/ppermute | solution.py:25
  93.5 12.5 %collective-permute-start.22 = (bf16[128,512]{1,0:T(8,128)(2,1)S(1)}, bf16[128,512]{1,0:T(8,128)(2,1)S(1)}, u32[]{:S(2)}, u32[]{:S(2)}) collective-permute-start(bf16[128,512]{1,0:T(8,128)(2,1)S(1)} %shard_map.82.refs_0_), channel_id=1, source_target_pairs={{0,3},{1,0},{2,1},{3,2},{4,7},{5,4},{6,5},{7,6},{8,11},{9,8},{10,9... | collective-permute-start | bytes 393224 | tf_op jit(solution)/shard_map/ppermute | solution.py:30
  95.1 11.4 %collective-permute-start.21 = (bf16[128,512]{1,0:T(8,128)(2,1)S(1)}, bf16[128,512]{1,0:T(8,128)(2,1)S(1)}, u32[]{:S(2)}, u32[]{:S(2)}) collective-permute-start(bf16[128,512]{1,0:T(8,128)(2,1)S(1)} %shard_map.82.refs_0_), channel_id=1, source_target_pairs={{0,2},{1,3},{2,0},{3,1},{4,6},{5,7},{6,4},{7,5},{8,10},{9,11},{10,... | collective-permute-start | bytes 393224 | tf_op jit(solution)/shard_map/ppermute | solution.py:30
  96.1 10.4 %collective-permute-start.20 = (bf16[128,512]{1,0:T(8,128)(2,1)S(1)}, bf16[128,512]{1,0:T(8,128)(2,1)S(1)}, u32[]{:S(2)}, u32[]{:S(2)}) collective-permute-start(bf16[128,512]{1,0:T(8,128)(2,1)S(1)} %shard_map.82.refs_0_), channel_id=1, source_target_pairs={{0,1},{1,2},{2,3},{3,0},{4,5},{5,6},{6,7},{7,4},{8,9},{9,10},{10,1... | collective-permute-start | bytes 393224 | tf_op jit(solution)/shard_map/ppermute | solution.py:30

commit v4 on v3

--- a/solution.py
+++ b/solution.py
@@ -14,6 +14,8 @@
 EPSILON = 1e-06
 GAMMA = 0.05
 CHUNK = 512
+COARSE_STEPS = 2
+LARGE = 44 << 20
 MIB = 1 << 20
 
 LOW = jnp.bfloat16
@@ -40,17 +42,20 @@
     )
 
 
-def call(body, flops, limit, out_shapes, position, *args):
+def call(body, flops, limit, out_shapes, *args, scratch=()):
     whole = pl.BlockSpec(memory_space=pltpu.VMEM)
     moved = sum(a.size * a.dtype.itemsize for a in args)
     return pl.pallas_call(
         body,
         out_shape=out_shapes,
-        in_specs=[pl.BlockSpec(memory_space=pltpu.SMEM)] + [whole] * len(args),
-        out_specs=jax.tree.map(lambda unused: whole, out_shapes),
+        in_specs=[whole] * len(args),
+        out_specs=jax.tree.map(
+            lambda unused: pl.BlockSpec(memory_space=pl.ANY) if scratch else whole, out_shapes
+        ),
+        scratch_shapes=list(scratch),
         compiler_params=pltpu.CompilerParams(vmem_limit_bytes=limit * MIB),
         cost_estimate=pl.CostEstimate(flops=flops, bytes_accessed=moved // 4, transcendentals=0),
-    )(position, *args)
+    )(*args)
 
 
 def shape(dims, kind):
@@ -72,9 +77,9 @@
 
 def block_adjoint(adjoint, slope_ref, unit_ref, scale_ref, up_ref, down_ref):
     for layer in reversed(range(up_ref.shape[0])):
-        toward_hidden = dot_transposed(adjoint, down_ref[layer])
+        toward_hidden = dot(adjoint, down_ref[layer])
         delta = (toward_hidden * slope_ref[layer]).astype(LOW)
-        toward_normed = dot_transposed(delta, up_ref[layer])
+        toward_normed = dot(delta, up_ref[layer])
         unit = unit_ref[layer]
         inner = jnp.mean(toward_normed * unit, axis=-1, keepdims=True)
         adjoint = adjoint + scale_ref[layer] * (toward_normed - unit * inner)
@@ -107,10 +112,39 @@
     return dot_transposed((columns == chosen).astype(LOW), values).astype(LOW)
 
 
-def coarse_kernel(position_ref, up_ref, down_ref, out_ref):
-    total = dot(up_ref[0], down_ref[0])
-    for layer in range(1, up_ref.shape[0]):
-        total = total + dot(up_ref[layer], down_ref[layer])
+def sum_kernel(*refs):
+    total = refs[0][...]
+    for ref in refs[1:-1]:
+        total = total + ref[...]
+    refs[-1][...] = total
+
+
+def turn_kernel(in_ref, out_ref):
+    for layer in range(in_ref.shape[0]):
+        out_ref[layer] = in_ref[layer].T
+
+
+def coarse_kernel(up_hbm, down_hbm, out_ref, up_ref, down_ref, sems):
+    layers, _, inner = up_ref.shape
+    step = inner // COARSE_STEPS
+    copies = []
+    for layer in range(layers):
+        for begin in range(0, inner, step):
+            for source, target in (
+                (up_hbm.at[layer, :, pl.ds(begin, step)], up_ref.at[layer, :, pl.ds(begin, step)]),
+                (down_hbm.at[layer, pl.ds(begin, step)], down_ref.at[layer, pl.ds(begin, step)]),
+            ):
+                copies.append(pltpu.make_async_copy(source, target, sems.at[len(copies)]))
+                copies[-1].start()
+    total = None
+    for layer in range(layers):
+        for begin in range(0, inner, step):
+            copies.pop(0).wait()
+            copies.pop(0).wait()
+            more = dot(
+                up_ref[layer, :, begin : begin + step], down_ref[layer, begin : begin + step]
+            )
+            total = more if total is None else total + more
     out_ref[...] = (GAMMA * total).astype(LOW)
 
 
@@ -118,9 +152,9 @@
     return left.astype(FULL) + right.astype(FULL) + dot(left, right)
 
 
-def join_kernel(bit, last, position_ref, whole_ref, *refs):
-    upper = ((position_ref[0] >> bit) & 1) == 1
-    odd = (position_ref[0] & 1) == 1
+def join_kernel(bit, last, whole_ref, *refs):
+    upper = ((lax.axis_index("depth") >> bit) & 1) == 1
+    odd = (lax.axis_index("depth") & 1) == 1
     refs = list(refs)
     whole = whole_ref[...]
     half = whole.shape[0] // 2
@@ -149,7 +183,7 @@
         refs[5][...] = jnp.where(odd, both[half:], both[:half])
 
 
-def matrix_scan(own, position, bits):
+def matrix_scan(own, bits):
     width = own.shape[0]
     square = shape(own.shape, LOW)
     half = shape((width // 2, width), LOW)
@@ -167,7 +201,6 @@
             6 * width**3,
             12,
             [square] * 4 + ([] if last else [square, half]),
-            position,
             *args,
         )
         steps.append((prefix, suffix, outs[0], outs[1]))
@@ -177,8 +210,8 @@
     return steps
 
 
-def scan_values(forward, bit, position_ref, value_ref, other_ref):
-    upper = ((position_ref[0] >> bit) & 1) == 1
+def scan_values(forward, bit, value_ref, other_ref):
+    upper = ((lax.axis_index("depth") >> bit) & 1) == 1
     value, other = value_ref[...].astype(FULL), other_ref[...].astype(FULL)
     lower_value = jnp.where(upper, other, value)
     upper_value = jnp.where(upper, value, other)
@@ -187,8 +220,8 @@
     return jnp.logical_not(upper), upper_value, lower_value
 
 
-def scan_kernel(forward, bit, position_ref, value_ref, other_ref, matrix_ref, *refs):
-    receives, donor, keep = scan_values(forward, bit, position_ref, value_ref, other_ref)
+def scan_kernel(forward, bit, value_ref, other_ref, matrix_ref, *refs):
+    receives, donor, keep = scan_values(forward, bit, value_ref, other_ref)
     times = dot if forward else dot_transposed
     if bit == 0:
         out_ref, next_ref = refs
@@ -201,8 +234,8 @@
     next_ref[...] = (keep + donor + times(donor, matrix_ref[...])).astype(LOW)
 
 
-def scan_end(forward, bit, position_ref, value_ref, other_ref, total_ref, part_ref):
-    receives, donor, _ = scan_values(forward, bit, position_ref, value_ref, other_ref)
+def scan_end(forward, bit, value_ref, other_ref, total_ref, part_ref):
+    receives, donor, _ = scan_values(forward, bit, value_ref, other_ref)
     times = dot if forward else dot_transposed
     more = donor + times(donor, part_ref[...])
     return total_ref[...] + jnp.where(receives, more, jnp.zeros_like(more))
@@ -212,14 +245,15 @@
     depth = lax.axis_size("depth")
     bits = depth.bit_length() - 1
     assert depth == 1 << bits and bits >= 2
-    position = lax.axis_index("depth")
     parts = lax.axis_size("dp")
-    place = jnp.stack([position, lax.axis_index("dp")]).astype(jnp.int32)
     layers, width, inner_width = w_up.shape
     rows = token_ids.shape[0]
     layer_flops = 4 * rows * width * inner_width
+    state_low = shape((rows, width), LOW)
+    state_full = shape((rows, width), FULL)
+    apart = pl.BlockSpec(memory_space=pltpu.HBM)
     vocab_rows = embedding.shape[0]
-    local_ids = token_ids - position * vocab_rows
+    local_ids = token_ids - lax.axis_index("depth") * vocab_rows
     inside = (local_ids >= 0) & (local_ids < vocab_rows)
     picked = jnp.take(embedding, jnp.clip(local_ids, 0, vocab_rows - 1), axis=0)
     picked = jnp.where(inside[:, None], picked, jnp.zeros_like(picked))
@@ -227,41 +261,47 @@
     arrivals = []
     for mask in range(2, depth, 2):
         arrivals.append(swapped(picked, "depth", mask))
-    for arrival in arrivals:
-        picked = picked + arrival
-    start = picked
-
-    own = call(
+    start = call(sum_kernel, rows * width, 8, state_low, picked, *arrivals)
+
+    whole = pl.BlockSpec(memory_space=pltpu.VMEM)
+    own, w_up, w_down = pl.pallas_call(
         coarse_kernel,
-        4 * width * width * inner_width,
-        12,
-        shape((width, width), LOW),
-        place,
-        w_up,
-        w_down,
-    )
-    steps = matrix_scan(own, place, bits)
-    state_low = shape((rows, width), LOW)
-    state_full = shape((rows, width), FULL)
-
-    def forward_kernel(position_ref, start_ref, arrived_ref, up_ref, down_ref, out_ref):
-        state = jnp.where(position_ref[0] == 0, start_ref[...], arrived_ref[...]).astype(FULL)
+        out_shape=[shape((width, width), LOW), shape(w_up.shape, LOW), shape(w_down.shape, LOW)],
+        in_specs=[apart, apart],
+        out_specs=[whole] * 3,
+        scratch_shapes=[pltpu.SemaphoreType.DMA((2 * layers * COARSE_STEPS,))],
+        name="coarse",
+        compiler_params=pltpu.CompilerParams(vmem_limit_bytes=LARGE),
+        cost_estimate=pl.CostEstimate(
+            flops=4 * width * width * inner_width, bytes_accessed=2 * MIB, transcendentals=0
+        ),
+    )(w_up, w_down)
+    steps = matrix_scan(own, bits)
+
+    def forward_kernel(start_ref, arrived_ref, up_ref, down_ref, out_ref):
+        state = jnp.where(lax.axis_index("depth") == 0, start_ref[...], arrived_ref[...]).astype(FULL)
         out_ref[...] = block_forward(state, up_ref, down_ref).astype(LOW)
 
-    def value_kernel(position_ref, start_ref, arrived_ref, own_ref, up_ref, down_ref, out_ref):
-        state = jnp.where(position_ref[0] == 0, start_ref[...], arrived_ref[...]).astype(FULL)
+    turned = {}
+    for name, weights in (("turn_up", w_up), ("turn_down", w_down)):
+        turned_shape = (layers, weights.shape[2], weights.shape[1])
+        turned[name] = call(turn_kernel, layer_flops, 12, shape(turned_shape, LOW), weights)
+    up_turned, down_turned = turned["turn_up"], turned["turn_down"]
+
+    def value_kernel(start_ref, arrived_ref, own_ref, up_ref, down_ref, out_ref):
+        state = jnp.where(lax.axis_index("depth") == 0, start_ref[...], arrived_ref[...]).astype(FULL)
         ended = block_forward(state, up_ref, down_ref)
         change = ended - state - dot(state, own_ref[...])
-        out_ref[...] = jnp.where(position_ref[0] == 0, ended, change).astype(LOW)
+        out_ref[...] = jnp.where(lax.axis_index("depth") == 0, ended, change).astype(LOW)
 
     arrived = start
     for _ in range(RELAX - 1):
         ended = call(
-            forward_kernel, layers * layer_flops, 12, state_low, place, start, arrived, w_up, w_down
+            forward_kernel, layers * layer_flops, 12, state_low, start, arrived, w_up, w_down
         )
         arrived = rotated(ended, "depth", 1)
     value = call(
-        value_kernel, layers * layer_flops, 12, state_low, place, start, arrived, own, w_up, w_down
+        value_kernel, layers * layer_flops, 12, state_low, start, arrived, own, w_up, w_down
     )
 
     def scanned(forward, value):
@@ -277,8 +317,7 @@
                 4 * rows * width * width,
                 8,
                 [state_full, state_low],
-                place,
-                *args,
+                    *args,
             )
         other = swapped(value, "depth", 1 << (bits - 1))
         prefix, suffix, unused, unused = steps[-1]
@@ -291,13 +330,13 @@
     ]
 
     def states_kernel(
-        position_ref, value_ref, other_ref, total_ref, part_ref, start_ref, up_ref, down_ref,
+        value_ref, other_ref, total_ref, part_ref, start_ref, up_ref, down_ref,
         low_ref, slope_ref, unit_ref, scale_ref,
     ):
         corrected = scan_end(
-            True, bits - 1, position_ref, value_ref, other_ref, total_ref, part_ref
-        )
-        corrected = jnp.where(position_ref[0] == 0, start_ref[...], corrected.astype(LOW))
+            True, bits - 1, value_ref, other_ref, total_ref, part_ref
+        )
+        corrected = jnp.where(lax.axis_index("depth") == 0, start_ref[...], corrected.astype(LOW))
         low_ref[...] = corrected
         save_forward(
             corrected.astype(FULL), up_ref, down_ref, slope_ref, unit_ref, scale_ref
@@ -308,7 +347,6 @@
         layers * layer_flops,
         12,
         [state_low] + saved_shapes(rows),
-        place,
         *scanned(True, value),
         start,
         w_up,
@@ -316,26 +354,32 @@
     )
 
     def adjoint_kernel(
-        position_ref, final_ref, arrived_ref, slope_ref, unit_ref, scale_ref, up_ref, down_ref,
+        final_ref, arrived_ref, slope_ref, unit_ref, scale_ref, up_ref, down_ref,
         out_ref,
     ):
-        ends = position_ref[0] == depth - 1
+        ends = lax.axis_index("depth") == depth - 1
         adjoint = jnp.where(ends, final_ref[...], arrived_ref[...]).astype(FULL)
         out_ref[...] = block_adjoint(
             adjoint, slope_ref, unit_ref, scale_ref, up_ref, down_ref
         ).astype(LOW)
 
     def adjoint_value_kernel(
-        position_ref, final_ref, arrived_ref, own_ref, slope_ref, unit_ref, scale_ref, up_ref,
+        final_ref, arrived_ref, own_ref, slope_ref, unit_ref, scale_ref, up_ref,
         down_ref, out_ref,
     ):
-        ends = position_ref[0] == depth - 1
+        ends = lax.axis_index("depth") == depth - 1
         adjoint = jnp.where(ends, final_ref[...], arrived_ref[...]).astype(FULL)
         begun = block_adjoint(adjoint, slope_ref, unit_ref, scale_ref, up_ref, down_ref)
         change = begun - adjoint - dot_transposed(adjoint, own_ref[...])
         out_ref[...] = jnp.where(ends, begun, change).astype(LOW)
 
-    pieces = lambda block: [block] + [rotated(block, "dp", d) for d in range(1, parts)]
+
+    def pieces(block):
+        arrived = [block]
+        for distance in range(1, parts):
+            arrived.append(rotated(block, "dp", distance))
+        return arrived
+
     arrived = cotangent
     for sweep in range(RELAX - 1):
         begun = call(
@@ -343,77 +387,85 @@
             layers * layer_flops,
             12,
             state_low,
-            place,
             cotangent,
             arrived,
             slope,
             unit,
             scale,
-            w_up,
-            w_down,
+            up_turned,
+            down_turned,
         )
         if sweep == 0:
             begun, corrected = lax.optimization_barrier((begun, corrected))
             corrected_pieces = pieces(corrected)
         arrived = rotated(begun, "depth", -1)
-    arrived, corrected_pieces = lax.optimization_barrier((arrived, corrected_pieces))
     value = call(
         adjoint_value_kernel,
         layers * layer_flops,
         12,
         state_low,
-        place,
         cotangent,
         arrived,
         own,
         slope,
         unit,
         scale,
-        w_up,
-        w_down,
+        up_turned,
+        down_turned,
     )
 
     def end_kernel(
-        position_ref, value_ref, other_ref, total_ref, part_ref, final_ref, out_ref
+        value_ref, other_ref, total_ref, part_ref, final_ref, out_ref
     ):
         adjoint = scan_end(
-            False, bits - 1, position_ref, value_ref, other_ref, total_ref, part_ref
-        )
-        ends = position_ref[0] == depth - 1
+            False, bits - 1, value_ref, other_ref, total_ref, part_ref
+        )
+        ends = lax.axis_index("depth") == depth - 1
         out_ref[...] = jnp.where(ends, final_ref[...], adjoint.astype(LOW))
 
     adjoint = call(
-        end_kernel, 2 * rows * width * width, 8, state_low, place, *scanned(False, value), cotangent
+        end_kernel, 2 * rows * width * width, 8, state_low, *scanned(False, value), cotangent
     )
 
     corrected_pieces, adjoint = lax.optimization_barrier((corrected_pieces, adjoint))
     adjoint_pieces = pieces(adjoint)
 
-    def recompute_kernel(count, position_ref, *refs):
+    def recompute_kernel(count, *refs):
         state = jnp.concatenate([ref[...] for ref in refs[:count]], axis=0).astype(FULL)
         normed_ref, hidden_ref = refs[-2:]
 
         def keep(layer, normed, hidden):
-            normed_ref[layer] = own_columns(normed, position_ref[1], width // parts)
-            hidden_ref[layer] = own_columns(hidden, position_ref[1], inner_width // parts)
+            normed_ref[layer] = own_columns(normed, lax.axis_index("dp"), width // parts)
+            hidden_ref[layer] = own_columns(hidden, lax.axis_index("dp"), inner_width // parts)
 
         save_forward(state, *refs[count:-2], keep)
 
-    def grads_kernel(count, position_ref, *refs):
+    def grads_kernel(count, *refs):
         adjoint = jnp.concatenate([ref[...] for ref in refs[:count]], axis=0).astype(FULL)
         slope_ref, unit_ref, scale_ref, normed_ref, hidden_ref = refs[count : count + 5]
-        up_ref, down_ref, grad_up_ref, grad_down_ref = refs[count + 5 :]
+        up_ref, down_ref, grad_up_ref, grad_down_ref = refs[count + 5 : count + 9]
+        up_scratch, down_scratch, sems = refs[count + 9 :]
+        copies = []
+
+        def put(scratch, out_ref, layer, value):
+            scratch[layer] = value
+            sem = sems.at[len(copies)]
+            copies.append(pltpu.make_async_copy(scratch.at[layer], out_ref.at[layer], sem))
+            copies[-1].start()
+
         for layer in reversed(range(layers)):
             low = adjoint.astype(LOW)
-            grad_down_ref[layer] = dot(hidden_ref[layer], low)
-            toward_hidden = dot_transposed(low, down_ref[layer])
+            put(down_scratch, grad_down_ref, layer, dot(hidden_ref[layer], low))
+            toward_hidden = dot(low, down_ref[layer])
             delta = (toward_hidden * slope_ref[layer]).astype(LOW)
-            grad_up_ref[layer] = dot(normed_ref[layer], delta)
+            put(up_scratch, grad_up_ref, layer, dot(normed_ref[layer], delta))
             if layer > 0:
-                toward_normed = dot_transposed(delta, up_ref[layer])
+                toward_normed = dot(delta, up_ref[layer])
                 unit = unit_ref[layer]
                 inner = jnp.mean(toward_normed * unit, axis=-1, keepdims=True)
                 adjoint = adjoint + scale_ref[layer] * (toward_normed - unit * inner)
+        for copy in copies:
+            copy.wait()
 
     group = max(1, min(parts, CHUNK // rows))
     grads = None
@@ -427,34 +479,35 @@
         slope, unit, scale, normed, hidden = call(
             functools.partial(recompute_kernel, count),
             layers * layer_flops * count,
-            24,
+            20,
             saved_shapes(tokens)
             + [
                 shape((layers, width // parts, tokens), LOW),
                 shape((layers, inner_width // parts, tokens), LOW),
             ],
-            place,
             *inputs,
             w_up,
             w_down,
         )
+        grad_shapes = [
+            shape((layers, width // parts, inner_width), FULL),
+            shape((layers, inner_width // parts, width), FULL),
+        ]
         more = call(
             functools.partial(grads_kernel, count),
             layers * layer_flops * count,
-            24,
-            [
-                shape((layers, width // parts, inner_width), FULL),
-                shape((layers, inner_width // parts, width), FULL),
-            ],
-            place,
+            20,
+            grad_shapes,
             *adjoint_pieces[chosen],
             slope,
             unit,
             scale,
             normed,
             hidden,
-            w_up,
-            w_down,
+            up_turned,
+            down_turned,
+            scratch=[pltpu.VMEM(leaf.shape, leaf.dtype) for leaf in grad_shapes]
+            + [pltpu.SemaphoreType.DMA((2 * layers,))],
         )
         grads = more if grads is None else [a + b for a, b in zip(grads, more)]
     return tuple(grads)

time: 114 us -> 106 us (0.930)
  Pallas kernels: 45.4 us -> 35.1 us
  starting transfers between devices: 23 us -> 28.7 us
  local copies, waits for them, and re-layouts: 5.78 us -> 1.4 us
    pallas_call x17 -> x20, Pallas kernels: 45.4 us -> 35.1 us  [the longest x19 30.4 us: call(): pl.pallas_call(body, out_shape=out_shapes, in_specs=[whole] * len(args),...]
    ppermute x10, waiting for transfers between devices: 11.6 us -> 17.4 us  [rotated(): lax.ppermute(block, axis, [(i, (i + distance) % size) for i in range(size)])]
    ppermute x13, waiting for transfers between devices: 26.2 us -> 20.5 us  [swapped(): return lax.ppermute(block, axis, [(i, i ^ mask) for i in devices])]
    unnamed x12 -> x4, local copies, waits for them, and re-layouts: 4.93 us -> 0.55 us
    ppermute x10, starting transfers between devices: 10.3 us -> 14.4 us  [rotated(): lax.ppermute(block, axis, [(i, (i + distance) % size) for i in range(size)])]
    ppermute x13, starting transfers between devices: 12.6 us -> 14.3 us  [swapped(): return lax.ppermute(block, axis, [(i, i ^ mask) for i in devices])]
  transfers between devices with their start and end apart: 23 -> 23, of which waited for: 14 -> 14; matrix products, arithmetic and copies ran while one was open for 0% -> 0% of each run, Pallas kernels for 22% -> 20%
where the time goes in v4:
time: 106 us; the launch traced here: 105 us
  waiting for transfers between devices  37.9 us (36%)
  Pallas kernels  35.1 us (33%)
  starting transfers between devices  28.7 us (27%)
  local copies, waits for them, and re-layouts  1.4 us (1%)
  between operations  1.06 us (1%)
    pallas_call x19, Pallas kernels, call(): pl.pallas_call(body, out_shape=out_shapes, in_specs=[whole] * len(args),...  30.4 us
    ppermute x13, waiting for transfers between devices, swapped(): return lax.ppermute(block, axis, [(i, i ^ mask) for i in devices])  20.5 us
    ppermute x10, waiting for transfers between devices, rotated(): lax.ppermute(block, axis, [(i, (i + distance) % size) for i in range(size)])  17.4 us
    ppermute x10, starting transfers between devices, rotated(): lax.ppermute(block, axis, [(i, (i + distance) % size) for i in range(size)])  14.4 us
    ppermute x13, starting transfers between devices, swapped(): return lax.ppermute(block, axis, [(i, i ^ mask) for i in devices])  14.3 us
    pallas_call x1, Pallas kernels, block_pass(): pl.pallas_call(coarse_kernel, out_shape=[shape((width, width), LOW), shap...  4.67 us
  transfers between devices with their start and end apart: 23, of which 14 were waited for; matrix products, arithmetic and copies ran while one was open for 0% of the time, Pallas kernels for 20%

profile of v4, /device:TPU:0, one launch (start us, length us, event | category | flops | bytes accessed | tf_op | source)
XLA Modules:
  0.0 105.1 jit_solution(7028076048859823609)
XLA Ops:
  3.5 4.7 %coarse.1 = (bf16[512,512]{1,0:T(8,128)(2,1)S(1)}, bf16[2,512,2048]{2,1,0:T(8,128)(2,1)S(1)}, bf16[2,2048,512]{2,1,0:T(8,128)(2,1)S(1)}) custom-call(bf16[2,512,2048]{2,1,0:T(8,128)(2,1)} %up_hbm.1, bf16[2,2048,512]{2,1,0:T(8,128)(2,1)} %down_hbm.1), custom_call_target="tpu_custom_call" | custom-call | flops 2147483648 | bytes 2097152 | tf_op jit(solution)/shard_map/coarse/pallas_call | solution.py:267
  8.4 3.0 %collective-permute-start.1 = (bf16[128,512]{1,0:T(8,128)(2,1)S(1)}, bf16[128,512]{1,0:T(8,128)(2,1)S(1)}, u32[]{:S(2)}, u32[]{:S(2)}) collective-permute-start(bf16[128,512]{1,0:T(8,128)(2,1)S(1)} %fusion.refs_0_), channel_id=1, source_target_pairs={{0,8},{4,12},{8,0},{12,4},{16,24},{20,28},{24,16},{28,20},{1,9},{5... | collective-permute-start | bytes 393224 | tf_op jit(solution)/shard_map/ppermute | solution.py:27
  11.4 1.5 %collective-permute-start.2 = (bf16[128,512]{1,0:T(8,128)(2,1)S(1)}, bf16[128,512]{1,0:T(8,128)(2,1)S(1)}, u32[]{:S(2)}, u32[]{:S(2)}) collective-permute-start(bf16[128,512]{1,0:T(8,128)(2,1)S(1)} %fusion.refs_0_), channel_id=1, source_target_pairs={{0,16},{4,20},{8,24},{12,28},{16,0},{20,4},{24,8},{28,12},{1,17},{... | collective-permute-start | bytes 393224 | tf_op jit(solution)/shard_map/ppermute | solution.py:27
  12.9 2.3 %collective-permute-done.1.refs_1_ = bf16[128,512]{1,0:T(8,128)(2,1)S(1)} collective-permute-done((bf16[128,512]{1,0:T(8,128)(2,1)S(1)}, bf16[128,512]{1,0:T(8,128)(2,1)S(1)}, u32[]{:S(2)}, u32[]{:S(2)}) %collective-permute-start.1) | collective-permute-done | bytes 131104 | tf_op jit(solution)/shard_map/ppermute | solution.py:27
  15.3 4.1 %collective-permute-done.2.refs_2_ = bf16[128,512]{1,0:T(8,128)(2,1)S(1)} collective-permute-done((bf16[128,512]{1,0:T(8,128)(2,1)S(1)}, bf16[128,512]{1,0:T(8,128)(2,1)S(1)}, u32[]{:S(2)}, u32[]{:S(2)}) %collective-permute-start.2) | collective-permute-done | bytes 131104 | tf_op jit(solution)/shard_map/ppermute | solution.py:27
  19.4 1.7 %shard_map.69 = bf16[128,512]{1,0:T(8,128)(2,1)S(1)} custom-call(bf16[128,512]{1,0:T(8,128)(2,1)S(1)} %shard_map.68.start_ref.arrived_ref, bf16[128,512]{1,0:T(8,128)(2,1)S(1)} %shard_map.68.start_ref.arrived_ref, bf16[2,512,2048]{2,1,0:T(8,128)(2,1)S(1)} %get-tuple-element.39.up_ref.in_ref.refs_4_, ...), custom_call_target="tpu_custom_call" | custom-call | flops 1073741824 | bytes 2162688 | tf_op jit(solution)/shard_map/pallas_call | solution.py:48
  22.9 3.6 %collective-permute-done.4.arrived_ref = bf16[128,512]{1,0:T(8,128)(2,1)S(1)} collective-permute-done((bf16[128,512]{1,0:T(8,128)(2,1)S(1)}, bf16[128,512]{1,0:T(8,128)(2,1)S(1)}, u32[]{:S(2)}, u32[]{:S(2)}) %collective-permute-start.4) | collective-permute-done | bytes 131104 | tf_op jit(solution)/shard_map/ppermute | solution.py:32
  26.6 1.7 %shard_map.70 = bf16[128,512]{1,0:T(8,128)(2,1)S(1)} custom-call(bf16[128,512]{1,0:T(8,128)(2,1)S(1)} %shard_map.68.start_ref.arrived_ref, bf16[128,512]{1,0:T(8,128)(2,1)S(1)} %collective-permute-done.4.arrived_ref, bf16[2,512,2048]{2,1,0:T(8,128)(2,1)S(1)} %get-tuple-element.39.up_ref.in_ref.refs_4_, ...), custom_call_target="tpu_custom_call" | custom-call | flops 1073741824 | bytes 2162688 | tf_op jit(solution)/shard_map/pallas_call | solution.py:48
  28.5 2.4 %collective-permute-done.9.refs_0_ = bf16[256,512]{1,0:T(8,128)(2,1)S(1)} collective-permute-done((bf16[256,512]{1,0:T(8,128)(2,1)S(1)}, bf16[256,512]{1,0:T(8,128)(2,1)S(1)}, u32[]{:S(2)}, u32[]{:S(2)}) %collective-permute-start.9) | collective-permute-done | bytes 262176 | tf_op jit(solution)/shard_map/ppermute | solution.py:27
  31.9 1.9 %collective-permute-done.5.arrived_ref = bf16[128,512]{1,0:T(8,128)(2,1)S(1)} collective-permute-done((bf16[128,512]{1,0:T(8,128)(2,1)S(1)}, bf16[128,512]{1,0:T(8,128)(2,1)S(1)}, u32[]{:S(2)}, u32[]{:S(2)}) %collective-permute-start.5) | collective-permute-done | bytes 131104 | tf_op jit(solution)/shard_map/ppermute | solution.py:32
  33.8 1.7 %shard_map.71.value_ref = bf16[128,512]{1,0:T(8,128)(2,1)S(1)} custom-call(bf16[128,512]{1,0:T(8,128)(2,1)S(1)} %shard_map.68.start_ref.arrived_ref, bf16[128,512]{1,0:T(8,128)(2,1)S(1)} %collective-permute-done.5.arrived_ref, bf16[512,512]{1,0:T(8,128)(2,1)S(1)} %get-tuple-element.41.own_ref.whole_ref, ...), custom_call_target="tpu_custom_call" | custom-call | flops 1073741824 | bytes 2293760 | tf_op jit(solution)/shard_map/pallas_call | solution.py:48
  38.4 4.4 %collective-permute-done.8.other_ref = bf16[128,512]{1,0:T(8,128)(2,1)S(1)} collective-permute-done((bf16[128,512]{1,0:T(8,128)(2,1)S(1)}, bf16[128,512]{1,0:T(8,128)(2,1)S(1)}, u32[]{:S(2)}, u32[]{:S(2)}) %collective-permute-start.8) | collective-permute-done | bytes 131104 | tf_op jit(solution)/shard_map/ppermute | solution.py:27
  43.1 2.6 %collective-permute-start.11 = (bf16[128,512]{1,0:T(8,128)(2,1)S(1)}, bf16[128,512]{1,0:T(8,128)(2,1)S(1)}, u32[]{:S(2)}, u32[]{:S(2)}) collective-permute-start(bf16[128,512]{1,0:T(8,128)(2,1)S(1)} %get-tuple-element.50.value_ref), channel_id=1, source_target_pairs={{0,16},{4,20},{8,24},{12,28},{16,0},{20,4},{24,8},{28,12},{1,17},{... | collective-permute-start | bytes 393224 | tf_op jit(solution)/shard_map/ppermute | solution.py:27
  48.6 1.8 %shard_map.76 = (bf16[128,512]{1,0:T(8,128)(2,1)S(1)}, f32[2,128,2048]{2,1,0:T(8,128)S(1)}, f32[2,128,512]{2,1,0:T(8,128)S(1)}, f32[2,128,1]{2,1,0:T(8,128)S(1)}) custom-call(bf16[128,512]{1,0:T(8,128)(2,1)S(1)} %get-tuple-element.50.value_ref, bf16[128,512]{1,0:T(8,128)(2,1)S(1)} %collective-permute-done.11.other_ref, ...), custom_call_target="tpu_custom_call" | custom-call | flops 1073741824 | bytes 2392064 | tf_op jit(solution)/shard_map/pallas_call | solution.py:48
  50.5 1.6 %shard_map.79 = bf16[128,512]{1,0:T(8,128)(2,1)S(1)} custom-call(bf16[128,512]{1,0:T(8,128)(2,1)S(1)} %copy-done.1, bf16[128,512]{1,0:T(8,128)(2,1)S(1)} %copy-done.1, f32[2,128,2048]{2,1,0:T(8,128)S(1)} %get-tuple-element.53.slope_ref, f32[2,128,512]{2,1,0:T(8,128)S(1)} %get-tuple-element.54.unit_ref, f32[2,128,1]{2,1,0:T(8,128)S(1)} %get-tuple-element.55.scale_ref, ...), custom_call_target="tpu_custom_call" | custom-call | flops 1073741824 | bytes 2818304 | tf_op jit(solution)/shard_map/pallas_call | solution.py:48
  52.2 2.5 %collective-permute-done.15.arrived_ref = bf16[128,512]{1,0:T(8,128)(2,1)S(1)} collective-permute-done((bf16[128,512]{1,0:T(8,128)(2,1)S(1)}, bf16[128,512]{1,0:T(8,128)(2,1)S(1)}, u32[]{:S(2)}, u32[]{:S(2)}) %collective-permute-start.15) | collective-permute-done | bytes 131104 | tf_op jit(solution)/shard_map/ppermute | solution.py:32
  54.7 1.6 %shard_map.80 = bf16[128,512]{1,0:T(8,128)(2,1)S(1)} custom-call(bf16[128,512]{1,0:T(8,128)(2,1)S(1)} %copy-done.1, bf16[128,512]{1,0:T(8,128)(2,1)S(1)} %collective-permute-done.15.arrived_ref, f32[2,128,2048]{2,1,0:T(8,128)S(1)} %get-tuple-element.53.slope_ref, f32[2,128,512]{2,1,0:T(8,128)S(1)} %get-tuple-element.54.unit_ref, ...), custom_call_target="tpu_custom_call" | custom-call | flops 1073741824 | bytes 2818304 | tf_op jit(solution)/shard_map/pallas_call | solution.py:48
  56.3 2.8 %collective-permute-start.16 = (bf16[128,512]{1,0:T(8,128)(2,1)S(1)}, bf16[128,512]{1,0:T(8,128)(2,1)S(1)}, u32[]{:S(2)}, u32[]{:S(2)}) collective-permute-start(bf16[128,512]{1,0:T(8,128)(2,1)S(1)} %shard_map.80), channel_id=1, source_target_pairs={{0,28},{4,0},{8,4},{12,8},{16,12},{20,16},{24,20},{28,24},{1,29},{... | collective-permute-start | bytes 393224 | tf_op jit(solution)/shard_map/ppermute | solution.py:32
  59.2 2.5 %collective-permute-done.16.arrived_ref = bf16[128,512]{1,0:T(8,128)(2,1)S(1)} collective-permute-done((bf16[128,512]{1,0:T(8,128)(2,1)S(1)}, bf16[128,512]{1,0:T(8,128)(2,1)S(1)}, u32[]{:S(2)}, u32[]{:S(2)}) %collective-permute-start.16) | collective-permute-done | bytes 131104 | tf_op jit(solution)/shard_map/ppermute | solution.py:32
  61.7 1.7 %shard_map.81.value_ref = bf16[128,512]{1,0:T(8,128)(2,1)S(1)} custom-call(bf16[128,512]{1,0:T(8,128)(2,1)S(1)} %copy-done.1, bf16[128,512]{1,0:T(8,128)(2,1)S(1)} %collective-permute-done.16.arrived_ref, bf16[512,512]{1,0:T(8,128)(2,1)S(1)} %get-tuple-element.41.own_ref.whole_ref, f32[2,128,2048]{2,1,0:T(8,128)S(1)} %get-tuple-element.53.slope_ref, ...), custom_call_target="tpu_custom_call" | custom-call | flops 1073741824 | bytes 2949376 | tf_op jit(solution)/shard_map/pallas_call | solution.py:48
  63.5 1.3 %collective-permute-done.17.other_ref = bf16[128,512]{1,0:T(8,128)(2,1)S(1)} collective-permute-done((bf16[128,512]{1,0:T(8,128)(2,1)S(1)}, bf16[128,512]{1,0:T(8,128)(2,1)S(1)}, u32[]{:S(2)}, u32[]{:S(2)}) %collective-permute-start.17) | collective-permute-done | bytes 131104 | tf_op jit(solution)/shard_map/ppermute | solution.py:27
  65.1 3.4 %collective-permute-start.18 = (bf16[128,512]{1,0:T(8,128)(2,1)S(1)}, bf16[128,512]{1,0:T(8,128)(2,1)S(1)}, u32[]{:S(2)}, u32[]{:S(2)}) collective-permute-start(bf16[128,512]{1,0:T(8,128)(2,1)S(1)} %get-tuple-element.60.value_ref), channel_id=1, source_target_pairs={{0,8},{4,12},{8,0},{12,4},{16,24},{20,28},{24,16},{28,20},{1,9},{5... | collective-permute-start | bytes 393224 | tf_op jit(solution)/shard_map/ppermute | solution.py:27
  68.5 4.0 %collective-permute-done.18.other_ref = bf16[128,512]{1,0:T(8,128)(2,1)S(1)} collective-permute-done((bf16[128,512]{1,0:T(8,128)(2,1)S(1)}, bf16[128,512]{1,0:T(8,128)(2,1)S(1)}, u32[]{:S(2)}, u32[]{:S(2)}) %collective-permute-start.18) | collective-permute-done | bytes 131104 | tf_op jit(solution)/shard_map/ppermute | solution.py:27
  73.3 1.6 %collective-permute-start.12 = (bf16[128,512]{1,0:T(8,128)(2,1)S(1)}, bf16[128,512]{1,0:T(8,128)(2,1)S(1)}, u32[]{:S(2)}, u32[]{:S(2)}) collective-permute-start(bf16[128,512]{1,0:T(8,128)(2,1)S(1)} %get-tuple-element.67.refs_0_), channel_id=1, source_target_pairs={{0,1},{1,2},{2,3},{3,0},{4,5},{5,6},{6,7},{7,4},{8,9},{9,10},{10,1... | collective-permute-start | bytes 393224 | tf_op jit(solution)/shard_map/ppermute | solution.py:32
  74.8 2.6 %collective-permute-start.13 = (bf16[128,512]{1,0:T(8,128)(2,1)S(1)}, bf16[128,512]{1,0:T(8,128)(2,1)S(1)}, u32[]{:S(2)}, u32[]{:S(2)}) collective-permute-start(bf16[128,512]{1,0:T(8,128)(2,1)S(1)} %get-tuple-element.67.refs_0_), channel_id=1, source_target_pairs={{0,2},{1,3},{2,0},{3,1},{4,6},{5,7},{6,4},{7,5},{8,10},{9,11},{10,... | collective-permute-start | bytes 393224 | tf_op jit(solution)/shard_map/ppermute | solution.py:32
  77.4 1.3 %collective-permute-start.14 = (bf16[128,512]{1,0:T(8,128)(2,1)S(1)}, bf16[128,512]{1,0:T(8,128)(2,1)S(1)}, u32[]{:S(2)}, u32[]{:S(2)}) collective-permute-start(bf16[128,512]{1,0:T(8,128)(2,1)S(1)} %get-tuple-element.67.refs_0_), channel_id=1, source_target_pairs={{0,3},{1,0},{2,1},{3,2},{4,7},{5,4},{6,5},{7,6},{8,11},{9,8},{10,9... | collective-permute-start | bytes 393224 | tf_op jit(solution)/shard_map/ppermute | solution.py:32
  79.1 2.4 %collective-permute-done.12.refs_1_ = bf16[128,512]{1,0:T(8,128)(2,1)S(1)} collective-permute-done((bf16[128,512]{1,0:T(8,128)(2,1)S(1)}, bf16[128,512]{1,0:T(8,128)(2,1)S(1)}, u32[]{:S(2)}, u32[]{:S(2)}) %collective-permute-start.12) | collective-permute-done | bytes 131104 | tf_op jit(solution)/shard_map/ppermute | solution.py:32
  81.5 4.4 %collective-permute-done.13.refs_2_ = bf16[128,512]{1,0:T(8,128)(2,1)S(1)} collective-permute-done((bf16[128,512]{1,0:T(8,128)(2,1)S(1)}, bf16[128,512]{1,0:T(8,128)(2,1)S(1)}, u32[]{:S(2)}, u32[]{:S(2)}) %collective-permute-start.13) | collective-permute-done | bytes 131104 | tf_op jit(solution)/shard_map/ppermute | solution.py:32
  85.9 3.3 %collective-permute-start.20 = (bf16[128,512]{1,0:T(8,128)(2,1)S(1)}, bf16[128,512]{1,0:T(8,128)(2,1)S(1)}, u32[]{:S(2)}, u32[]{:S(2)}) collective-permute-start(bf16[128,512]{1,0:T(8,128)(2,1)S(1)} %shard_map.84.refs_0_), channel_id=1, source_target_pairs={{0,1},{1,2},{2,3},{3,0},{4,5},{5,6},{6,7},{7,4},{8,9},{9,10},{10,1... | collective-permute-start | bytes 393224 | tf_op jit(solution)/shard_map/ppermute | solution.py:32
  89.2 1.6 %collective-permute-start.21 = (bf16[128,512]{1,0:T(8,128)(2,1)S(1)}, bf16[128,512]{1,0:T(8,128)(2,1)S(1)}, u32[]{:S(2)}, u32[]{:S(2)}) collective-permute-start(bf16[128,512]{1,0:T(8,128)(2,1)S(1)} %shard_map.84.refs_0_), channel_id=1, source_target_pairs={{0,2},{1,3},{2,0},{3,1},{4,6},{5,7},{6,4},{7,5},{8,10},{9,11},{10,... | collective-permute-start | bytes 393224 | tf_op jit(solution)/shard_map/ppermute | solution.py:32
  91.5 7.3 %shard_map.85 = (f32[2,512,2048]{2,1,0:T(8,128)S(1)}, f32[2,512,512]{2,1,0:T(8,128)S(1)}, f32[2,512,1]{2,1,0:T(8,128)S(1)}, bf16[2,128,512]{2,1,0:T(8,128)(2,1)S(1)}, bf16[2,512,512]{2,1,0:T(8,128)(2,1)S(1)}) custom-call(bf16[128,512]{1,0:T(8,128)(2,1)S(1)} %get-tuple-element.67.refs_0_, bf16[128,512]{1,0:T(8,128)(2,1)S(1)} %collective-permute-done.12.refs_1_, ...), custom_call_target="tpu_custom_call" | custom-call | flops 4294967296 | bytes 2228224 | tf_op jit(solution)/shard_map/pallas_call | solution.py:48
  98.9 6.0 %shard_map.86 = (f32[2,128,2048]{2,1,0:T(8,128)}, f32[2,512,512]{2,1,0:T(8,128)}) custom-call(bf16[128,512]{1,0:T(8,128)(2,1)S(1)} %shard_map.84.refs_0_, bf16[128,512]{1,0:T(8,128)(2,1)S(1)} %collective-permute-done.20.refs_1_, bf16[128,512]{1,0:T(8,128)(2,1)S(1)} %collective-permute-done.21.refs_2_, bf16[128,512]{1,0:T(8,128)(2,1)S(1)} %collective-permute-done.22.refs_3_, ...), custom_call_target="tpu_custom_call" | custom-call | flops 4294967296 | bytes 5178368 | tf_op jit(solution)/shard_map/pallas_call | solution.py:48
  (43 shorter events, 14.6 us)
Async XLA Ops:
  0.6 1.3 %copy-start = (bf16[1280,512]{1,0:T(8,128)(2,1)S(1)}, bf16[1280,512]{1,0:T(8,128)(2,1)}, u32[]{:S(2)}) copy-start(bf16[1280,512]{1,0:T(8,128)(2,1)} %param.6) | copy-start | bytes 3932164
  2.9 5.3 %collective-permute-start = (bf16[128,512]{1,0:T(8,128)(2,1)S(1)}, bf16[128,512]{1,0:T(8,128)(2,1)S(1)}, u32[]{:S(2)}, u32[]{:S(2)}) collective-permute-start(bf16[128,512]{1,0:T(8,128)(2,1)S(1)} %select_select_fusion), channel_id=1, source_target_pairs={{0,4},{4,0},{8,12},{12,8},{16,20},{20,16},{24,28},{28,24},{1,5},{5... | collective-permute-start | bytes 393224 | tf_op jit(solution)/shard_map/ppermute | solution.py:27
  8.2 12.9 %collective-permute-start.7 = (bf16[512,512]{1,0:T(8,128)(2,1)S(1)}, bf16[512,512]{1,0:T(8,128)(2,1)S(1)}, u32[]{:S(2)}, u32[]{:S(2)}) collective-permute-start(bf16[512,512]{1,0:T(8,128)(2,1)S(1)} %get-tuple-element.41.own_ref.whole_ref), channel_id=1, source_target_pairs={{0,4},{4,0},{8,12},{12,8},{16,20},{20,16},{24,28},{28,24},{1,5},{5... | collective-permute-start | bytes 1572872 | tf_op jit(solution)/shard_map/ppermute | solution.py:27
  8.4 6.9 %collective-permute-start.1 = (bf16[128,512]{1,0:T(8,128)(2,1)S(1)}, bf16[128,512]{1,0:T(8,128)(2,1)S(1)}, u32[]{:S(2)}, u32[]{:S(2)}) collective-permute-start(bf16[128,512]{1,0:T(8,128)(2,1)S(1)} %fusion.refs_0_), channel_id=1, source_target_pairs={{0,8},{4,12},{8,0},{12,4},{16,24},{20,28},{24,16},{28,20},{1,9},{5... | collective-permute-start | bytes 393224 | tf_op jit(solution)/shard_map/ppermute | solution.py:27
  11.4 8.0 %collective-permute-start.2 = (bf16[128,512]{1,0:T(8,128)(2,1)S(1)}, bf16[128,512]{1,0:T(8,128)(2,1)S(1)}, u32[]{:S(2)}, u32[]{:S(2)}) collective-permute-start(bf16[128,512]{1,0:T(8,128)(2,1)S(1)} %fusion.refs_0_), channel_id=1, source_target_pairs={{0,16},{4,20},{8,24},{12,28},{16,0},{20,4},{24,8},{28,12},{1,17},{... | collective-permute-start | bytes 393224 | tf_op jit(solution)/shard_map/ppermute | solution.py:27
  12.9 6.4 %collective-permute-start.3 = (bf16[128,512]{1,0:T(8,128)(2,1)S(1)}, bf16[128,512]{1,0:T(8,128)(2,1)S(1)}, u32[]{:S(2)}, u32[]{:S(2)}) collective-permute-start(bf16[128,512]{1,0:T(8,128)(2,1)S(1)} %fusion.refs_0_), channel_id=1, source_target_pairs={{0,24},{4,28},{8,16},{12,20},{16,8},{20,12},{24,0},{28,4},{1,25},{... | collective-permute-start | bytes 393224 | tf_op jit(solution)/shard_map/ppermute | solution.py:27
  21.0 5.5 %collective-permute-start.4 = (bf16[128,512]{1,0:T(8,128)(2,1)S(1)}, bf16[128,512]{1,0:T(8,128)(2,1)S(1)}, u32[]{:S(2)}, u32[]{:S(2)}) collective-permute-start(bf16[128,512]{1,0:T(8,128)(2,1)S(1)} %shard_map.69), channel_id=1, source_target_pairs={{0,4},{4,8},{8,12},{12,16},{16,20},{20,24},{24,28},{28,0},{1,5},{5... | collective-permute-start | bytes 393224 | tf_op jit(solution)/shard_map/ppermute | solution.py:32
  21.6 9.2 %collective-permute-start.9 = (bf16[256,512]{1,0:T(8,128)(2,1)S(1)}, bf16[256,512]{1,0:T(8,128)(2,1)S(1)}, u32[]{:S(2)}, u32[]{:S(2)}) collective-permute-start(bf16[256,512]{1,0:T(8,128)(2,1)S(1)} %get-tuple-element.45), channel_id=1, source_target_pairs={{0,8},{4,12},{8,0},{12,4},{16,24},{20,28},{24,16},{28,20},{1,9},{5... | collective-permute-start | bytes 786440 | tf_op jit(solution)/shard_map/ppermute | solution.py:27
  28.2 5.5 %collective-permute-start.5 = (bf16[128,512]{1,0:T(8,128)(2,1)S(1)}, bf16[128,512]{1,0:T(8,128)(2,1)S(1)}, u32[]{:S(2)}, u32[]{:S(2)}) collective-permute-start(bf16[128,512]{1,0:T(8,128)(2,1)S(1)} %shard_map.70), channel_id=1, source_target_pairs={{0,4},{4,8},{8,12},{12,16},{16,20},{20,24},{24,28},{28,0},{1,5},{5... | collective-permute-start | bytes 393224 | tf_op jit(solution)/shard_map/ppermute | solution.py:32
  30.9 6.7 %collective-permute-start.10 = (bf16[256,512]{1,0:T(8,128)(2,1)S(1)}, bf16[256,512]{1,0:T(8,128)(2,1)S(1)}, u32[]{:S(2)}, u32[]{:S(2)}) collective-permute-start(bf16[256,512]{1,0:T(8,128)(2,1)S(1)} %collective-permute-done.9.refs_0_), channel_id=1, source_target_pairs={{0,4},{4,0},{8,12},{12,8},{16,20},{20,16},{24,28},{28,24},{1,5},{5... | collective-permute-start | bytes 786440 | tf_op jit(solution)/shard_map/ppermute | solution.py:27
  35.5 1.4 %collective-permute-start.6 = (bf16[128,512]{1,0:T(8,128)(2,1)S(1)}, bf16[128,512]{1,0:T(8,128)(2,1)S(1)}, u32[]{:S(2)}, u32[]{:S(2)}) collective-permute-start(bf16[128,512]{1,0:T(8,128)(2,1)S(1)} %shard_map.71.value_ref), channel_id=1, source_target_pairs={{0,4},{4,0},{8,12},{12,8},{16,20},{20,16},{24,28},{28,24},{1,5},{5... | collective-permute-start | bytes 393224 | tf_op jit(solution)/shard_map/ppermute | solution.py:27
  37.1 5.6 %collective-permute-start.8 = (bf16[128,512]{1,0:T(8,128)(2,1)S(1)}, bf16[128,512]{1,0:T(8,128)(2,1)S(1)}, u32[]{:S(2)}, u32[]{:S(2)}) collective-permute-start(bf16[128,512]{1,0:T(8,128)(2,1)S(1)} %get-tuple-element.43.value_ref), channel_id=1, source_target_pairs={{0,8},{4,12},{8,0},{12,4},{16,24},{20,28},{24,16},{28,20},{1,9},{5... | collective-permute-start | bytes 393224 | tf_op jit(solution)/shard_map/ppermute | solution.py:27
  43.1 5.5 %collective-permute-start.11 = (bf16[128,512]{1,0:T(8,128)(2,1)S(1)}, bf16[128,512]{1,0:T(8,128)(2,1)S(1)}, u32[]{:S(2)}, u32[]{:S(2)}) collective-permute-start(bf16[128,512]{1,0:T(8,128)(2,1)S(1)} %get-tuple-element.50.value_ref), channel_id=1, source_target_pairs={{0,16},{4,20},{8,24},{12,28},{16,0},{20,4},{24,8},{28,12},{1,17},{... | collective-permute-start | bytes 393224 | tf_op jit(solution)/shard_map/ppermute | solution.py:27
  48.6 1.8 %copy-start.1 = (bf16[128,512]{1,0:T(8,128)(2,1)S(1)}, bf16[128,512]{1,0:T(8,128)(2,1)}, u32[]{:S(2)}) copy-start(bf16[128,512]{1,0:T(8,128)(2,1)} %final_ref.7) | copy-start | bytes 393220
  52.1 2.6 %collective-permute-start.15 = (bf16[128,512]{1,0:T(8,128)(2,1)S(1)}, bf16[128,512]{1,0:T(8,128)(2,1)S(1)}, u32[]{:S(2)}, u32[]{:S(2)}) collective-permute-start(bf16[128,512]{1,0:T(8,128)(2,1)S(1)} %shard_map.79), channel_id=1, source_target_pairs={{0,28},{4,0},{8,4},{12,8},{16,12},{20,16},{24,20},{28,24},{1,29},{... | collective-permute-start | bytes 393224 | tf_op jit(solution)/shard_map/ppermute | solution.py:32
  56.3 5.4 %collective-permute-start.16 = (bf16[128,512]{1,0:T(8,128)(2,1)S(1)}, bf16[128,512]{1,0:T(8,128)(2,1)S(1)}, u32[]{:S(2)}, u32[]{:S(2)}) collective-permute-start(bf16[128,512]{1,0:T(8,128)(2,1)S(1)} %shard_map.80), channel_id=1, source_target_pairs={{0,28},{4,0},{8,4},{12,8},{16,12},{20,16},{24,20},{28,24},{1,29},{... | collective-permute-start | bytes 393224 | tf_op jit(solution)/shard_map/ppermute | solution.py:32
  63.4 1.4 %collective-permute-start.17 = (bf16[128,512]{1,0:T(8,128)(2,1)S(1)}, bf16[128,512]{1,0:T(8,128)(2,1)S(1)}, u32[]{:S(2)}, u32[]{:S(2)}) collective-permute-start(bf16[128,512]{1,0:T(8,128)(2,1)S(1)} %shard_map.81.value_ref), channel_id=1, source_target_pairs={{0,4},{4,0},{8,12},{12,8},{16,20},{20,16},{24,28},{28,24},{1,5},{5... | collective-permute-start | bytes 393224 | tf_op jit(solution)/shard_map/ppermute | solution.py:27
  65.1 7.4 %collective-permute-start.18 = (bf16[128,512]{1,0:T(8,128)(2,1)S(1)}, bf16[128,512]{1,0:T(8,128)(2,1)S(1)}, u32[]{:S(2)}, u32[]{:S(2)}) collective-permute-start(bf16[128,512]{1,0:T(8,128)(2,1)S(1)} %get-tuple-element.60.value_ref), channel_id=1, source_target_pairs={{0,8},{4,12},{8,0},{12,4},{16,24},{20,28},{24,16},{28,20},{1,9},{5... | collective-permute-start | bytes 393224 | tf_op jit(solution)/shard_map/ppermute | solution.py:27
  73.0 5.8 %collective-permute-start.19 = (bf16[128,512]{1,0:T(8,128)(2,1)S(1)}, bf16[128,512]{1,0:T(8,128)(2,1)S(1)}, u32[]{:S(2)}, u32[]{:S(2)}) collective-permute-start(bf16[128,512]{1,0:T(8,128)(2,1)S(1)} %get-tuple-element.63.value_ref), channel_id=1, source_target_pairs={{0,16},{4,20},{8,24},{12,28},{16,0},{20,4},{24,8},{28,12},{1,17},{... | collective-permute-start | bytes 393224 | tf_op jit(solution)/shard_map/ppermute | solution.py:27
  73.3 8.3 %collective-permute-start.12 = (bf16[128,512]{1,0:T(8,128)(2,1)S(1)}, bf16[128,512]{1,0:T(8,128)(2,1)S(1)}, u32[]{:S(2)}, u32[]{:S(2)}) collective-permute-start(bf16[128,512]{1,0:T(8,128)(2,1)S(1)} %get-tuple-element.67.refs_0_), channel_id=1, source_target_pairs={{0,1},{1,2},{2,3},{3,0},{4,5},{5,6},{6,7},{7,4},{8,9},{9,10},{10,1... | collective-permute-start | bytes 393224 | tf_op jit(solution)/shard_map/ppermute | solution.py:32
  74.8 11.1 %collective-permute-start.13 = (bf16[128,512]{1,0:T(8,128)(2,1)S(1)}, bf16[128,512]{1,0:T(8,128)(2,1)S(1)}, u32[]{:S(2)}, u32[]{:S(2)}) collective-permute-start(bf16[128,512]{1,0:T(8,128)(2,1)S(1)} %get-tuple-element.67.refs_0_), channel_id=1, source_target_pairs={{0,2},{1,3},{2,0},{3,1},{4,6},{5,7},{6,4},{7,5},{8,10},{9,11},{10,... | collective-permute-start | bytes 393224 | tf_op jit(solution)/shard_map/ppermute | solution.py:32
  77.4 8.5 %collective-permute-start.14 = (bf16[128,512]{1,0:T(8,128)(2,1)S(1)}, bf16[128,512]{1,0:T(8,128)(2,1)S(1)}, u32[]{:S(2)}, u32[]{:S(2)}) collective-permute-start(bf16[128,512]{1,0:T(8,128)(2,1)S(1)} %get-tuple-element.67.refs_0_), channel_id=1, source_target_pairs={{0,3},{1,0},{2,1},{3,2},{4,7},{5,4},{6,5},{7,6},{8,11},{9,8},{10,9... | collective-permute-start | bytes 393224 | tf_op jit(solution)/shard_map/ppermute | solution.py:32
  85.9 13.0 %collective-permute-start.20 = (bf16[128,512]{1,0:T(8,128)(2,1)S(1)}, bf16[128,512]{1,0:T(8,128)(2,1)S(1)}, u32[]{:S(2)}, u32[]{:S(2)}) collective-permute-start(bf16[128,512]{1,0:T(8,128)(2,1)S(1)} %shard_map.84.refs_0_), channel_id=1, source_target_pairs={{0,1},{1,2},{2,3},{3,0},{4,5},{5,6},{6,7},{7,4},{8,9},{9,10},{10,1... | collective-permute-start | bytes 393224 | tf_op jit(solution)/shard_map/ppermute | solution.py:32
  89.2 9.7 %collective-permute-start.21 = (bf16[128,512]{1,0:T(8,128)(2,1)S(1)}, bf16[128,512]{1,0:T(8,128)(2,1)S(1)}, u32[]{:S(2)}, u32[]{:S(2)}) collective-permute-start(bf16[128,512]{1,0:T(8,128)(2,1)S(1)} %shard_map.84.refs_0_), channel_id=1, source_target_pairs={{0,2},{1,3},{2,0},{3,1},{4,6},{5,7},{6,4},{7,5},{8,10},{9,11},{10,... | collective-permute-start | bytes 393224 | tf_op jit(solution)/shard_map/ppermute | solution.py:32
  90.8 8.1 %collective-permute-start.22 = (bf16[128,512]{1,0:T(8,128)(2,1)S(1)}, bf16[128,512]{1,0:T(8,128)(2,1)S(1)}, u32[]{:S(2)}, u32[]{:S(2)}) collective-permute-start(bf16[128,512]{1,0:T(8,128)(2,1)S(1)} %shard_map.84.refs_0_), channel_id=1, source_target_pairs={{0,3},{1,0},{2,1},{3,2},{4,7},{5,4},{6,5},{7,6},{8,11},{9,8},{10,9... | collective-permute-start | bytes 393224 | tf_op jit(solution)/shard_map/ppermute | solution.py:32
